TPU v7x, 32 devices: a whole 2x2x4 slice. The times are simulated.
32 devices in a mesh: px: 4 (over z), py: 8 (over y, x, core).
Axes of the slice: x: 2, y: 2, z: 4, core: 2. Of those that a mesh axis runs over, the one named last changes fastest.
Arguments:
- charge: float32 [32, 768, 768], P(('px', 'py')), may hold values from -5 to 5
Outputs:
- potential_field: float32 [32, 768, 768], P(('px', 'py'))
All inputs are finite; a program needn't handle non-finite values.
Results may differ from a plain program's by a relative error of at most 0.0003.
Values sent between devices are 32-bit elements; how exact they have to be, the bound alone decides.
No kernel may reach another device: no remote copies, remote signals or barrier semaphores. Data moves between devices by JAX's collectives and lax.ppermute only.
A program may use at most 192 MiB of HBM per device.

v0:
```python
import functools
import math

import jax
import jax.numpy as jnp
import numpy as np
from jax import lax
from jax.experimental import pallas as pl
from jax.experimental.pallas import tpu as pltpu
from jax.sharding import PartitionSpec as P

PANELS = 128
HIGHEST = lax.Precision.HIGHEST
HIGH = lax.Precision.HIGH
FOUR_PI = 4.0 * math.pi
AXES = ("px", "py")


def dot(a, b, dims=((1,), (0,)), precision=HIGHEST):
    return lax.dot_general(
        a, b, (dims, ((), ())), precision=precision, preferred_element_type=jnp.float32
    )


def sine_table(n):
    order = np.arange(1, n + 1, dtype=np.int64)
    phase = (order[:, None] * order[None, :]) % (2 * (n + 1))
    return np.sqrt(2.0 / (n + 1)) * np.sin(np.pi * phase / (n + 1.0))


def eigen_values(n):
    return 2.0 - 2.0 * np.cos(np.pi * np.arange(1, n + 1) / (n + 1.0))


def fold_panels(grid, edge):
    sums = sine_table(grid).reshape(grid, PANELS, edge).sum(2)[:, : PANELS // 2]
    even = (np.arange(grid) % 2 == 0)[:, None]
    return np.concatenate([np.where(even, sums, 0.0), np.where(even, 0.0, sums)], axis=1)


def wave_basis(n):
    place = np.arange(n // 2) - (n - 1) / 2.0
    even = np.cos(np.pi * np.arange(n)[:, None] * place[None, :] / n)
    even *= np.sqrt(np.where(np.arange(n) == 0, 1.0, 2.0) / n)[:, None]
    odd = np.sin(np.pi * np.arange(1, n + 1)[:, None] * place[None, :] / n)
    odd *= np.sqrt(np.where(np.arange(1, n + 1) == n, 1.0, 2.0) / n)[:, None]
    return even, odd


def wave_values(n):
    distance = np.arange(n)[:, None]
    order = np.concatenate([np.arange(n), np.arange(1, n + 1)])[None, :]
    return np.where(distance == 0, 1.0, 2.0) * np.cos(np.pi * distance * order / n)


def distance_power(*squares):
    return lax.rsqrt(functools.reduce(lambda a, b: a + b, squares))


def iota(shape, axis):
    return lax.broadcasted_iota(jnp.int32, shape, axis).astype(jnp.float32)


def mixed_body(edge, depth, wave_ref, out_ref):
    hb = PANELS // 2
    soft = edge * edge / 4.0
    level = (pl.program_id(0) + 1).astype(jnp.float32)
    shape = (hb, PANELS)
    first = (edge - 1) / 2.0 + 1.0
    front = iota(shape, 0) * edge + first
    back = (PANELS - 1 - iota(shape, 0)) * edge + first
    along = iota(shape, 1) * edge
    along = along * along + soft
    front = front * front + along
    back = back * back + along
    own = level * level
    far = (depth + 1.0 - level) * (depth + 1.0 - level)
    own_front, own_back = distance_power(front, own), distance_power(back, own)
    far_front, far_back = distance_power(front, far), distance_power(back, far)
    rows = []
    for sign in (1.0, -1.0):
        one, two = own_front + sign * far_front, own_back + sign * far_back
        rows += [one + two, one - two]
    value = dot(jnp.concatenate(rows, 0), wave_ref[...])
    out_ref[0, 0] = value[:PANELS]
    out_ref[1, 0] = value[PANELS:]


def mixed_table(edge, depth, wave):
    half = depth // 2
    return pl.pallas_call(
        functools.partial(mixed_body, edge, depth),
        grid=(half,),
        in_specs=[pl.BlockSpec((PANELS, 2 * PANELS), lambda i: (0, 0))],
        out_specs=pl.BlockSpec((2, 1, PANELS, 2 * PANELS), lambda i: (0, i, 0, 0)),
        out_shape=jax.ShapeDtypeStruct((2, half, PANELS, 2 * PANELS), jnp.float32),
        cost_estimate=pl.CostEstimate(
            flops=2 * depth * PANELS**3, bytes_accessed=4 * depth * PANELS * PANELS,
            transcendentals=0,
        ),
    )(wave)


STRIP = 8


def corner_body(edge, depth, wave_ref, front_ref, back_ref):
    hb = PANELS // 2
    soft = edge * edge / 4.0
    shape = (hb, 2 * depth)
    first = (edge - 1) / 2.0 + 1.0
    lane = lax.broadcasted_iota(jnp.int32, shape, 1)
    odd = lane >= depth
    level = jnp.where(odd, lane - depth, lane).astype(jnp.float32)
    sign = jnp.where(odd, -1.0, 1.0)
    level = level * level + soft
    near = iota(shape, 0) * edge + first
    distant = (PANELS - 1 - iota(shape, 0)) * edge + first
    near = near * near + level
    distant = distant * distant + level
    sums, gaps = [], []
    for k in range(STRIP):
        b = (pl.program_id(0) * STRIP + k).astype(jnp.float32)
        front = b * edge + first
        back = (PANELS - 1 - b) * edge + first
        front, back = front * front, back * back
        one = distance_power(near, front) + sign * distance_power(distant, front)
        two = distance_power(near, back) + sign * distance_power(distant, back)
        sums.append(one + two)
        gaps.append(one - two)
    wave = wave_ref[...]
    front_ref[...] = dot(jnp.concatenate(sums, 0), wave).reshape(front_ref.shape)
    back_ref[...] = dot(jnp.concatenate(gaps, 0), wave).reshape(back_ref.shape)


def corner_table(edge, depth, wave):
    hb = PANELS // 2
    width = 4 * depth
    block = pl.BlockSpec((STRIP, hb, width), lambda i: (i, 0, 0))
    shape = jax.ShapeDtypeStruct((hb, hb, width), jnp.float32)
    return pl.pallas_call(
        functools.partial(corner_body, edge, depth),
        grid=(hb // STRIP,),
        in_specs=[pl.BlockSpec((2 * depth, width), lambda i: (0, 0))],
        out_specs=[block, block],
        out_shape=[shape, shape],
        cost_estimate=pl.CostEstimate(
            flops=2 * depth * PANELS**3, bytes_accessed=4 * depth * PANELS * PANELS,
            transcendentals=0,
        ),
    )(wave)


def small_tables(depth, grid, edge):
    half = depth // 2
    soft = edge * edge / 4.0

    def kernel(dz, dy, dx):
        return 1.0 / np.sqrt(dz * dz + dy * dy + dx * dx + soft) / FOUR_PI

    step = edge * np.arange(PANELS, dtype=np.float64)
    vx = wave_values(PANELS)
    vz = wave_values(depth)
    even, odd = wave_basis(PANELS)
    zero = np.zeros_like(even)
    basis_x = np.concatenate(
        [np.concatenate([even, zero], 1), np.concatenate([zero, odd], 1)], 0
    )
    bz = np.stack(wave_basis(depth))
    face, side = [], []
    z = np.arange(depth, dtype=np.float64)
    for s, sign in enumerate((1.0, -1.0)):
        k = kernel(0.0, step[:, None], step[None, :])
        k = k + sign * kernel(depth + 1.0, step[:, None], step[None, :])
        face.append(vx.T @ k @ vx)
        for other in (1.0, -1.0):
            k = kernel(z[:, None], 0.0, step[None, :])
            k = k + other * kernel(z[:, None], grid + 1.0, step[None, :])
            side.append(vz[:, s * depth : (s + 1) * depth].T @ k @ vx)
    level = np.zeros((2, 2, half, 2, 2, depth))
    cross = np.zeros((2, 2, half, 2, 2, depth))
    turn = np.zeros((2, 2, 2, half, 2, 2, 2, depth))
    for s in (0, 1):
        for t in (0, 1):
            level[s, t, :, s, t] = bz[s].T
            cross[s, t, :, t, s] = bz[s].T
            for x in (0, 1):
                turn[x, s, t, :, t, x, s] = bz[s].T
    lift = np.zeros((2, depth, 2, 2, depth))
    for x in (0, 1):
        for s in (0, 1):
            lift[x, :, x, s] = vz[:, s * depth : (s + 1) * depth]
    return dict(
        basis=basis_x,
        face=np.stack(face),
        side=np.concatenate(side),
        level=level.reshape(4 * half, 4 * depth),
        cross=cross.reshape(4 * half, 4 * depth),
        turn=turn.reshape(2, 4 * half, 8 * depth),
        wave_x=vx / FOUR_PI,
        lift=lift.reshape(2 * depth, 4 * depth) / FOUR_PI,
    )


NT = ((1,), (1,))
TN = ((0,), (0,))


def panels_body(
    own_ref, other_ref, basis_ref, face_ref, side_ref, level_ref, cross_ref, turn_ref,
    mixed_ref, front_ref, back_ref, face_out_ref, side_out_ref,
    fx_ref, hat_ref, acc_ref, toside_ref, xs_ref, tox_ref,
):
    half = mixed_ref.shape[1]
    hb = PANELS // 2
    total = (own_ref[...] + other_ref[...]) * 0.5
    gap = (own_ref[...] - other_ref[...]) * 0.5
    basis = basis_ref[...]
    level = level_ref[...]
    faces = [total[:PANELS], gap[:PANELS]]
    sides = []
    for axis in (0, 1):
        rows = slice(PANELS + axis * 2 * half, PANELS + (axis + 1) * 2 * half)
        sides.append(jnp.concatenate([total[rows], gap[rows]], 0))
        hat_ref[axis] = dot(sides[axis], basis, NT)
    for s in (0, 1):
        fx_ref[0, s] = dot(faces[s], basis, NT)
        fx_ref[1, s] = dot(faces[s], basis, ((0,), (1,)))

    for s in (0, 1):

        def face_rows(block, _, s=s):
            at = pl.multiple_of(block * 8, 8)
            odd = (block >= 8).astype(jnp.int32)
            base = (2 * s + odd) * half

            def add(chunk, acc):
                one, two = acc
                for k in range(8):
                    j = chunk * 8 + k
                    t = mixed_ref[s, j, pl.ds(at, 8), :]
                    one = one + t * hat_ref[0, pl.ds(base + j, 1), :]
                    two = two + t * hat_ref[1, pl.ds(base + j, 1), :]
                return one, two

            zero = jnp.zeros((8, 2 * PANELS), jnp.float32)
            one, two = lax.fori_loop(0, half // 8, add, (zero, zero))
            acc_ref[0, s, pl.ds(at, 8), :] = one
            acc_ref[1, s, pl.ds(at, 8), :] = two
            return 0

        lax.fori_loop(0, PANELS // 8, face_rows, 0)

        def side_rows(j, _, s=s):
            for t in (0, 1):
                sums = [None, None]
                for block in range(hb // 8):
                    rows = slice(t * hb + block * 8, t * hb + block * 8 + 8)
                    table = mixed_ref[s, j, rows, :]
                    for axis in (0, 1):
                        term = table * fx_ref[axis, s, rows, :]
                        sums[axis] = term if block == 0 else sums[axis] + term
                for axis in (0, 1):
                    toside_ref[axis, pl.ds((2 * s + t) * half + j, 1), :] = jnp.sum(
                        sums[axis], axis=0, keepdims=True
                    )
            return 0

        lax.fori_loop(0, half, side_rows, 0)

    xs_ref[...] = dot(sides[1], cross_ref[...], TN)
    ys = dot(sides[0][:, :hb], turn_ref[0], TN) + dot(sides[0][:, hb:], turn_ref[1], TN)
    width = xs_ref.shape[1]
    to_y = []
    for t, table_ref in ((0, front_ref), (1, back_ref)):
        mine = ys[:, t * width : (t + 1) * width]

        def corner_rows(b, acc, t=t, table_ref=table_ref, mine=mine):
            table = table_ref[b]
            row = pl.ds(t * hb + b, 1)
            tox_ref[row, :] = jnp.sum(table * mine, axis=0, keepdims=True)
            return acc + table * xs_ref[row, :]

        to_y.append(lax.fori_loop(0, hb, corner_rows, jnp.zeros((hb, width), jnp.float32)))
    to_y = jnp.concatenate(to_y, 1)
    corner = [
        jnp.concatenate([dot(turn_ref[x], to_y, NT) for x in (0, 1)], 1),
        dot(cross_ref[...], tox_ref[...], NT),
    ]
    for axis in (0, 1):
        waves = dot(level, hat_ref[axis], TN) * side_ref[...]
        waves = dot(level, waves) + toside_ref[axis]
        value = dot(waves, basis) + corner[axis]
        even, odd = value[: 2 * half], value[2 * half :]
        for part, v in ((0, even + odd), (1, even - odd)):
            for t in (0, 1):
                at = (2 * t + part) * half
                side_out_ref[axis, at : at + half, :] = v[t * half : (t + 1) * half]
    value = []
    for s in (0, 1):
        full = dot(basis, fx_ref[0, s]) * face_ref[s]
        rows = dot(basis, full, TN) + acc_ref[0, s]
        value.append(dot(rows, basis) + dot(basis, acc_ref[1, s], ((0,), (1,))))
    face_out_ref[0] = value[0] + value[1]
    face_out_ref[1] = value[0] - value[1]


def panel_potential(own, other, tb, mixed, corner):
    half = mixed.shape[1]
    width = corner[0].shape[2]
    f32 = jnp.float32
    return pl.pallas_call(
        panels_body,
        out_shape=[
            jax.ShapeDtypeStruct((2, PANELS, PANELS), f32),
            jax.ShapeDtypeStruct((2, 4 * half, PANELS), f32),
        ],
        scratch_shapes=[
            pltpu.VMEM((2, 2, PANELS, 2 * PANELS), f32),
            pltpu.VMEM((2, 4 * half, 2 * PANELS), f32),
            pltpu.VMEM((2, 2, PANELS, 2 * PANELS), f32),
            pltpu.VMEM((2, 4 * half, 2 * PANELS), f32),
            pltpu.VMEM((PANELS, width), f32),
            pltpu.VMEM((PANELS, width), f32),
        ],
    )(
        own, other, tb["basis"], tb["face"], tb["side"], tb["level"], tb["cross"], tb["turn"],
        mixed, *corner,
    )


WIDTH = 256


def block_specs(planes, rows):
    block = pl.BlockSpec((planes, rows, WIDTH), lambda i, *_: (0, 0, i))
    flat = pl.BlockSpec((rows, WIDTH), lambda i, *_: (0, i))
    return block, flat


def factor_body(mu_ref, coef_ref, join_ref):
    planes = coef_ref.shape[0]
    for col in range(0, WIDTH, 128):
        part = slice(col, col + 128)
        diag = mu_ref[:, part] + 2.0
        coef = 1.0 / diag
        coef_ref[0, :, part] = coef
        for j in range(1, planes):
            coef = 1.0 / (diag - coef)
            coef_ref[j, :, part] = coef
        join_ref[:, part] = 1.0 / (1.0 - coef * coef)


def factors(mu, planes):
    rows, cols = mu.shape
    block, flat = block_specs(planes, rows)
    return pl.pallas_call(
        factor_body,
        grid=(cols // WIDTH,),
        in_specs=[flat],
        out_specs=[block, flat],
        out_shape=[
            jax.ShapeDtypeStruct((planes, rows, cols), jnp.float32),
            jax.ShapeDtypeStruct((rows, cols), jnp.float32),
        ],
        cost_estimate=pl.CostEstimate(
            flops=20 * planes * rows * cols, bytes_accessed=4 * planes * rows * cols, transcendentals=0
        ),
    )(mu)


def sweep_body(half_ref, f_ref, coef_ref, g_ref, last_ref):
    planes = f_ref.shape[0]
    upper = half_ref[0]
    value = jnp.zeros_like(last_ref)
    for j in range(planes):
        place = jnp.where(upper == 1, planes - 1 - j, j)
        value = (f_ref[place] + value) * coef_ref[j]
        g_ref[j] = value
    last_ref[...] = value


def sweep(upper, spectrum, coef):
    planes, rows, cols = spectrum.shape
    block, flat = block_specs(planes, rows)
    return pl.pallas_call(
        sweep_body,
        grid_spec=pltpu.PrefetchScalarGridSpec(
            num_scalar_prefetch=1,
            grid=(cols // WIDTH,),
            in_specs=[block, block],
            out_specs=[block, flat],
        ),
        out_shape=[
            jax.ShapeDtypeStruct(spectrum.shape, jnp.float32),
            jax.ShapeDtypeStruct((rows, cols), jnp.float32),
        ],
    )(upper, spectrum, coef)


def finish_body(half_ref, g_ref, coef_ref, join_ref, far_ref, u_ref, edge_ref):
    planes = g_ref.shape[0]
    upper = half_ref[0]
    value = (far_ref[...] + coef_ref[planes - 1] * g_ref[planes - 1]) * join_ref[...]
    for j in range(planes - 1, -1, -1):
        value = g_ref[j] + coef_ref[j] * value
        u_ref[jnp.where(upper == 1, planes - 1 - j, j)] = value
    edge_ref[...] = value


def finish(upper, g, coef, join, far):
    planes, rows, cols = g.shape
    block, flat = block_specs(planes, rows)
    return pl.pallas_call(
        finish_body,
        grid_spec=pltpu.PrefetchScalarGridSpec(
            num_scalar_prefetch=1,
            grid=(cols // WIDTH,),
            in_specs=[block, block, flat, flat],
            out_specs=[block, flat],
        ),
        out_shape=[
            jax.ShapeDtypeStruct(g.shape, jnp.float32),
            jax.ShapeDtypeStruct((rows, cols), jnp.float32),
        ],
    )(upper, g, coef, join, far)


def ghost_body(
    half_ref, u_ref, coef_ref, join_ref, row_ref, col_ref, along_ref, across_ref, near_ref,
    far_ref, out_ref, g_ref,
):
    planes, rows, width = u_ref.shape
    upper = half_ref[0]
    row_odd = lax.broadcasted_iota(jnp.int32, (rows, width), 0) % 2 == 1
    col_odd = lax.broadcasted_iota(jnp.int32, (rows, width), 1) % 2 == 1
    row_value, col_value = row_ref[...], col_ref[...]

    def layer(index):
        even = along_ref[index : index + 1, :]
        odd = along_ref[2 * planes + index : 2 * planes + index + 1, :]
        side_y = row_value * jnp.where(row_odd, odd, even)
        even = across_ref[:, index : index + 1]
        odd = across_ref[:, 2 * planes + index : 2 * planes + index + 1]
        return side_y + col_value * jnp.where(col_odd, odd, even)

    own, far = near_ref[...], far_ref[...]
    for j in range(planes):
        coef = coef_ref[j]
        own = (layer(j) + own) * coef
        far = (layer(planes + j) + far) * coef
        g_ref[j] = own
    value = (far + coef * own) * join_ref[...]
    for j in range(planes - 1, -1, -1):
        value = g_ref[j] + coef_ref[j] * value
        place = jnp.where(upper == 1, planes - 1 - j, j)
        out_ref[place] = u_ref[place] + value


def add_ghost(upper, u, coef, join, row_value, col_value, along, across, near, far):
    planes, rows, cols = u.shape
    block, flat = block_specs(planes, rows)
    return pl.pallas_call(
        ghost_body,
        grid_spec=pltpu.PrefetchScalarGridSpec(
            num_scalar_prefetch=1,
            grid=(cols // WIDTH,),
            in_specs=[
                block,
                block,
                flat,
                pl.BlockSpec((rows, 1), lambda i, u: (0, 0)),
                pl.BlockSpec((1, WIDTH), lambda i, u: (0, i)),
                pl.BlockSpec((4 * planes, WIDTH), lambda i, u: (0, i)),
                pl.BlockSpec((rows, 4 * planes), lambda i, u: (0, 0)),
                flat,
                flat,
            ],
            out_specs=block,
            scratch_shapes=[pltpu.VMEM((planes, rows, WIDTH), jnp.float32)],
        ),
        out_shape=jax.ShapeDtypeStruct(u.shape, jnp.float32),
    )(upper, u, coef, join, row_value, col_value, along, across, near, far)


def build(mesh, grid, depth):
    slow, fast = mesh.shape["px"], mesh.shape["py"]
    devices = slow * fast
    half = devices // 2
    rows = grid // half
    edge = grid // PANELS
    groups = [list(range(half)), list(range(half, devices))]
    tables = {
        name: value.astype(np.float32) for name, value in small_tables(depth, grid, edge).items()
    }
    sine_np = sine_table(grid).astype(np.float32)
    eigen_np = eigen_values(grid)
    fold_np = fold_panels(grid, edge).astype(np.float32)

    def exchange(x):
        return lax.all_to_all(
            x, AXES, split_axis=0, concat_axis=0, tiled=True, axis_index_groups=groups
        )

    def hop(x, bit):
        return lax.ppermute(x, "px", [(i, i ^ bit) for i in range(slow)])

    def on_device(charge):
        rank = lax.axis_index(AXES)
        upper = (rank // half).astype(jnp.int32).reshape(1)
        is_upper = rank // half == 1
        start = (rank % half) * rows
        sine = jnp.asarray(sine_np)
        fold = jnp.asarray(fold_np)
        tb = {name: jnp.asarray(value) for name, value in tables.items()}
        eigen = jnp.asarray(eigen_np.astype(np.float32))
        edge_value = jnp.asarray(sine_np[:, 0])
        my_eigen = lax.dynamic_slice_in_dim(eigen, start, rows, 0)
        my_edge = lax.dynamic_slice_in_dim(edge_value, start, rows, 0)
        my_fold = lax.dynamic_slice_in_dim(fold, start, rows, 0)
        mu = my_eigen[:, None] + eigen[None, :]
        parity = jnp.arange(grid) % 2
        edge_pair = jnp.stack([edge_value * (parity == 0), edge_value * (parity == 1)])
        my_pair = jnp.stack([my_edge * (parity[:rows] == 0), my_edge * (parity[:rows] == 1)])

        plane = charge.reshape(grid, grid)
        spectrum = dot(sine, dot(plane, sine, precision=HIGH), precision=HIGH)
        spectrum = exchange(spectrum.reshape(half, rows, grid))
        coef, join = factors(mu, half)
        mixed = mixed_table(edge, depth, tb["wave_x"])
        corner = corner_table(edge, depth, tb["lift"])
        spectrum, mixed, corner = lax.optimization_barrier((spectrum, mixed, corner))
        g, last = sweep(upper, spectrum, coef)
        far = lax.ppermute(last, AXES, [(i, i ^ half) for i in range(devices)])
        u, outer = finish(upper, g, coef, join, far)

        face = dot(my_fold, dot(outer, fold), ((0,), (0,)))
        lines_y = jnp.einsum("tk,jkx->tjx", my_pair, u, precision=HIGHEST)
        lines_y = jnp.einsum("tjx,xb->tjb", lines_y, fold, precision=HIGHEST)
        lines_x = jnp.einsum("jkx,tx->tjk", u, edge_pair, precision=HIGHEST)
        lines_x = jnp.einsum("tjk,kb->tjb", lines_x, my_fold, precision=HIGHEST)
        lines = jnp.stack([lines_y, lines_x])
        lines = jnp.where(is_upper, lines[:, :, ::-1], lines)
        part = jnp.concatenate([face, lines.reshape(-1, PANELS)])
        part = lax.all_gather(part, "py", axis=0, tiled=False).sum(0)
        bit = 1
        while bit < slow // 2:
            part = part + hop(part, bit)
            bit *= 2
        other = hop(part, bit)
        face_v, side_v = panel_potential(part, other, tb, mixed, corner)
        near, distant = (
            4.0 * dot(dot(my_fold, face_v[i]), fold, ((1,), (1,))) for i in (0, 1)
        )
        along = 4.0 * dot(side_v[0], fold, ((1,), (1,)))
        across = 4.0 * dot(my_fold, side_v[1], ((1,), (1,)))
        u = add_ghost(
            upper, u, coef, join, my_edge[:, None], edge_value[None, :], along, across, near, distant
        )
        u = exchange(u).reshape(grid, grid)
        return dot(dot(sine, u, precision=HIGH), sine, precision=HIGH)[None]

    return on_device


def solution(mesh):
    spec = P(AXES, None, None)

    def run(charge):
        depth, grid, _ = charge.shape
        body = build(mesh, grid, depth)
        return jax.shard_map(body, mesh=mesh, in_specs=(spec,), out_specs=spec, check_vma=False)(
            charge
        )

    return run
```

profile of v0, /device:TPU:0, one launch (start us, length us, event | category | flops | bytes accessed | tf_op | source)
XLA Modules:
  0.0 180.0 jit_solution(11804384273085244115)
XLA Ops:
  0.0 0.0 copy-start
  0.0 1.7 copy-done
  1.7 7.4 %fusion = f32[768,768]{1,0:T(8,128)S(1)} fusion(f32[768,768]{1,0:T(8,128)} %constant.96.clone, f32[1,768,768]{2,1,0:T(8,128)S(1)} %copy-done), kind=kOutput, calls=%fused_computation | convolution fusion | flops 2717908992 | bytes 7077888 | tf_op jit(solution)/shard_map/dot_general | solution.py:20
  9.1 0.0 copy-done.1
  9.1 4.5 %fusion.37 = f32[768,768]{1,0:T(8,128)} fusion(f32[768,768]{1,0:T(8,128)S(1)} %copy-done.1, f32[768,768]{1,0:T(8,128)S(1)} %fusion), kind=kOutput, calls=%fused_computation.58 | convolution fusion | flops 2717908992 | bytes 7077888 | tf_op jit(solution)/shard_map/dot_general | solution.py:20
  13.6 6.5 %all-to-all-start = ((f32[16,48,768]{2,1,0:T(8,128)}), f32[16,48,768]{2,1,0:T(8,128)}, u32[]{:S(2)}, u32[]{:S(2)}) async-start(f32[16,48,768]{2,1,0:T(8,128)} %bitcast.60), calls=%async_computation | async-start | bytes 4718592 | tf_op jit(solution)/shard_map/all_to_all | solution.py:501
  20.1 0.0 copy-done.10
  20.2 0.0 copy-done.11
  20.2 0.1 dynamic_slice.9
  20.3 0.7 broadcast_add_fusion.mu_ref
  21.0 3.1 %shard_map.129 = (f32[16,48,768]{2,1,0:T(8,128)}, f32[48,768]{1,0:T(8,128)}) custom-call(f32[48,768]{1,0:T(8,128)} %broadcast_add_fusion.mu_ref), custom_call_target="tpu_custom_call" | custom-call | flops 11796480 | bytes 2359296 | tf_op jit(solution)/shard_map/pallas_call | solution.py:357
  24.1 7.6 %shard_map.128 = (f32[64,64,128]{2,1,0:T(8,128)}, f32[64,64,128]{2,1,0:T(8,128)}) custom-call(f32[64,128]{1,0:T(8,128)} %constant.105.clone.wave_ref), custom_call_target="tpu_custom_call" | custom-call | flops 134217728 | bytes 2097152 | tf_op jit(solution)/shard_map/pallas_call | solution.py:141
  31.7 10.0 %shard_map.127.mixed_ref = f32[2,16,128,256]{3,2,1,0:T(8,128)} custom-call(f32[128,256]{1,0:T(8,128)} %constant.104.clone.wave_ref), custom_call_target="tpu_custom_call" | custom-call | flops 134217728 | bytes 2097152 | tf_op jit(solution)/shard_map/pallas_call | solution.py:91
  41.7 10.8 %all-to-all-done.f_ref = f32[16,48,768]{2,1,0:T(8,128)} async-done(((f32[16,48,768]{2,1,0:T(8,128)}), f32[16,48,768]{2,1,0:T(8,128)}, u32[]{:S(2)}, u32[]{:S(2)}) %all-to-all-start) | async-done | bytes 2359328 | tf_op jit(solution)/shard_map/all_to_all | solution.py:501
  52.6 4.5 %shard_map.130 = (f32[16,48,768]{2,1,0:T(8,128)}, f32[48,768]{1,0:T(8,128)}) custom-call(s32[1]{0:T(128)} %bitcast.half_ref, f32[16,48,768]{2,1,0:T(8,128)} %all-to-all-done.f_ref, f32[16,48,768]{2,1,0:T(8,128)} %get-tuple-element.22.coef_ref), custom_call_target="tpu_custom_call" | custom-call | tf_op jit(solution)/shard_map/pallas_call | solution.py:386
  57.1 2.6 %collective-permute-start = (f32[48,768]{1,0:T(8,128)}, f32[48,768]{1,0:T(8,128)S(1)}, u32[]{:S(2)}, u32[]{:S(2)}) collective-permute-start(f32[48,768]{1,0:T(8,128)} %get-tuple-element.25), channel_id=1, source_target_pairs={{0,16},{1,17},{2,18},{3,19},{4,20},{5,21},{6,22},{7,23},{8,24},{9,... | collective-permute-start | bytes 442376 | tf_op jit(solution)/shard_map/ppermute | solution.py:534
  59.7 0.1 fusion.28
  59.7 6.9 %collective-permute-done.far_ref = f32[48,768]{1,0:T(8,128)S(1)} collective-permute-done((f32[48,768]{1,0:T(8,128)}, f32[48,768]{1,0:T(8,128)S(1)}, u32[]{:S(2)}, u32[]{:S(2)}) %collective-permute-start) | collective-permute-done | bytes 147488 | tf_op jit(solution)/shard_map/ppermute | solution.py:534
  66.6 0.7 copy-done.8
  67.3 4.7 %shard_map.131 = (f32[16,48,768]{2,1,0:T(8,128)}, f32[48,768]{1,0:T(8,128)}) custom-call(s32[1]{0:T(128)} %bitcast.half_ref, f32[16,48,768]{2,1,0:T(8,128)} %get-tuple-element.23.g_ref, f32[16,48,768]{2,1,0:T(8,128)} %get-tuple-element.22.coef_ref, f32[48,768]{1,0:T(8,128)} %get-tuple-element.24.join_ref, f32[48,768]{1,0:T(8,128)} %copy-done.8), custom_call_target="tpu_custom_call" | custom-call | tf_op jit(solution)/shard_map/pallas_call | solution.py:414
  72.0 3.0 %fusion.25 = f32[2,16,768]{2,0,1:T(2,128)S(1)} fusion(f32[16,48,768]{2,1,0:T(8,128)} %get-tuple-element.26.u_ref, f32[1,48]{1,0:T(1,128)S(1)} %get-tuple-element.34, f32[1,48]{1,0:T(1,128)S(1)} %get-tuple-element.33), kind=kOutput, calls=%fused_computation.45 | convolution fusion | flops 14155872 | bytes 2457984 | tf_op jit(solution)/shard_map/tk,jkx->tjx/dot_general | solution.py:538
  75.1 0.3 convolution_bitcast_fusion.2
  75.4 3.5 %fusion.19 = f32[2,16,48]{2,0,1:T(2,128)S(1)} fusion(f32[16,48,768]{2,1,0:T(8,128)S(1)} %copy-done.3, f32[1,768]{1,0:T(1,128)S(1)} %stack.32, f32[1,768]{1,0:T(1,128)S(1)} %stack.31), kind=kOutput, calls=%fused_computation.32 | convolution fusion | flops 14157312 | bytes 2371584 | tf_op jit(solution)/shard_map/jkx,tx->tjk/dot_general | solution.py:540
  78.9 0.2 convolution_bitcast_fusion.1
  79.1 0.0 copy-done.7
  79.1 0.3 fusion.38
  79.4 0.3 fusion.8
  79.8 13.1 %all-gather = f32[1536,128]{1,0:T(8,128)S(1)} all-gather(f32[192,128]{1,0:T(8,128)S(1)} %pad_maximum_fusion), channel_id=2, replica_groups=mesh['px'=4,'py'=8] {'py'}, dimensions={0}, use_global_device_ids=true | all-gather | bytes 884736 | tf_op jit(solution)/shard_map/all_gather | solution.py:545
  92.8 0.7 reduce_sum.9
  93.5 0.3 collective-permute-start.1
  93.8 5.0 %collective-permute-done.1 = f32[192,128]{1,0:T(8,128)S(1)} collective-permute-done((f32[192,128]{1,0:T(8,128)}, f32[192,128]{1,0:T(8,128)S(1)}, u32[]{:S(2)}, u32[]{:S(2)}) %collective-permute-start.1) | collective-permute-done | bytes 98336 | tf_op jit(solution)/shard_map/ppermute | solution.py:506
  98.8 0.9 add.48.own_ref
  99.7 0.0 copy-start.5
  99.7 1.9 %collective-permute-start.2 = (f32[192,128]{1,0:T(8,128)S(1)}, f32[192,128]{1,0:T(8,128)S(1)}, u32[]{:S(2)}, u32[]{:S(2)}) collective-permute-start(f32[192,128]{1,0:T(8,128)S(1)} %add.48.own_ref), channel_id=1, source_target_pairs={{0,16},{8,24},{16,0},{24,8},{1,17},{9,25},{17,1},{25,9},{2,18},{10... | collective-permute-start | bytes 294920 | tf_op jit(solution)/shard_map/ppermute | solution.py:506
  101.6 0.7 copy.14.row_ref
  102.3 4.7 %collective-permute-done.2.other_ref = f32[192,128]{1,0:T(8,128)S(1)} collective-permute-done((f32[192,128]{1,0:T(8,128)S(1)}, f32[192,128]{1,0:T(8,128)S(1)}, u32[]{:S(2)}, u32[]{:S(2)}) %collective-permute-start.2) | collective-permute-done | bytes 98336 | tf_op jit(solution)/shard_map/ppermute | solution.py:506
  107.0 0.6 copy-done.9
  107.6 13.8 %shard_map.132 = (f32[2,128,128]{2,1,0:T(8,128)}, f32[2,64,128]{2,1,0:T(8,128)}) custom-call(f32[192,128]{1,0:T(8,128)} %copy-done.5, f32[192,128]{1,0:T(8,128)} %copy-done.9, f32[256,128]{1,0:T(8,128)} %constant.98.clone.basis_ref, f32[2,256,256]{2,1,0:T(8,128)} %constant.99.clone.face_ref, f32[128,256]{1,0:T(8,128)} %constant.100.clone.side_ref, ...), custom_call_target="tpu_custom_call" | custom-call | tf_op jit(solution)/shard_map/pallas_call | solution.py:312
  121.4 1.0 fusion.3
  122.4 1.0 fusion.5
  123.4 2.0 %convolution_multiply_fusion.along_ref = f32[64,768]{1,0:T(8,128)} fusion(f32[768,128]{1,0:T(8,128)S(1)} %copy-done.4, f32[2,64,128]{2,1,0:T(8,128)} %get-tuple-element.31), kind=kOutput, calls=%fused_computation.3 | convolution fusion | flops 75546624 | bytes 622592 | tf_op jit(solution)/shard_map/dot_general | solution.py:20
  125.4 1.5 convolution_multiply_fusion.3.across_ref
  126.9 1.2 convolution_multiply_fusion.1.far_ref
  128.1 1.2 convolution_multiply_fusion.2.near_ref
  129.2 6.1 %shard_map.133 = f32[16,48,768]{2,1,0:T(8,128)} custom-call(s32[1]{0:T(128)} %bitcast.half_ref, f32[16,48,768]{2,1,0:T(8,128)} %get-tuple-element.26.u_ref, f32[16,48,768]{2,1,0:T(8,128)} %get-tuple-element.22.coef_ref, f32[48,768]{1,0:T(8,128)} %get-tuple-element.24.join_ref, f32[48,1]{1,0:T(8,128)} %copy.14.row_ref, f32[1,768]{1,0:T(1,128)} %constant.109.col_ref, ...), custom_call_target="tpu_custom_call" | custom-call | tf_op jit(solution)/shard_map/pallas_call | solution.py:463
  135.3 34.0 %all_to_all.10 = f32[16,48,768]{2,1,0:T(8,128)S(1)} all-to-all(f32[16,48,768]{2,1,0:T(8,128)} %shard_map.133), channel_id=1, replica_groups={{0,1,2,3,4,5,6,7,8,9,10,11,12,13,14,15},{16,17,18,19,20,21,22,23,24,25,..., dimensions={0} | all-to-all | bytes 4718592 | tf_op jit(solution)/shard_map/all_to_all | solution.py:501
  169.3 5.8 %fusion.39 = f32[768,768]{1,0:T(8,128)S(1)} fusion(f32[768,768]{1,0:T(8,128)S(1)} %bitcast.61, f32[768,768]{1,0:T(8,128)S(1)} %copy-done.2), kind=kOutput, calls=%fused_computation.60 | convolution fusion | flops 2717908992 | bytes 7077888 | tf_op jit(solution)/shard_map/dot_general | solution.py:20
  175.1 4.9 %convolution_bitcast_fusion = f32[1,768,768]{2,1,0:T(8,128)} fusion(f32[768,768]{1,0:T(8,128)S(1)} %fusion.39, f32[768,768]{1,0:T(8,128)S(1)} %copy-done.2), kind=kOutput, calls=%fused_computation.2 | convolution fusion | flops 2717908992 | bytes 7077888 | tf_op jit(solution)/shard_map/dot_general | solution.py:20
  (23 shorter events, 0.1 us)
Async XLA Ops:
  0.0 1.7 copy-start
  0.0 9.1 %copy-start.1 = (f32[768,768]{1,0:T(8,128)S(1)}, f32[768,768]{1,0:T(8,128)}, u32[]{:S(2)}) copy-start(f32[768,768]{1,0:T(8,128)} %constant.96.clone) | copy-start | bytes 7077892
  13.6 6.5 %copy-start.10 = (f32[768]{0:T(1024)S(1)}, f32[768]{0:T(1024)}, u32[]{:S(2)}) copy-start(f32[768]{0:T(1024)} %constant.107.clone) | copy-start | bytes 9220
  13.6 6.6 %copy-start.11 = (f32[768]{0:T(1024)S(1)}, f32[768]{0:T(1024)}, u32[]{:S(2)}) copy-start(f32[768]{0:T(1024)} %constant.106.clone) | copy-start | bytes 9220
  13.6 38.9 %all-to-all-start = ((f32[16,48,768]{2,1,0:T(8,128)}), f32[16,48,768]{2,1,0:T(8,128)}, u32[]{:S(2)}, u32[]{:S(2)}) async-start(f32[16,48,768]{2,1,0:T(8,128)} %bitcast.60), calls=%async_computation | async-start | bytes 4718592 | tf_op jit(solution)/shard_map/all_to_all | solution.py:501
  57.1 9.6 %collective-permute-start = (f32[48,768]{1,0:T(8,128)}, f32[48,768]{1,0:T(8,128)S(1)}, u32[]{:S(2)}, u32[]{:S(2)}) collective-permute-start(f32[48,768]{1,0:T(8,128)} %get-tuple-element.25), channel_id=1, source_target_pairs={{0,16},{1,17},{2,18},{3,19},{4,20},{5,21},{6,22},{7,23},{8,24},{9,... | collective-permute-start | bytes 442376 | tf_op jit(solution)/shard_map/ppermute | solution.py:534
  66.6 0.7 copy-start.8
  67.3 7.8 %copy-start.6 = (f32[768,128,1]{1,0,2:T(8,128)S(1)}, f32[768,128,1]{1,0,2:T(8,128)}, u32[]{:S(2)}) copy-start(f32[768,128,1]{1,0,2:T(8,128)} %constant.110) | copy-start | bytes 1179652
  72.0 3.4 %copy-start.3 = (f32[16,48,768]{2,1,0:T(8,128)S(1)}, f32[16,48,768]{2,1,0:T(8,128)}, u32[]{:S(2)}) copy-start(f32[16,48,768]{2,1,0:T(8,128)} %get-tuple-element.26.u_ref) | copy-start | bytes 7077892
  72.0 6.9 %copy-start.4 = (f32[768,128]{1,0:T(8,128)S(1)}, f32[768,128]{1,0:T(8,128)}, u32[]{:S(2)}) copy-start(f32[768,128]{1,0:T(8,128)} %constant.97.clone) | copy-start | bytes 1179652
  72.0 7.0 %copy-start.7 = (f32[48,768]{1,0:T(8,128)S(1)}, f32[48,768]{1,0:T(8,128)}, u32[]{:S(2)}) copy-start(f32[48,768]{1,0:T(8,128)} %get-tuple-element.27) | copy-start | bytes 442372
  93.5 5.3 %collective-permute-start.1 = (f32[192,128]{1,0:T(8,128)}, f32[192,128]{1,0:T(8,128)S(1)}, u32[]{:S(2)}, u32[]{:S(2)}) collective-permute-start(f32[192,128]{1,0:T(8,128)} %reduce_sum.9), channel_id=1, source_target_pairs={{0,8},{8,0},{16,24},{24,16},{1,9},{9,1},{17,25},{25,17},{2,10},{10... | collective-permute-start | bytes 294920 | tf_op jit(solution)/shard_map/ppermute | solution.py:506
  99.7 7.3 %copy-start.5 = (f32[192,128]{1,0:T(8,128)}, f32[192,128]{1,0:T(8,128)S(1)}, u32[]{:S(2)}) copy-start(f32[192,128]{1,0:T(8,128)S(1)} %add.48.own_ref) | copy-start | bytes 294916
  99.7 7.3 %collective-permute-start.2 = (f32[192,128]{1,0:T(8,128)S(1)}, f32[192,128]{1,0:T(8,128)S(1)}, u32[]{:S(2)}, u32[]{:S(2)}) collective-permute-start(f32[192,128]{1,0:T(8,128)S(1)} %add.48.own_ref), channel_id=1, source_target_pairs={{0,16},{8,24},{16,0},{24,8},{1,17},{9,25},{17,1},{25,9},{2,18},{10... | collective-permute-start | bytes 294920 | tf_op jit(solution)/shard_map/ppermute | solution.py:506
  107.0 0.6 copy-start.9
  135.3 34.0 %copy-start.2 = (f32[768,768]{1,0:T(8,128)S(1)}, f32[768,768]{1,0:T(8,128)}, u32[]{:S(2)}) copy-start(f32[768,768]{1,0:T(8,128)} %constant.96.clone) | copy-start | bytes 7077892
where the time goes:
time: 181 us; the launch traced here: 180 us
  Pallas kernels  49.7 us (27%)
  blocking collectives  47.1 us (26%)
  matrix products  38.1 us (21%)
  waiting for transfers between devices  27.4 us (15%)
  starting transfers between devices  11.3 us (6%)
  local copies, waits for them, and re-layouts  3.78 us (2%)
  other arithmetic  2.43 us (1%)
    all_to_all x1, blocking collectives, exchange(): lax.all_to_all(x, AXES, split_axis=0, concat_axis=0, tiled=True, axis_ind...  34 us
    dot_general x12, matrix products, dot(): lax.dot_general(a, b, (dims, ((), ())), precision=precision, preferred_el...  31.1 us
    pallas_call x1, Pallas kernels, panel_potential(): pl.pallas_call(panels_body, out_shape=[jax.ShapeDtypeStruct((2, PANELS, P...  13.8 us
    all_gather x1, blocking collectives, on_device(): part = lax.all_gather(part, 'py', axis=0, tiled=False).sum(0)  13.1 us
    all_to_all x1, waiting for transfers between devices, exchange(): lax.all_to_all(x, AXES, split_axis=0, concat_axis=0, tiled=True, axis_ind...  10.8 us
    pallas_call x1, Pallas kernels, mixed_table(): pl.pallas_call(functools.partial(mixed_body, edge, depth), grid=(half,),...  10 us
    ppermute x2, waiting for transfers between devices, hop(): return lax.ppermute(x, 'px', [(i, i ^ bit) for i in range(slow)])  9.66 us
    pallas_call x1, Pallas kernels, corner_table(): pl.pallas_call(functools.partial(corner_body, edge, depth), grid=(hb // S...  7.58 us
  transfers between devices with their start and end apart: 4, of which 4 were waited for; matrix products, arithmetic and copies ran while one was open for 1% of the time, Pallas kernels for 11%

commit v1 on v0

--- a/solution.py
+++ b/solution.py
@@ -483,6 +483,242 @@
     )(upper, u, coef, join, row_value, col_value, along, across, near, far)
 
 
+def boundary_body(
+    half_ref, g_ref, coef_ref, join_ref, far_ref, row_ref, col_ref, fold_ref, mine_ref,
+    pick_row_ref, pick_col_ref, u_ref, part_ref, face_ref, rows_ref, cols_ref, stage_ref,
+):
+    planes, rows, width = g_ref.shape
+    upper = half_ref[0]
+    step = pl.program_id(0)
+
+    @pl.when(step == 0)
+    def _():
+        face_ref[...] = jnp.zeros_like(face_ref)
+        rows_ref[...] = jnp.zeros_like(rows_ref)
+        cols_ref[...] = jnp.zeros_like(cols_ref)
+
+    row_value, col_value = row_ref[...], col_ref[...]
+    value = (far_ref[...] + coef_ref[planes - 1] * g_ref[planes - 1]) * join_ref[...]
+    for j in range(planes - 1, -1, -1):
+        value = g_ref[j] + coef_ref[j] * value
+        u_ref[jnp.where(upper == 1, planes - 1 - j, j)] = value
+        by_row = value * row_value
+        total = by_row[:8]
+        for k in range(8, rows, 8):
+            total = total + by_row[k : k + 8]
+        stage_ref[8 * j : 8 * j + 8, :] = total
+        by_col = value * col_value
+        total = by_col[:, :PANELS]
+        for k in range(PANELS, width, PANELS):
+            total = total + by_col[:, k : k + PANELS]
+        cols_ref[:, j * PANELS : (j + 1) * PANELS] += total
+    fold = fold_ref[...]
+    face_ref[...] += dot(value, fold)
+    rows_ref[...] += dot(stage_ref[...], fold)
+
+    @pl.when(step == pl.num_programs(0) - 1)
+    def _():
+        mine = mine_ref[...]
+        part_ref[:PANELS, :] = dot(mine, face_ref[...], TN)
+        part_ref[PANELS : PANELS + 2 * planes, :] = dot(pick_row_ref[...], rows_ref[...])
+        part_ref[PANELS + 2 * planes :, :] = dot(
+            dot(cols_ref[...], pick_col_ref[...]), mine, TN
+        )
+
+
+def finish_boundary(upper, g, coef, join, far, row_value, col_value, fold, mine):
+    planes, rows, cols = g.shape
+    block, flat = block_specs(planes, rows)
+    pick_row = np.zeros((2, planes, planes, 8), np.float32)
+    pick_col = np.zeros((planes, PANELS, 2, planes), np.float32)
+    for j in range(planes):
+        for t in (0, 1):
+            pick_row[t, j, j, t::2] = 1.0
+            pick_col[j, t::2, t, j] = 1.0
+    whole = lambda shape: pl.BlockSpec(shape, lambda i, u: (0, 0))
+    f32 = jnp.float32
+    return pl.pallas_call(
+        boundary_body,
+        grid_spec=pltpu.PrefetchScalarGridSpec(
+            num_scalar_prefetch=1,
+            grid=(cols // WIDTH,),
+            in_specs=[
+                block,
+                block,
+                flat,
+                flat,
+                whole((rows, 1)),
+                pl.BlockSpec((1, WIDTH), lambda i, u: (0, i)),
+                pl.BlockSpec((WIDTH, PANELS), lambda i, u: (i, 0)),
+                whole((rows, PANELS)),
+                whole((2 * planes, 8 * planes)),
+                whole((planes * PANELS, 2 * planes)),
+            ],
+            out_specs=[block, whole((PANELS + 4 * planes, PANELS))],
+            scratch_shapes=[
+                pltpu.VMEM((rows, PANELS), f32),
+                pltpu.VMEM((8 * planes, PANELS), f32),
+                pltpu.VMEM((rows, planes * PANELS), f32),
+                pltpu.VMEM((8 * planes, WIDTH), f32),
+            ],
+        ),
+        out_shape=[
+            jax.ShapeDtypeStruct(g.shape, f32),
+            jax.ShapeDtypeStruct((PANELS + 4 * planes, PANELS), f32),
+        ],
+    )(
+        upper, g, coef, join, far, row_value, col_value, fold, mine,
+        pick_row.reshape(2 * planes, -1), pick_col.reshape(-1, 2 * planes),
+    )
+
+
+TINY = 2.0**-60
+GROUP = 16
+
+
+def weight_body(depth, place_ref, row_ref, col_ref, low_ref, high_ref):
+    place = place_ref[0]
+
+    def rows(index, _):
+        at = pl.ds(pl.multiple_of(index * GROUP, GROUP), GROUP)
+        diag = row_ref[at, :] + col_ref[...] + 2.0
+
+        def step(_, pair):
+            return pair[1], diag * pair[1] - pair[0]
+
+        zero = diag - diag
+        pair = (zero, zero + 1.0)
+        pair = lax.fori_loop(0, place - 1, step, pair)
+        near = pair[1]
+        pair = lax.fori_loop(0, depth + 1 - 2 * place, step, pair)
+        distant = pair[1]
+        pair = lax.fori_loop(0, place, step, pair)
+        scale = 1.0 / pair[1]
+        low_ref[at, :] = distant * scale
+        high_ref[at, :] = near * scale
+        return 0
+
+    lax.fori_loop(0, low_ref.shape[0] // GROUP, rows, 0)
+
+
+def weights(depth, place, row_eigen, col_eigen, block):
+    grid = row_eigen.shape[0]
+    out = jax.ShapeDtypeStruct((grid, grid), jnp.float32)
+    spec = pl.BlockSpec((block, grid), lambda i, u: (i, 0))
+    return pl.pallas_call(
+        functools.partial(weight_body, depth),
+        grid_spec=pltpu.PrefetchScalarGridSpec(
+            num_scalar_prefetch=1,
+            grid=(grid // block,),
+            in_specs=[
+                pl.BlockSpec((block, 1), lambda i, u: (i, 0)),
+                pl.BlockSpec((1, grid), lambda i, u: (0, 0)),
+            ],
+            out_specs=[spec, spec],
+        ),
+        out_shape=[out, out],
+        cost_estimate=pl.CostEstimate(
+            flops=4 * depth * grid * grid, bytes_accessed=8 * grid * grid, transcendentals=0
+        ),
+    )(place, row_eigen, col_eigen)
+
+
+def plane_body(
+    depth, place_ref, u_ref, low_ref, high_ref, row_eigen_ref, col_eigen_ref, row_ref, col_ref,
+    face_ref, side_ref, rows_fold_ref, fold_ref, out_ref, along_ref, across_ref, near_ref,
+    distant_ref,
+):
+    half = depth // 2
+    block, grid = u_ref.shape
+    place = place_ref[0]
+    levels = [k if k < half else half + depth - 1 - k for k in range(depth)]
+
+    @pl.when(pl.program_id(0) == 0)
+    def _():
+        along = dot(side_ref[0], fold_ref[...], NT) * (4.0 * TINY / col_ref[...])
+        odd = lax.broadcasted_iota(jnp.int32, (GROUP, grid), 0) % 2 == 1
+        for k, at in enumerate(levels):
+            even_row = along[at : at + 1, :]
+            odd_row = along[depth + at : depth + at + 1, :]
+            along_ref[k] = jnp.where(odd, odd_row, even_row)
+
+    rows_fold = rows_fold_ref[...]
+    across = dot(rows_fold, side_ref[1], NT) * (4.0 * TINY / row_ref[...])
+    near_ref[...] = 4.0 * dot(dot(rows_fold, face_ref[0]), fold_ref[...], NT)
+    distant_ref[...] = 4.0 * dot(dot(rows_fold, face_ref[1]), fold_ref[...], NT)
+    odd = lax.broadcasted_iota(jnp.int32, (block, PANELS), 1) % 2 == 1
+    for k, at in enumerate(levels):
+        across_ref[k] = jnp.where(
+            odd, across[:, depth + at : depth + at + 1], across[:, at : at + 1]
+        )
+    copies = grid // PANELS
+
+    def rows(index, _):
+        at = pl.ds(pl.multiple_of(index * GROUP, GROUP), GROUP)
+        diag = row_eigen_ref[at, :] + col_eigen_ref[...] + 2.0
+        zero = diag - diag
+
+        def layer(k):
+            return along_ref[k] + jnp.concatenate([across_ref[k, at, :]] * copies, 1)
+
+        def down(k, pair):
+            return layer(place - 1 - k) + (diag * pair[0] - pair[1]), pair[0]
+
+        def up(k, pair):
+            return layer(place + k) + (diag * pair[0] - pair[1]), pair[0]
+
+        lower = lax.fori_loop(0, place, down, (zero, zero))[0]
+        upper = lax.fori_loop(0, depth - place, up, (zero, zero))[0]
+        both = row_ref[at, :] * col_ref[...] * (1.0 / TINY)
+        out_ref[at, :] = (
+            u_ref[at, :]
+            + low_ref[at, :] * (both * lower + near_ref[at, :])
+            + high_ref[at, :] * (both * upper + distant_ref[at, :])
+        )
+        return 0
+
+    lax.fori_loop(0, block // GROUP, rows, 0)
+
+
+def plane_layers(depth, place, u, low, high, eigen, edge_value, face_v, side_v, fold, block):
+    grid = u.shape[0]
+    f32 = jnp.float32
+    wide = pl.BlockSpec((block, grid), lambda i, u: (i, 0))
+    tall = pl.BlockSpec((block, 1), lambda i, u: (i, 0))
+    flat = pl.BlockSpec((1, grid), lambda i, u: (0, 0))
+    return pl.pallas_call(
+        functools.partial(plane_body, depth),
+        grid_spec=pltpu.PrefetchScalarGridSpec(
+            num_scalar_prefetch=1,
+            grid=(grid // block,),
+            in_specs=[
+                wide,
+                wide,
+                wide,
+                tall,
+                flat,
+                tall,
+                flat,
+                pl.BlockSpec(face_v.shape, lambda i, u: (0, 0, 0)),
+                pl.BlockSpec(side_v.shape, lambda i, u: (0, 0, 0)),
+                pl.BlockSpec((block, PANELS), lambda i, u: (i, 0)),
+                pl.BlockSpec((grid, PANELS), lambda i, u: (0, 0)),
+            ],
+            out_specs=wide,
+            scratch_shapes=[
+                pltpu.VMEM((depth, GROUP, grid), f32),
+                pltpu.VMEM((depth, block, PANELS), f32),
+                pltpu.VMEM((block, grid), f32),
+                pltpu.VMEM((block, grid), f32),
+            ],
+        ),
+        out_shape=jax.ShapeDtypeStruct((grid, grid), f32),
+    )(
+        place, u, low, high, eigen[:, None], eigen[None, :], edge_value[:, None],
+        edge_value[None, :], face_v, side_v, fold, fold,
+    )
+
+
 def build(mesh, grid, depth):
     slow, fast = mesh.shape["px"], mesh.shape["py"]
     devices = slow * fast
@@ -490,6 +726,8 @@
     rows = grid // half
     edge = grid // PANELS
     groups = [list(range(half)), list(range(half, devices))]
+    local = depth <= 32 and rows % 8 == 0
+    block = grid // 8
     tables = {
         name: value.astype(np.float32) for name, value in small_tables(depth, grid, edge).items()
     }
@@ -529,19 +767,33 @@
         coef, join = factors(mu, half)
         mixed = mixed_table(edge, depth, tb["wave_x"])
         corner = corner_table(edge, depth, tb["lift"])
-        spectrum, mixed, corner = lax.optimization_barrier((spectrum, mixed, corner))
+        if local:
+            index = (rank % half).astype(jnp.int32)
+            place = jnp.where(is_upper, half - index, index + 1).reshape(1)
+            weight = weights(depth, place, eigen[:, None], eigen[None, :], block)
+            spectrum, mixed, corner, weight = lax.optimization_barrier(
+                (spectrum, mixed, corner, weight)
+            )
+        else:
+            spectrum, mixed, corner = lax.optimization_barrier((spectrum, mixed, corner))
         g, last = sweep(upper, spectrum, coef)
         far = lax.ppermute(last, AXES, [(i, i ^ half) for i in range(devices)])
-        u, outer = finish(upper, g, coef, join, far)
-
-        face = dot(my_fold, dot(outer, fold), ((0,), (0,)))
-        lines_y = jnp.einsum("tk,jkx->tjx", my_pair, u, precision=HIGHEST)
-        lines_y = jnp.einsum("tjx,xb->tjb", lines_y, fold, precision=HIGHEST)
-        lines_x = jnp.einsum("jkx,tx->tjk", u, edge_pair, precision=HIGHEST)
-        lines_x = jnp.einsum("tjk,kb->tjb", lines_x, my_fold, precision=HIGHEST)
-        lines = jnp.stack([lines_y, lines_x])
-        lines = jnp.where(is_upper, lines[:, :, ::-1], lines)
-        part = jnp.concatenate([face, lines.reshape(-1, PANELS)])
+        if local:
+            u, part = finish_boundary(
+                upper, g, coef, join, far, my_edge[:, None], edge_value[None, :], fold, my_fold
+            )
+            u = exchange(u).reshape(grid, grid)
+        else:
+            u, outer = finish(upper, g, coef, join, far)
+
+            face = dot(my_fold, dot(outer, fold), ((0,), (0,)))
+            lines_y = jnp.einsum("tk,jkx->tjx", my_pair, u, precision=HIGHEST)
+            lines_y = jnp.einsum("tjx,xb->tjb", lines_y, fold, precision=HIGHEST)
+            lines_x = jnp.einsum("jkx,tx->tjk", u, edge_pair, precision=HIGHEST)
+            lines_x = jnp.einsum("tjk,kb->tjb", lines_x, my_fold, precision=HIGHEST)
+            lines = jnp.stack([lines_y, lines_x])
+            lines = jnp.where(is_upper, lines[:, :, ::-1], lines)
+            part = jnp.concatenate([face, lines.reshape(-1, PANELS)])
         part = lax.all_gather(part, "py", axis=0, tiled=False).sum(0)
         bit = 1
         while bit < slow // 2:
@@ -549,15 +801,20 @@
             bit *= 2
         other = hop(part, bit)
         face_v, side_v = panel_potential(part, other, tb, mixed, corner)
-        near, distant = (
-            4.0 * dot(dot(my_fold, face_v[i]), fold, ((1,), (1,))) for i in (0, 1)
-        )
-        along = 4.0 * dot(side_v[0], fold, ((1,), (1,)))
-        across = 4.0 * dot(my_fold, side_v[1], ((1,), (1,)))
-        u = add_ghost(
-            upper, u, coef, join, my_edge[:, None], edge_value[None, :], along, across, near, distant
-        )
-        u = exchange(u).reshape(grid, grid)
+        if local:
+            u = plane_layers(
+                depth, place, u, *weight, eigen, edge_value, face_v, side_v, fold, block
+            )
+        else:
+            near, distant = (
+                4.0 * dot(dot(my_fold, face_v[i]), fold, ((1,), (1,))) for i in (0, 1)
+            )
+            along = 4.0 * dot(side_v[0], fold, ((1,), (1,)))
+            across = 4.0 * dot(my_fold, side_v[1], ((1,), (1,)))
+            u = add_ghost(
+                upper, u, coef, join, my_edge[:, None], edge_value[None, :], along, across, near, distant
+            )
+            u = exchange(u).reshape(grid, grid)
         return dot(dot(sine, u, precision=HIGH), sine, precision=HIGH)[None]
 
     return on_device

time: 181 us -> 216 us (1.19)
  Pallas kernels: 49.7 us -> 113 us
  waiting for transfers between devices: 27.4 us -> 14.2 us
  matrix products: 38.1 us -> 25.1 us
  blocking collectives: 47.1 us -> 37.7 us
  starting transfers between devices: 11.3 us -> 18 us
    pallas_call x2 -> x3, Pallas kernels: 10.8 us -> 74.4 us  [the longest x1 45.6 us: plane_layers(): pl.pallas_call(functools.partial(plane_body, depth), grid_spec=pltpu.Pref...]
    all_to_all x1 -> x0, blocking collectives: 34 us -> none  [exchange(): lax.all_to_all(x, AXES, split_axis=0, concat_axis=0, tiled=True, axis_ind...]
    all_gather x1, blocking collectives: 13.1 us -> 37.7 us  [on_device(): part = lax.all_gather(part, 'py', axis=0, tiled=False).sum(0)]
    all_to_all x1 -> x2, waiting for transfers between devices: 10.8 us -> 0.01 us  [exchange(): lax.all_to_all(x, AXES, split_axis=0, concat_axis=0, tiled=True, axis_ind...]
    dot_general x4 -> x0, matrix products: 6.97 us -> none  [the longest x1 3.46 us: on_device(): lines_x = jnp.einsum('jkx,tx->tjk', u, edge_pair, precision=HIGHEST)]
    dot_general x12 -> x4, matrix products: 31.1 us -> 25.1 us  [dot(): lax.dot_general(a, b, (dims, ((), ())), precision=precision, preferred_el...]
    all_to_all x1 -> x2, starting transfers between devices: 6.51 us -> 11.1 us  [exchange(): lax.all_to_all(x, AXES, split_axis=0, concat_axis=0, tiled=True, axis_ind...]
  transfers between devices with their start and end apart: 4 -> 5, of which waited for: 4 -> 3; matrix products, arithmetic and copies ran while one was open for 1% -> 2% of each run, Pallas kernels for 11% -> 26%
where the time goes in v1:
time: 216 us; the launch traced here: 215 us
  Pallas kernels  113 us (52%)
  blocking collectives  37.7 us (17%)
  matrix products  25.1 us (12%)
  starting transfers between devices  18 us (8%)
  waiting for transfers between devices  14.2 us (7%)
  local copies, waits for them, and re-layouts  5.85 us (3%)
    pallas_call x1, Pallas kernels, plane_layers(): pl.pallas_call(functools.partial(plane_body, depth), grid_spec=pltpu.Pref...  45.6 us
    all_gather x1, blocking collectives, on_device(): part = lax.all_gather(part, 'py', axis=0, tiled=False).sum(0)  37.7 us
    dot_general x4, matrix products, dot(): lax.dot_general(a, b, (dims, ((), ())), precision=precision, preferred_el...  25.1 us
    pallas_call x1, Pallas kernels, weights(): pl.pallas_call(functools.partial(weight_body, depth), grid_spec=pltpu.Pre...  21.8 us
    pallas_call x1, Pallas kernels, panel_potential(): pl.pallas_call(panels_body, out_shape=[jax.ShapeDtypeStruct((2, PANELS, P...  13.8 us
    all_to_all x2, starting transfers between devices, exchange(): lax.all_to_all(x, AXES, split_axis=0, concat_axis=0, tiled=True, axis_ind...  11.1 us
    pallas_call x1, Pallas kernels, mixed_table(): pl.pallas_call(functools.partial(mixed_body, edge, depth), grid=(half,),...  10.1 us
    ppermute x2, waiting for transfers between devices, hop(): return lax.ppermute(x, 'px', [(i, i ^ bit) for i in range(slow)])  9.39 us
  transfers between devices with their start and end apart: 5, of which 3 were waited for; matrix products, arithmetic and copies ran while one was open for 2% of the time, Pallas kernels for 26%

profile of v1, /device:TPU:0, one launch (start us, length us, event | category | flops | bytes accessed | tf_op | source)
XLA Modules:
  0.0 215.1 jit_solution(11611643082069087611)
XLA Ops:
  0.0 0.0 copy-start
  0.0 0.0 copy-start.1
  0.0 1.7 copy-done
  1.7 7.4 %fusion = f32[768,768]{1,0:T(8,128)S(1)} fusion(f32[768,768]{1,0:T(8,128)} %constant.76.clone, f32[1,768,768]{2,1,0:T(8,128)S(1)} %copy-done), kind=kOutput, calls=%fused_computation | convolution fusion | flops 2717908992 | bytes 7077888 | tf_op jit(solution)/shard_map/dot_general | solution.py:20
  9.1 0.0 copy-done.1
  9.1 4.5 %fusion.2 = f32[768,768]{1,0:T(8,128)} fusion(f32[768,768]{1,0:T(8,128)S(1)} %copy-done.1, f32[768,768]{1,0:T(8,128)S(1)} %fusion), kind=kOutput, calls=%fused_computation.6 | convolution fusion | flops 2717908992 | bytes 7077888 | tf_op jit(solution)/shard_map/dot_general | solution.py:20
  13.6 0.0 copy-start.7
  13.6 6.5 %all-to-all-start = ((f32[16,48,768]{2,1,0:T(8,128)}), f32[16,48,768]{2,1,0:T(8,128)}, u32[]{:S(2)}, u32[]{:S(2)}) async-start(f32[16,48,768]{2,1,0:T(8,128)} %bitcast.19), calls=%async_computation | async-start | bytes 4718592 | tf_op jit(solution)/shard_map/all_to_all | solution.py:739
  20.2 0.0 copy-done.7
  20.2 0.1 dynamic_slice.9
  20.2 0.7 broadcast_add_fusion.mu_ref
  21.0 3.0 %shard_map.148 = (f32[16,48,768]{2,1,0:T(8,128)}, f32[48,768]{1,0:T(8,128)}) custom-call(f32[48,768]{1,0:T(8,128)} %broadcast_add_fusion.mu_ref), custom_call_target="tpu_custom_call" | custom-call | flops 11796480 | bytes 2359296 | tf_op jit(solution)/shard_map/pallas_call | solution.py:357
  23.9 21.8 %shard_map.147 = (f32[768,768]{1,0:T(8,128)}, f32[768,768]{1,0:T(8,128)}) custom-call(s32[1]{0:T(128)} %bitcast.place_ref, f32[768,1]{1,0:T(8,128)} %constant.91.row_ref.row_eigen_ref, f32[1,768]{1,0:T(1,128)} %constant.92.col_ref.col_eigen_ref), custom_call_target="tpu_custom_call" | custom-call | flops 75497472 | bytes 4718592 | tf_op jit(solution)/shard_map/pallas_call | solution.py:608
  45.7 10.1 %shard_map.145.mixed_ref = f32[2,16,128,256]{3,2,1,0:T(8,128)} custom-call(f32[128,256]{1,0:T(8,128)} %constant.84.clone.wave_ref), custom_call_target="tpu_custom_call" | custom-call | flops 134217728 | bytes 2097152 | tf_op jit(solution)/shard_map/pallas_call | solution.py:91
  55.8 7.6 %shard_map.146 = (f32[64,64,128]{2,1,0:T(8,128)}, f32[64,64,128]{2,1,0:T(8,128)}) custom-call(f32[64,128]{1,0:T(8,128)} %constant.85.clone.wave_ref), custom_call_target="tpu_custom_call" | custom-call | flops 134217728 | bytes 2097152 | tf_op jit(solution)/shard_map/pallas_call | solution.py:141
  63.4 0.0 all-to-all-done.f_ref
  63.4 4.5 %shard_map.149 = (f32[16,48,768]{2,1,0:T(8,128)}, f32[48,768]{1,0:T(8,128)}) custom-call(s32[1]{0:T(128)} %bitcast.1.half_ref, f32[16,48,768]{2,1,0:T(8,128)} %all-to-all-done.f_ref, f32[16,48,768]{2,1,0:T(8,128)} %get-tuple-element.28.coef_ref), custom_call_target="tpu_custom_call" | custom-call | tf_op jit(solution)/shard_map/pallas_call | solution.py:386
  68.0 3.9 %collective-permute-start = (f32[48,768]{1,0:T(8,128)}, f32[48,768]{1,0:T(8,128)S(1)}, u32[]{:S(2)}, u32[]{:S(2)}) collective-permute-start(f32[48,768]{1,0:T(8,128)} %get-tuple-element.31), channel_id=1, source_target_pairs={{0,16},{1,17},{2,18},{3,19},{4,20},{5,21},{6,22},{7,23},{8,24},{9,... | collective-permute-start | bytes 442376 | tf_op jit(solution)/shard_map/ppermute | solution.py:780
  71.8 0.8 dynamic-slice_bitcast_fusion
  72.6 0.7 copy.16.row_ref
  73.3 1.3 constant_dynamic-slice_fusion.mine_ref
  74.6 4.8 %collective-permute-done.far_ref = f32[48,768]{1,0:T(8,128)S(1)} collective-permute-done((f32[48,768]{1,0:T(8,128)}, f32[48,768]{1,0:T(8,128)S(1)}, u32[]{:S(2)}, u32[]{:S(2)}) %collective-permute-start) | collective-permute-done | bytes 147488 | tf_op jit(solution)/shard_map/ppermute | solution.py:780
  79.4 0.0 copy-start.4
  79.4 0.6 copy-done.4
  80.1 7.0 %shard_map.150 = (f32[16,48,768]{2,1,0:T(8,128)}, f32[192,128]{1,0:T(8,128)}) custom-call(s32[1]{0:T(128)} %bitcast.1.half_ref, f32[16,48,768]{2,1,0:T(8,128)} %get-tuple-element.29.g_ref, f32[16,48,768]{2,1,0:T(8,128)} %get-tuple-element.28.coef_ref, f32[48,768]{1,0:T(8,128)} %get-tuple-element.30.join_ref, f32[48,768]{1,0:T(8,128)} %copy-done.4, ...), custom_call_target="tpu_custom_call" | custom-call | tf_op jit(solution)/shard_map/pallas_call | solution.py:540
  87.1 0.0 copy-start.6
  87.1 4.6 %all-to-all-start.1 = ((f32[16,48,768]{2,1,0:T(8,128)}), f32[16,48,768]{2,1,0:T(8,128)}, u32[]{:S(2)}, u32[]{:S(2)}) async-start(f32[16,48,768]{2,1,0:T(8,128)} %get-tuple-element.32), calls=%async_computation.1 | async-start | bytes 4718592 | tf_op jit(solution)/shard_map/all_to_all | solution.py:739
  91.7 0.0 copy-done.6
  91.8 37.7 %all-gather = f32[1536,128]{1,0:T(8,128)S(1)} all-gather(f32[192,128]{1,0:T(8,128)S(1)} %copy-done.6), channel_id=2, replica_groups=mesh['px'=4,'py'=8] {'py'}, dimensions={0}, use_global_device_ids=true | all-gather | bytes 884736 | tf_op jit(solution)/shard_map/all_gather | solution.py:797
  129.5 1.0 collective-permute-start.1
  130.5 4.1 %collective-permute-done.1 = f32[192,128]{1,0:T(8,128)S(1)} collective-permute-done((f32[192,128]{1,0:T(8,128)S(1)}, f32[192,128]{1,0:T(8,128)S(1)}, u32[]{:S(2)}, u32[]{:S(2)}) %collective-permute-start.1) | collective-permute-done | bytes 98336 | tf_op jit(solution)/shard_map/ppermute | solution.py:744
  134.6 0.0 copy-start.3
  134.7 2.0 collective-permute-start.2
  136.7 5.3 %collective-permute-done.2.other_ref = f32[192,128]{1,0:T(8,128)S(1)} collective-permute-done((f32[192,128]{1,0:T(8,128)S(1)}, f32[192,128]{1,0:T(8,128)S(1)}, u32[]{:S(2)}, u32[]{:S(2)}) %collective-permute-start.2) | collective-permute-done | bytes 98336 | tf_op jit(solution)/shard_map/ppermute | solution.py:744
  141.9 0.0 copy-done.3
  141.9 0.0 copy-start.5
  141.9 0.6 copy-done.5
  142.6 13.8 %shard_map.151 = (f32[2,128,128]{2,1,0:T(8,128)}, f32[2,64,128]{2,1,0:T(8,128)}) custom-call(f32[192,128]{1,0:T(8,128)} %copy-done.3, f32[192,128]{1,0:T(8,128)} %copy-done.5, f32[256,128]{1,0:T(8,128)} %constant.78.clone.basis_ref, f32[2,256,256]{2,1,0:T(8,128)} %constant.79.clone.face_ref, f32[128,256]{1,0:T(8,128)} %constant.80.clone.side_ref, ...), custom_call_target="tpu_custom_call" | custom-call | tf_op jit(solution)/shard_map/pallas_call | solution.py:312
  156.4 0.0 all-to-all-done.1
  156.4 45.6 %shard_map.152 = f32[768,768]{1,0:T(8,128)} custom-call(s32[1]{0:T(128)} %bitcast.place_ref, f32[768,768]{1,0:T(8,128)} %bitcast.5.u_ref, f32[768,768]{1,0:T(8,128)} %get-tuple-element.33.low_ref, f32[768,768]{1,0:T(8,128)} %get-tuple-element.34.high_ref, f32[768,1]{1,0:T(8,128)} %constant.91.row_ref.row_eigen_ref, f32[1,768]{1,0:T(1,128)} %constant.92.col_ref.col_eigen_ref, ...), custom_call_target="tpu_custom_call" | custom-call | tf_op jit(solution)/shard_map/pallas_call | solution.py:689
  201.9 0.0 copy-start.2
  201.9 8.3 %fusion.3 = f32[768,768]{1,0:T(8,128)S(1)} fusion(f32[768,768]{1,0:T(8,128)} %shard_map.152, f32[768,768]{1,0:T(8,128)} %constant.76.clone), kind=kOutput, calls=%fused_computation.7 | convolution fusion | flops 2717908992 | bytes 7077888 | tf_op jit(solution)/shard_map/dot_general | solution.py:20
  210.2 0.0 copy-done.2
  210.2 4.9 %convolution_bitcast_fusion = f32[1,768,768]{2,1,0:T(8,128)} fusion(f32[768,768]{1,0:T(8,128)S(1)} %fusion.3, f32[768,768]{1,0:T(8,128)S(1)} %copy-done.2), kind=kOutput, calls=%fused_computation.2 | convolution fusion | flops 2717908992 | bytes 7077888 | tf_op jit(solution)/shard_map/dot_general | solution.py:20
  (2 shorter events, 0.1 us)
Async XLA Ops:
  0.0 1.7 copy-start
  0.0 9.1 %copy-start.1 = (f32[768,768]{1,0:T(8,128)S(1)}, f32[768,768]{1,0:T(8,128)}, u32[]{:S(2)}) copy-start(f32[768,768]{1,0:T(8,128)} %constant.76.clone) | copy-start | bytes 7077892
  13.6 6.6 %copy-start.7 = (f32[768]{0:T(1024)S(1)}, f32[768]{0:T(1024)}, u32[]{:S(2)}) copy-start(f32[768]{0:T(1024)} %constant.86.clone) | copy-start | bytes 9220
  13.6 49.8 %all-to-all-start = ((f32[16,48,768]{2,1,0:T(8,128)}), f32[16,48,768]{2,1,0:T(8,128)}, u32[]{:S(2)}, u32[]{:S(2)}) async-start(f32[16,48,768]{2,1,0:T(8,128)} %bitcast.19), calls=%async_computation | async-start | bytes 4718592 | tf_op jit(solution)/shard_map/all_to_all | solution.py:739
  68.0 11.5 %collective-permute-start = (f32[48,768]{1,0:T(8,128)}, f32[48,768]{1,0:T(8,128)S(1)}, u32[]{:S(2)}, u32[]{:S(2)}) collective-permute-start(f32[48,768]{1,0:T(8,128)} %get-tuple-element.31), channel_id=1, source_target_pairs={{0,16},{1,17},{2,18},{3,19},{4,20},{5,21},{6,22},{7,23},{8,24},{9,... | collective-permute-start | bytes 442376 | tf_op jit(solution)/shard_map/ppermute | solution.py:780
  79.4 0.6 copy-start.4
  87.1 4.6 %copy-start.6 = (f32[192,128]{1,0:T(8,128)S(1)}, f32[192,128]{1,0:T(8,128)}, u32[]{:S(2)}) copy-start(f32[192,128]{1,0:T(8,128)} %get-tuple-element.35) | copy-start | bytes 294916
  87.1 69.2 %all-to-all-start.1 = ((f32[16,48,768]{2,1,0:T(8,128)}), f32[16,48,768]{2,1,0:T(8,128)}, u32[]{:S(2)}, u32[]{:S(2)}) async-start(f32[16,48,768]{2,1,0:T(8,128)} %get-tuple-element.32), calls=%async_computation.1 | async-start | bytes 4718592 | tf_op jit(solution)/shard_map/all_to_all | solution.py:739
  129.5 5.1 %collective-permute-start.1 = (f32[192,128]{1,0:T(8,128)S(1)}, f32[192,128]{1,0:T(8,128)S(1)}, u32[]{:S(2)}, u32[]{:S(2)}) collective-permute-start(f32[192,128]{1,0:T(8,128)S(1)} %reduce_sum.9), channel_id=1, source_target_pairs={{0,8},{8,0},{16,24},{24,16},{1,9},{9,1},{17,25},{25,17},{2,10},{10... | collective-permute-start | bytes 294920 | tf_op jit(solution)/shard_map/ppermute | solution.py:744
  134.6 7.3 %copy-start.3 = (f32[192,128]{1,0:T(8,128)}, f32[192,128]{1,0:T(8,128)S(1)}, u32[]{:S(2)}) copy-start(f32[192,128]{1,0:T(8,128)S(1)} %add.40.own_ref) | copy-start | bytes 294916
  134.7 7.3 %collective-permute-start.2 = (f32[192,128]{1,0:T(8,128)S(1)}, f32[192,128]{1,0:T(8,128)S(1)}, u32[]{:S(2)}, u32[]{:S(2)}) collective-permute-start(f32[192,128]{1,0:T(8,128)S(1)} %add.40.own_ref), channel_id=1, source_target_pairs={{0,16},{8,24},{16,0},{24,8},{1,17},{9,25},{17,1},{25,9},{2,18},{10... | collective-permute-start | bytes 294920 | tf_op jit(solution)/shard_map/ppermute | solution.py:744
  141.9 0.6 copy-start.5
  201.9 8.3 %copy-start.2 = (f32[768,768]{1,0:T(8,128)S(1)}, f32[768,768]{1,0:T(8,128)}, u32[]{:S(2)}) copy-start(f32[768,768]{1,0:T(8,128)} %constant.76.clone) | copy-start | bytes 7077892

commit v2 on v1

--- a/solution.py
+++ b/solution.py
@@ -53,18 +53,75 @@
     return np.where(distance == 0, 1.0, 2.0) * np.cos(np.pi * distance * order / n)
 
 
+def halves(value):
+    high = value.astype(jnp.bfloat16)
+    return high, (value - high.astype(jnp.float32)).astype(jnp.bfloat16)
+
+
+def bf16_dot(a, b):
+    return lax.dot_general(a, b, (((1,), (0,)), ((), ())), preferred_element_type=jnp.float32)
+
+
+STRIPE = 256
+
+
+def product_body(count, high_ref, low_ref, *refs):
+    in_refs, out_ref, mid_high_ref, mid_low_ref = refs[:count], *refs[count:]
+    grid = out_ref.shape[0]
+
+    def first(index, _):
+        at = pl.ds(pl.multiple_of(index * STRIPE, STRIPE), STRIPE)
+        value = in_refs[0][at, :]
+        if count == 3:
+            value = jnp.concatenate([value + in_refs[1][at, :], in_refs[2][at, :]], 1)
+        high, low = halves(value)
+        value = bf16_dot(high, high_ref[...])
+        value = value + bf16_dot(high, low_ref[...])
+        value = value + bf16_dot(low, high_ref[...])
+        high, low = halves(value)
+        mid_high_ref[at, :] = high
+        mid_low_ref[at, :] = low
+        return 0
+
+    lax.fori_loop(0, grid // STRIPE, first, 0)
+
+    def second(index, _):
+        at = pl.ds(pl.multiple_of(index * STRIPE, STRIPE), STRIPE)
+        value = bf16_dot(high_ref[at, :], mid_high_ref[...])
+        value = value + bf16_dot(high_ref[at, :], mid_low_ref[...])
+        value = value + bf16_dot(low_ref[at, :], mid_high_ref[...])
+        out_ref[at, :] = value
+        return 0
+
+    lax.fori_loop(0, grid // STRIPE, second, 0)
+
+
+def double_product(values, high, low):
+    grid = high.shape[0]
+    return pl.pallas_call(
+        functools.partial(product_body, len(values)),
+        out_shape=jax.ShapeDtypeStruct((grid, grid), jnp.float32),
+        scratch_shapes=[
+            pltpu.VMEM((grid, grid), jnp.bfloat16),
+            pltpu.VMEM((grid, grid), jnp.bfloat16),
+        ],
+    )(high, low, *values)
+
+
 def distance_power(*squares):
     return lax.rsqrt(functools.reduce(lambda a, b: a + b, squares))
 
 
 def iota(shape, axis):
     return lax.broadcasted_iota(jnp.int32, shape, axis).astype(jnp.float32)
+
+
+LEVELS = 4
 
 
 def mixed_body(edge, depth, wave_ref, out_ref):
     hb = PANELS // 2
     soft = edge * edge / 4.0
-    level = (pl.program_id(0) + 1).astype(jnp.float32)
     shape = (hb, PANELS)
     first = (edge - 1) / 2.0 + 1.0
     front = iota(shape, 0) * edge + first
@@ -73,26 +130,30 @@
     along = along * along + soft
     front = front * front + along
     back = back * back + along
-    own = level * level
-    far = (depth + 1.0 - level) * (depth + 1.0 - level)
-    own_front, own_back = distance_power(front, own), distance_power(back, own)
-    far_front, far_back = distance_power(front, far), distance_power(back, far)
     rows = []
-    for sign in (1.0, -1.0):
-        one, two = own_front + sign * far_front, own_back + sign * far_back
-        rows += [one + two, one - two]
+    for k in range(LEVELS):
+        level = (pl.program_id(0) * LEVELS + k + 1).astype(jnp.float32)
+        own = level * level
+        far = (depth + 1.0 - level) * (depth + 1.0 - level)
+        own_front, own_back = distance_power(front, own), distance_power(back, own)
+        far_front, far_back = distance_power(front, far), distance_power(back, far)
+        for sign in (1.0, -1.0):
+            one, two = own_front + sign * far_front, own_back + sign * far_back
+            rows += [one + two, one - two]
     value = dot(jnp.concatenate(rows, 0), wave_ref[...])
-    out_ref[0, 0] = value[:PANELS]
-    out_ref[1, 0] = value[PANELS:]
+    for k in range(LEVELS):
+        for s in (0, 1):
+            at = (2 * k + s) * PANELS
+            out_ref[s, k] = value[at : at + PANELS]
 
 
 def mixed_table(edge, depth, wave):
     half = depth // 2
     return pl.pallas_call(
         functools.partial(mixed_body, edge, depth),
-        grid=(half,),
+        grid=(half // LEVELS,),
         in_specs=[pl.BlockSpec((PANELS, 2 * PANELS), lambda i: (0, 0))],
-        out_specs=pl.BlockSpec((2, 1, PANELS, 2 * PANELS), lambda i: (0, i, 0, 0)),
+        out_specs=pl.BlockSpec((2, LEVELS, PANELS, 2 * PANELS), lambda i: (0, i, 0, 0)),
         out_shape=jax.ShapeDtypeStruct((2, half, PANELS, 2 * PANELS), jnp.float32),
         cost_estimate=pl.CostEstimate(
             flops=2 * depth * PANELS**3, bytes_accessed=4 * depth * PANELS * PANELS,
@@ -332,9 +393,9 @@
 WIDTH = 256
 
 
-def block_specs(planes, rows):
-    block = pl.BlockSpec((planes, rows, WIDTH), lambda i, *_: (0, 0, i))
-    flat = pl.BlockSpec((rows, WIDTH), lambda i, *_: (0, i))
+def block_specs(planes, rows, width=WIDTH, first=0):
+    block = pl.BlockSpec((planes, rows, width), lambda i, *_: (0, 0, i + first))
+    flat = pl.BlockSpec((rows, width), lambda i, *_: (0, i + first))
     return block, flat
 
 
@@ -457,27 +518,28 @@
         out_ref[place] = u_ref[place] + value
 
 
-def add_ghost(upper, u, coef, join, row_value, col_value, along, across, near, far):
+def add_ghost(upper, u, coef, join, row_value, col_value, along, across, near, far, width=WIDTH, first=0):
     planes, rows, cols = u.shape
-    block, flat = block_specs(planes, rows)
+    block, flat = block_specs(planes, rows, width)
+    far_block, far_flat = block_specs(planes, rows, width, first)
     return pl.pallas_call(
         ghost_body,
         grid_spec=pltpu.PrefetchScalarGridSpec(
             num_scalar_prefetch=1,
-            grid=(cols // WIDTH,),
+            grid=(cols // width,),
             in_specs=[
                 block,
-                block,
-                flat,
+                far_block,
+                far_flat,
                 pl.BlockSpec((rows, 1), lambda i, u: (0, 0)),
-                pl.BlockSpec((1, WIDTH), lambda i, u: (0, i)),
-                pl.BlockSpec((4 * planes, WIDTH), lambda i, u: (0, i)),
+                pl.BlockSpec((1, width), lambda i, u: (0, i + first)),
+                pl.BlockSpec((4 * planes, width), lambda i, u: (0, i)),
                 pl.BlockSpec((rows, 4 * planes), lambda i, u: (0, 0)),
                 flat,
                 flat,
             ],
             out_specs=block,
-            scratch_shapes=[pltpu.VMEM((planes, rows, WIDTH), jnp.float32)],
+            scratch_shapes=[pltpu.VMEM((planes, rows, width), jnp.float32)],
         ),
         out_shape=jax.ShapeDtypeStruct(u.shape, jnp.float32),
     )(upper, u, coef, join, row_value, col_value, along, across, near, far)
@@ -485,7 +547,8 @@
 
 def boundary_body(
     half_ref, g_ref, coef_ref, join_ref, far_ref, row_ref, col_ref, fold_ref, mine_ref,
-    pick_row_ref, pick_col_ref, u_ref, part_ref, face_ref, rows_ref, cols_ref, stage_ref,
+    pick_row_ref, pick_col_ref, front_ref, back_ref, part_ref, face_ref, rows_ref, cols_ref,
+    stage_ref, u_ref,
 ):
     planes, rows, width = g_ref.shape
     upper = half_ref[0]
@@ -512,6 +575,12 @@
         for k in range(PANELS, width, PANELS):
             total = total + by_col[:, k : k + PANELS]
         cols_ref[:, j * PANELS : (j + 1) * PANELS] += total
+    for target, turn in ((front_ref, 0), (back_ref, 1)):
+
+        @pl.when(step == turn)
+        def _(target=target):
+            target[...] = u_ref[...]
+
     fold = fold_ref[...]
     face_ref[...] += dot(value, fold)
     rows_ref[...] += dot(stage_ref[...], fold)
@@ -528,7 +597,9 @@
 
 def finish_boundary(upper, g, coef, join, far, row_value, col_value, fold, mine):
     planes, rows, cols = g.shape
-    block, flat = block_specs(planes, rows)
+    width = cols // 2
+    block, flat = block_specs(planes, rows, width)
+    still = pl.BlockSpec((planes, rows, width), lambda i, u: (0, 0, 0))
     pick_row = np.zeros((2, planes, planes, 8), np.float32)
     pick_col = np.zeros((planes, PANELS, 2, planes), np.float32)
     for j in range(planes):
@@ -541,29 +612,31 @@
         boundary_body,
         grid_spec=pltpu.PrefetchScalarGridSpec(
             num_scalar_prefetch=1,
-            grid=(cols // WIDTH,),
+            grid=(2,),
             in_specs=[
                 block,
                 block,
                 flat,
                 flat,
                 whole((rows, 1)),
-                pl.BlockSpec((1, WIDTH), lambda i, u: (0, i)),
-                pl.BlockSpec((WIDTH, PANELS), lambda i, u: (i, 0)),
+                pl.BlockSpec((1, width), lambda i, u: (0, i)),
+                pl.BlockSpec((width, PANELS), lambda i, u: (i, 0)),
                 whole((rows, PANELS)),
                 whole((2 * planes, 8 * planes)),
                 whole((planes * PANELS, 2 * planes)),
             ],
-            out_specs=[block, whole((PANELS + 4 * planes, PANELS))],
+            out_specs=[still, still, whole((PANELS + 4 * planes, PANELS))],
             scratch_shapes=[
                 pltpu.VMEM((rows, PANELS), f32),
                 pltpu.VMEM((8 * planes, PANELS), f32),
                 pltpu.VMEM((rows, planes * PANELS), f32),
-                pltpu.VMEM((8 * planes, WIDTH), f32),
+                pltpu.VMEM((8 * planes, width), f32),
+                pltpu.VMEM((planes, rows, width), f32),
             ],
         ),
         out_shape=[
-            jax.ShapeDtypeStruct(g.shape, f32),
+            jax.ShapeDtypeStruct((planes, rows, width), f32),
+            jax.ShapeDtypeStruct((planes, rows, width), f32),
             jax.ShapeDtypeStruct((PANELS + 4 * planes, PANELS), f32),
         ],
     )(
@@ -573,27 +646,47 @@
 
 
 TINY = 2.0**-60
-GROUP = 16
+GROUP = 32
+UNROLL = 4
+TALL = 24
+LANES = 384
+
+
+def whole_steps(count):
+    return (count + UNROLL - 1) // UNROLL * UNROLL
 
 
 def weight_body(depth, place_ref, row_ref, col_ref, low_ref, high_ref):
     place = place_ref[0]
+    first_steps = whole_steps(place - 1)
+    behind = (first_steps - (place - 1)).astype(jnp.float32)
+    pairs = depth // 2 - place
 
     def rows(index, _):
         at = pl.ds(pl.multiple_of(index * GROUP, GROUP), GROUP)
         diag = row_ref[at, :] + col_ref[...] + 2.0
 
-        def step(_, pair):
-            return pair[1], diag * pair[1] - pair[0]
+        def advance(count, pair):
+            for _ in range(count):
+                pair = (pair[1], diag * pair[1] - pair[0])
+            return pair
 
         zero = diag - diag
-        pair = (zero, zero + 1.0)
-        pair = lax.fori_loop(0, place - 1, step, pair)
-        near = pair[1]
-        pair = lax.fori_loop(0, depth + 1 - 2 * place, step, pair)
+        back, here = zero, zero + 1.0
+        for k in range(1, UNROLL):
+            step = diag * back - here
+            take = behind >= k
+            back, here = jnp.where(take, step, back), jnp.where(take, back, here)
+        pair = lax.fori_loop(
+            0, first_steps // UNROLL, lambda _, pair: advance(UNROLL, pair), (back, here)
+        )
+        before, near = pair
+        pair = advance(1, pair)
+        pair = lax.fori_loop(0, pairs // 2, lambda _, pair: advance(4, pair), pair)
+        pair = lax.fori_loop(0, pairs % 2, lambda _, pair: advance(2, pair), pair)
         distant = pair[1]
-        pair = lax.fori_loop(0, place, step, pair)
-        scale = 1.0 / pair[1]
+        after = diag * distant - pair[0]
+        scale = 1.0 / (near * after - before * distant)
         low_ref[at, :] = distant * scale
         high_ref[at, :] = near * scale
         return 0
@@ -602,9 +695,9 @@
 
 
 def weights(depth, place, row_eigen, col_eigen, block):
-    grid = row_eigen.shape[0]
-    out = jax.ShapeDtypeStruct((grid, grid), jnp.float32)
-    spec = pl.BlockSpec((block, grid), lambda i, u: (i, 0))
+    grid, cols = row_eigen.shape[0], col_eigen.shape[1]
+    out = jax.ShapeDtypeStruct((grid, cols), jnp.float32)
+    spec = pl.BlockSpec((block, cols), lambda i, u: (i, 0))
     return pl.pallas_call(
         functools.partial(weight_body, depth),
         grid_spec=pltpu.PrefetchScalarGridSpec(
@@ -612,80 +705,109 @@
             grid=(grid // block,),
             in_specs=[
                 pl.BlockSpec((block, 1), lambda i, u: (i, 0)),
-                pl.BlockSpec((1, grid), lambda i, u: (0, 0)),
+                pl.BlockSpec((1, cols), lambda i, u: (0, 0)),
             ],
             out_specs=[spec, spec],
         ),
         out_shape=[out, out],
         cost_estimate=pl.CostEstimate(
-            flops=4 * depth * grid * grid, bytes_accessed=8 * grid * grid, transcendentals=0
+            flops=4 * depth * grid * cols, bytes_accessed=8 * grid * cols, transcendentals=0
         ),
     )(place, row_eigen, col_eigen)
 
 
 def plane_body(
-    depth, place_ref, u_ref, low_ref, high_ref, row_eigen_ref, col_eigen_ref, row_ref, col_ref,
-    face_ref, side_ref, rows_fold_ref, fold_ref, out_ref, along_ref, across_ref, near_ref,
-    distant_ref,
+    depth, place_ref, low_ref, high_ref, row_eigen_ref, col_eigen_ref, row_ref, col_ref,
+    near_ref, distant_ref, side_ref, rows_fold_ref, fold_ref, out_ref, along_ref, across_ref,
+    pick_ref,
 ):
     half = depth // 2
-    block, grid = u_ref.shape
+    block, grid = out_ref.shape
     place = place_ref[0]
     levels = [k if k < half else half + depth - 1 - k for k in range(depth)]
+    base = whole_steps(half)
+    lower_steps = whole_steps(place)
+    upper_steps = whole_steps(depth - place)
+
+    def slot(k):
+        return jnp.where(
+            k < place, lower_steps - 1 - k, base + upper_steps - depth + k
+        )
 
     @pl.when(pl.program_id(0) == 0)
     def _():
         along = dot(side_ref[0], fold_ref[...], NT) * (4.0 * TINY / col_ref[...])
-        odd = lax.broadcasted_iota(jnp.int32, (GROUP, grid), 0) % 2 == 1
+        odd = lax.broadcasted_iota(jnp.int32, (8, grid), 0) % 2 == 1
+        for k in range(UNROLL - 1):
+            along_ref[k] = jnp.zeros((8, grid), jnp.float32)
+            along_ref[base + k] = jnp.zeros((8, grid), jnp.float32)
+            across_ref[k] = jnp.zeros((block, PANELS), jnp.float32)
+            across_ref[base + k] = jnp.zeros((block, PANELS), jnp.float32)
         for k, at in enumerate(levels):
             even_row = along[at : at + 1, :]
             odd_row = along[depth + at : depth + at + 1, :]
-            along_ref[k] = jnp.where(odd, odd_row, even_row)
-
-    rows_fold = rows_fold_ref[...]
-    across = dot(rows_fold, side_ref[1], NT) * (4.0 * TINY / row_ref[...])
-    near_ref[...] = 4.0 * dot(dot(rows_fold, face_ref[0]), fold_ref[...], NT)
-    distant_ref[...] = 4.0 * dot(dot(rows_fold, face_ref[1]), fold_ref[...], NT)
-    odd = lax.broadcasted_iota(jnp.int32, (block, PANELS), 1) % 2 == 1
-    for k, at in enumerate(levels):
-        across_ref[k] = jnp.where(
-            odd, across[:, depth + at : depth + at + 1], across[:, at : at + 1]
-        )
-    copies = grid // PANELS
-
-    def rows(index, _):
-        at = pl.ds(pl.multiple_of(index * GROUP, GROUP), GROUP)
-        diag = row_eigen_ref[at, :] + col_eigen_ref[...] + 2.0
-        zero = diag - diag
-
-        def layer(k):
-            return along_ref[k] + jnp.concatenate([across_ref[k, at, :]] * copies, 1)
-
-        def down(k, pair):
-            return layer(place - 1 - k) + (diag * pair[0] - pair[1]), pair[0]
-
-        def up(k, pair):
-            return layer(place + k) + (diag * pair[0] - pair[1]), pair[0]
-
-        lower = lax.fori_loop(0, place, down, (zero, zero))[0]
-        upper = lax.fori_loop(0, depth - place, up, (zero, zero))[0]
-        both = row_ref[at, :] * col_ref[...] * (1.0 / TINY)
-        out_ref[at, :] = (
-            u_ref[at, :]
-            + low_ref[at, :] * (both * lower + near_ref[at, :])
-            + high_ref[at, :] * (both * upper + distant_ref[at, :])
-        )
-        return 0
-
-    lax.fori_loop(0, block // GROUP, rows, 0)
-
-
-def plane_layers(depth, place, u, low, high, eigen, edge_value, face_v, side_v, fold, block):
-    grid = u.shape[0]
+            along_ref[slot(k)] = jnp.where(odd, odd_row, even_row)
+        shape = (2 * depth, depth * PANELS)
+        column = lax.broadcasted_iota(jnp.int32, shape, 1)
+        row = lax.broadcasted_iota(jnp.int32, shape, 0)
+        layer = column // PANELS
+        layer = jnp.where(layer < half, layer, half + depth - 1 - layer)
+        pick = jnp.where(row == (column % 2) * depth + layer, 1.0, 0.0).astype(jnp.bfloat16)
+        for k in range(3):
+            pick_ref[2 * depth * k : 2 * depth * (k + 1), :] = pick
+
+    across = dot(rows_fold_ref[...], side_ref[1], NT) * (4.0 * TINY / row_ref[...])
+    high = across.astype(jnp.bfloat16)
+    rest = across - high.astype(jnp.float32)
+    middle = rest.astype(jnp.bfloat16)
+    low = (rest - middle.astype(jnp.float32)).astype(jnp.bfloat16)
+    across = jnp.concatenate([high, middle, low], 1)
+    for k in range(0, depth, 2):
+        pair = bf16_dot(across, pick_ref[:, k * PANELS : (k + 2) * PANELS])
+        across_ref[slot(k)] = pair[:, :PANELS]
+        across_ref[slot(k + 1)] = pair[:, PANELS:]
+
+    for part in range(grid // LANES):
+        lanes = slice(part * LANES, (part + 1) * LANES)
+
+        def rows(index, _, lanes=lanes):
+            at = pl.ds(pl.multiple_of(index * TALL, 8), TALL)
+            diag = row_eigen_ref[at, :] + col_eigen_ref[:, lanes] + 2.0
+            zero = diag - diag
+
+            def run(first, steps):
+                def leap(turn, pair):
+                    one, two = pair
+                    for k in range(UNROLL):
+                        here = first + turn * UNROLL + k
+                        along = along_ref[here, :, lanes]
+                        across = across_ref[here, at, :]
+                        layer = jnp.concatenate([along] * (TALL // 8), 0) + jnp.concatenate(
+                            [across] * (LANES // PANELS), 1
+                        )
+                        one, two = (layer - two) + diag * one, one
+                    return one, two
+
+                return lax.fori_loop(0, steps // UNROLL, leap, (zero, zero))[0]
+
+            lower = run(0, lower_steps)
+            upper = run(base, upper_steps)
+            both = row_ref[at, :] * col_ref[:, lanes] * (1.0 / TINY)
+            out_ref[at, lanes] = low_ref[at, lanes] * (
+                both * lower + near_ref[at, lanes]
+            ) + high_ref[at, lanes] * (both * upper + distant_ref[at, lanes])
+            return 0
+
+        lax.fori_loop(0, block // TALL, rows, 0)
+
+
+def plane_layers(depth, place, low, high, eigen, edge_value, near, distant, side_v, fold, block):
+    grid, cols = low.shape
+    slots = whole_steps(depth // 2) + whole_steps(depth)
     f32 = jnp.float32
-    wide = pl.BlockSpec((block, grid), lambda i, u: (i, 0))
+    wide = pl.BlockSpec((block, cols), lambda i, u: (i, 0))
     tall = pl.BlockSpec((block, 1), lambda i, u: (i, 0))
-    flat = pl.BlockSpec((1, grid), lambda i, u: (0, 0))
+    flat = pl.BlockSpec((1, cols), lambda i, u: (0, 0))
     return pl.pallas_call(
         functools.partial(plane_body, depth),
         grid_spec=pltpu.PrefetchScalarGridSpec(
@@ -694,28 +816,30 @@
             in_specs=[
                 wide,
                 wide,
-                wide,
                 tall,
                 flat,
                 tall,
                 flat,
-                pl.BlockSpec(face_v.shape, lambda i, u: (0, 0, 0)),
+                wide,
+                wide,
                 pl.BlockSpec(side_v.shape, lambda i, u: (0, 0, 0)),
                 pl.BlockSpec((block, PANELS), lambda i, u: (i, 0)),
-                pl.BlockSpec((grid, PANELS), lambda i, u: (0, 0)),
+                pl.BlockSpec((cols, PANELS), lambda i, u: (0, 0)),
             ],
             out_specs=wide,
             scratch_shapes=[
-                pltpu.VMEM((depth, GROUP, grid), f32),
-                pltpu.VMEM((depth, block, PANELS), f32),
-                pltpu.VMEM((block, grid), f32),
-                pltpu.VMEM((block, grid), f32),
+                pltpu.VMEM((slots, 8, cols), f32),
+                pltpu.VMEM((slots, block, PANELS), f32),
+                pltpu.VMEM((6 * depth, depth * PANELS), jnp.bfloat16),
             ],
         ),
-        out_shape=jax.ShapeDtypeStruct((grid, grid), f32),
+        out_shape=jax.ShapeDtypeStruct((grid, cols), f32),
+        cost_estimate=pl.CostEstimate(
+            flops=20 * depth * grid * cols, bytes_accessed=24 * grid * cols, transcendentals=0
+        ),
     )(
-        place, u, low, high, eigen[:, None], eigen[None, :], edge_value[:, None],
-        edge_value[None, :], face_v, side_v, fold, fold,
+        place, low, high, eigen[:, None], eigen[None, :], edge_value[:, None],
+        edge_value[None, :], near, distant, side_v, fold, fold,
     )
 
 
@@ -727,11 +851,14 @@
     edge = grid // PANELS
     groups = [list(range(half)), list(range(half, devices))]
     local = depth <= 32 and rows % 8 == 0
-    block = grid // 8
+    block = grid // 4
+    split = grid // 2
     tables = {
         name: value.astype(np.float32) for name, value in small_tables(depth, grid, edge).items()
     }
     sine_np = sine_table(grid).astype(np.float32)
+    sine_high = sine_np.astype(jnp.bfloat16)
+    sine_low = (sine_np - sine_high.astype(np.float32)).astype(jnp.bfloat16)
     eigen_np = eigen_values(grid)
     fold_np = fold_panels(grid, edge).astype(np.float32)
 
@@ -748,7 +875,7 @@
         upper = (rank // half).astype(jnp.int32).reshape(1)
         is_upper = rank // half == 1
         start = (rank % half) * rows
-        sine = jnp.asarray(sine_np)
+        sine_pair = (jnp.asarray(sine_high), jnp.asarray(sine_low))
         fold = jnp.asarray(fold_np)
         tb = {name: jnp.asarray(value) for name, value in tables.items()}
         eigen = jnp.asarray(eigen_np.astype(np.float32))
@@ -762,7 +889,7 @@
         my_pair = jnp.stack([my_edge * (parity[:rows] == 0), my_edge * (parity[:rows] == 1)])
 
         plane = charge.reshape(grid, grid)
-        spectrum = dot(sine, dot(plane, sine, precision=HIGH), precision=HIGH)
+        spectrum = double_product([plane], *sine_pair)
         spectrum = exchange(spectrum.reshape(half, rows, grid))
         coef, join = factors(mu, half)
         mixed = mixed_table(edge, depth, tb["wave_x"])
@@ -770,7 +897,7 @@
         if local:
             index = (rank % half).astype(jnp.int32)
             place = jnp.where(is_upper, half - index, index + 1).reshape(1)
-            weight = weights(depth, place, eigen[:, None], eigen[None, :], block)
+            weight = weights(depth, place, eigen[:, None], eigen[None, :split], block)
             spectrum, mixed, corner, weight = lax.optimization_barrier(
                 (spectrum, mixed, corner, weight)
             )
@@ -779,10 +906,9 @@
         g, last = sweep(upper, spectrum, coef)
         far = lax.ppermute(last, AXES, [(i, i ^ half) for i in range(devices)])
         if local:
-            u, part = finish_boundary(
+            u, sent, part = finish_boundary(
                 upper, g, coef, join, far, my_edge[:, None], edge_value[None, :], fold, my_fold
             )
-            u = exchange(u).reshape(grid, grid)
         else:
             u, outer = finish(upper, g, coef, join, far)
 
@@ -800,11 +926,30 @@
             part = part + hop(part, bit)
             bit *= 2
         other = hop(part, bit)
+        if local:
+            u, part, other = lax.optimization_barrier((u, part, other))
+            u = exchange(u).reshape(grid, split)
         face_v, side_v = panel_potential(part, other, tb, mixed, corner)
         if local:
-            u = plane_layers(
-                depth, place, u, *weight, eigen, edge_value, face_v, side_v, fold, block
+            back = fold[split:]
+            near, distant = (
+                4.0 * dot(dot(my_fold, face_v[i]), back, NT, precision=HIGH) for i in (0, 1)
             )
+            along = 4.0 * dot(side_v[0], back, NT)
+            across = 4.0 * dot(my_fold, side_v[1], NT)
+            sent = add_ghost(
+                upper, sent, coef, join, my_edge[:, None], edge_value[None, :], along, across,
+                near, distant, split, 1,
+            )
+            sent = exchange(sent).reshape(grid, split)
+            front = fold[:split]
+            rows_v = dot(fold * 4.0, jnp.concatenate([face_v[0], face_v[1]], 1), precision=HIGH)
+            near = dot(rows_v[:, :PANELS], front, NT, precision=HIGH)
+            distant = dot(rows_v[:, PANELS:], front, NT, precision=HIGH)
+            layers = plane_layers(
+                depth, place, *weight, eigen, edge_value, near, distant, side_v, fold, block
+            )
+            return double_product([u, layers, sent], *sine_pair)[None]
         else:
             near, distant = (
                 4.0 * dot(dot(my_fold, face_v[i]), fold, ((1,), (1,))) for i in (0, 1)
@@ -815,7 +960,7 @@
                 upper, u, coef, join, my_edge[:, None], edge_value[None, :], along, across, near, distant
             )
             u = exchange(u).reshape(grid, grid)
-        return dot(dot(sine, u, precision=HIGH), sine, precision=HIGH)[None]
+        return double_product([u], *sine_pair)[None]
 
     return on_device
 

time: 216 us -> 171 us (0.79)
  blocking collectives: 37.7 us -> 13.1 us
  Pallas kernels: 113 us -> 96.8 us
  matrix products: 25.1 us -> 10.9 us
  waiting for transfers between devices: 14.2 us -> 19.6 us
  local copies, waits for them, and re-layouts: 5.85 us -> 8.08 us
    pallas_call x1, Pallas kernels: 45.6 us -> 20.9 us  [plane_layers(): pl.pallas_call(functools.partial(plane_body, depth), grid_spec=pltpu.Pref...]
    all_gather x1, blocking collectives: 37.7 us -> 13.1 us  [on_device(): part = lax.all_gather(part, 'py', axis=0, tiled=False).sum(0)]
    pallas_call x1 -> x4, Pallas kernels: 10.1 us -> 30.6 us  [the longest x2 21.1 us: double_product(): pl.pallas_call(functools.partial(product_body, len(values)), out_shape=ja...]
    dot_general x4 -> x9, matrix products: 25.1 us -> 10.9 us  [dot(): lax.dot_general(a, b, (dims, ((), ())), precision=precision, preferred_el...]
    pallas_call x1, Pallas kernels: 21.8 us -> 9.7 us  [weights(): pl.pallas_call(functools.partial(weight_body, depth), grid_spec=pltpu.Pre...]
    all_to_all x2 -> x3, waiting for transfers between devices: 0.01 us -> 5.32 us  [exchange(): lax.all_to_all(x, AXES, split_axis=0, concat_axis=0, tiled=True, axis_ind...]
    all_to_all x2 -> x3, starting transfers between devices: 11.1 us -> 15.2 us  [exchange(): lax.all_to_all(x, AXES, split_axis=0, concat_axis=0, tiled=True, axis_ind...]
    unnamed x16 -> x22, local copies, waits for them, and re-layouts: 2.98 us -> 5.19 us
  transfers between devices with their start and end apart: 5 -> 6, of which waited for: 3 -> 4; matrix products, arithmetic and copies ran while one was open for 2% -> 9% of each run, Pallas kernels for 26% -> 38%
where the time goes in v2:
time: 171 us; the launch traced here: 170 us
  Pallas kernels  96.8 us (57%)
  starting transfers between devices  20 us (12%)
  waiting for transfers between devices  19.6 us (11%)
  blocking collectives  13.1 us (8%)
  matrix products  10.9 us (6%)
  local copies, waits for them, and re-layouts  8.08 us (5%)
    pallas_call x2, Pallas kernels, double_product(): pl.pallas_call(functools.partial(product_body, len(values)), out_shape=ja...  21.1 us
    pallas_call x1, Pallas kernels, plane_layers(): pl.pallas_call(functools.partial(plane_body, depth), grid_spec=pltpu.Pref...  20.9 us
    all_to_all x3, starting transfers between devices, exchange(): lax.all_to_all(x, AXES, split_axis=0, concat_axis=0, tiled=True, axis_ind...  15.2 us
    pallas_call x1, Pallas kernels, panel_potential(): pl.pallas_call(panels_body, out_shape=[jax.ShapeDtypeStruct((2, PANELS, P...  13.8 us
    all_gather x1, blocking collectives, on_device(): part = lax.all_gather(part, 'py', axis=0, tiled=False).sum(0)  13.1 us
    dot_general x9, matrix products, dot(): lax.dot_general(a, b, (dims, ((), ())), precision=precision, preferred_el...  10.9 us
    ppermute x2, waiting for transfers between devices, hop(): return lax.ppermute(x, 'px', [(i, i ^ bit) for i in range(slow)])  10.1 us
    pallas_call x1, Pallas kernels, weights(): pl.pallas_call(functools.partial(weight_body, depth), grid_spec=pltpu.Pre...  9.7 us
  transfers between devices with their start and end apart: 6, of which 4 were waited for; matrix products, arithmetic and copies ran while one was open for 9% of the time, Pallas kernels for 38%

profile of v2, /device:TPU:0, one launch (start us, length us, event | category | flops | bytes accessed | tf_op | source)
XLA Modules:
  0.0 169.5 jit_solution(9873900428588929891)
XLA Ops:
  0.0 10.4 %shard_map.154 = f32[768,768]{1,0:T(8,128)} custom-call(bf16[768,768]{1,0:T(8,128)(2,1)} %constant.83.clone.high_ref, bf16[768,768]{1,0:T(8,128)(2,1)} %constant.84.clone.low_ref, f32[768,768]{1,0:T(8,128)} %bitcast.34), custom_call_target="tpu_custom_call" | custom-call | tf_op jit(solution)/shard_map/pallas_call | solution.py:101
  10.4 6.4 %all-to-all-start = ((f32[16,48,768]{2,1,0:T(8,128)}), f32[16,48,768]{2,1,0:T(8,128)S(1)}, u32[]{:S(2)}, u32[]{:S(2)}) async-start(f32[16,48,768]{2,1,0:T(8,128)} %bitcast.30), calls=%async_computation | async-start | bytes 4718592 | tf_op jit(solution)/shard_map/all_to_all | solution.py:866
  16.9 0.0 copy-done.10
  16.9 0.1 dynamic_slice.9
  17.0 0.7 broadcast_add_fusion.mu_ref
  17.7 3.0 %shard_map.158 = (f32[16,48,768]{2,1,0:T(8,128)}, f32[48,768]{1,0:T(8,128)}) custom-call(f32[48,768]{1,0:T(8,128)} %broadcast_add_fusion.mu_ref), custom_call_target="tpu_custom_call" | custom-call | flops 11796480 | bytes 2359296 | tf_op jit(solution)/shard_map/pallas_call | solution.py:418
  20.7 9.7 %shard_map.157 = (f32[768,384]{1,0:T(8,128)}, f32[768,384]{1,0:T(8,128)}) custom-call(s32[1]{0:T(128)} %bitcast.3.place_ref, f32[768,1]{1,0:T(8,128)} %constant.99.row_ref.row_eigen_ref, f32[1,384]{1,0:T(1,128)} %constant.101.col_ref), custom_call_target="tpu_custom_call" | custom-call | flops 37748736 | bytes 2359296 | tf_op jit(solution)/shard_map/pallas_call | solution.py:701
  30.4 5.9 %shard_map.155.mixed_ref = f32[2,16,128,256]{3,2,1,0:T(8,128)} custom-call(f32[128,256]{1,0:T(8,128)} %constant.92.clone.wave_ref), custom_call_target="tpu_custom_call" | custom-call | flops 134217728 | bytes 2097152 | tf_op jit(solution)/shard_map/pallas_call | solution.py:152
  36.3 7.6 %shard_map.156 = (f32[64,64,128]{2,1,0:T(8,128)}, f32[64,64,128]{2,1,0:T(8,128)}) custom-call(f32[64,128]{1,0:T(8,128)} %constant.93.clone.wave_ref), custom_call_target="tpu_custom_call" | custom-call | flops 134217728 | bytes 2097152 | tf_op jit(solution)/shard_map/pallas_call | solution.py:202
  43.9 5.3 %all-to-all-done.f_ref = f32[16,48,768]{2,1,0:T(8,128)S(1)} async-done(((f32[16,48,768]{2,1,0:T(8,128)}), f32[16,48,768]{2,1,0:T(8,128)S(1)}, u32[]{:S(2)}, u32[]{:S(2)}) %all-to-all-start) | async-done | bytes 2359328 | tf_op jit(solution)/shard_map/all_to_all | solution.py:866
  49.2 1.4 copy-done
  50.6 4.6 %shard_map.159 = (f32[16,48,768]{2,1,0:T(8,128)}, f32[48,768]{1,0:T(8,128)}) custom-call(s32[1]{0:T(128)} %bitcast.half_ref, f32[16,48,768]{2,1,0:T(8,128)} %copy-done, f32[16,48,768]{2,1,0:T(8,128)} %get-tuple-element.32.coef_ref), custom_call_target="tpu_custom_call" | custom-call | tf_op jit(solution)/shard_map/pallas_call | solution.py:447
  55.2 2.6 %collective-permute-start = (f32[48,768]{1,0:T(8,128)}, f32[48,768]{1,0:T(8,128)S(1)}, u32[]{:S(2)}, u32[]{:S(2)}) collective-permute-start(f32[48,768]{1,0:T(8,128)} %get-tuple-element.35), channel_id=1, source_target_pairs={{0,16},{1,17},{2,18},{3,19},{4,20},{5,21},{6,22},{7,23},{8,24},{9,... | collective-permute-start | bytes 442376 | tf_op jit(solution)/shard_map/ppermute | solution.py:907
  57.8 0.8 dynamic-slice_bitcast_fusion
  58.6 0.7 copy.17.row_ref
  59.3 1.3 constant_dynamic-slice_fusion.mine_ref
  60.6 4.2 %collective-permute-done.far_ref = f32[48,768]{1,0:T(8,128)S(1)} collective-permute-done((f32[48,768]{1,0:T(8,128)}, f32[48,768]{1,0:T(8,128)S(1)}, u32[]{:S(2)}, u32[]{:S(2)}) %collective-permute-start) | collective-permute-done | bytes 147488 | tf_op jit(solution)/shard_map/ppermute | solution.py:907
  64.8 0.7 copy-done.8
  65.5 6.5 %shard_map.160 = (f32[16,48,384]{2,1,0:T(8,128)}, f32[16,48,384]{2,1,0:T(8,128)}, f32[192,128]{1,0:T(8,128)}) custom-call(s32[1]{0:T(128)} %bitcast.half_ref, f32[16,48,768]{2,1,0:T(8,128)} %get-tuple-element.33.g_ref, f32[16,48,768]{2,1,0:T(8,128)} %get-tuple-element.32.coef_ref, f32[48,768]{1,0:T(8,128)} %get-tuple-element.34.join_ref, ...), custom_call_target="tpu_custom_call" | custom-call | tf_op jit(solution)/shard_map/pallas_call | solution.py:611
  72.0 13.1 %all-gather = f32[1536,128]{1,0:T(8,128)S(1)} all-gather(f32[192,128]{1,0:T(8,128)} %get-tuple-element.37), channel_id=2, replica_groups=mesh['px'=4,'py'=8] {'py'}, dimensions={0}, use_global_device_ids=true | all-gather | bytes 884736 | tf_op jit(solution)/shard_map/all_gather | solution.py:923
  85.2 0.4 collective-permute-start.1
  85.5 4.8 %collective-permute-done.1 = f32[192,128]{1,0:T(8,128)S(1)} collective-permute-done((f32[192,128]{1,0:T(8,128)S(1)}, f32[192,128]{1,0:T(8,128)S(1)}, u32[]{:S(2)}, u32[]{:S(2)}) %collective-permute-start.1) | collective-permute-done | bytes 98336 | tf_op jit(solution)/shard_map/ppermute | solution.py:871
  90.3 1.9 %collective-permute-start.2 = (f32[192,128]{1,0:T(8,128)S(1)}, f32[192,128]{1,0:T(8,128)S(1)}, u32[]{:S(2)}, u32[]{:S(2)}) collective-permute-start(f32[192,128]{1,0:T(8,128)S(1)} %add.40.own_ref), channel_id=1, source_target_pairs={{0,16},{8,24},{16,0},{24,8},{1,17},{9,25},{17,1},{25,9},{2,18},{10... | collective-permute-start | bytes 294920 | tf_op jit(solution)/shard_map/ppermute | solution.py:871
  92.2 5.4 %collective-permute-done.2.other_ref = f32[192,128]{1,0:T(8,128)S(1)} collective-permute-done((f32[192,128]{1,0:T(8,128)S(1)}, f32[192,128]{1,0:T(8,128)S(1)}, u32[]{:S(2)}, u32[]{:S(2)}) %collective-permute-start.2) | collective-permute-done | bytes 98336 | tf_op jit(solution)/shard_map/ppermute | solution.py:871
  97.6 0.6 copy-done.9
  98.2 3.9 %all-to-all-start.1 = ((f32[16,48,384]{2,1,0:T(8,128)}), f32[16,48,384]{2,1,0:T(8,128)S(1)}, u32[]{:S(2)}, u32[]{:S(2)}) async-start(f32[16,48,384]{2,1,0:T(8,128)} %get-tuple-element.38), calls=%async_computation.1 | async-start | bytes 2359296 | tf_op jit(solution)/shard_map/all_to_all | solution.py:866
  102.1 0.0 copy-start.3
  102.1 13.8 %shard_map.161 = (f32[2,128,128]{2,1,0:T(8,128)}, f32[2,64,128]{2,1,0:T(8,128)}) custom-call(f32[192,128]{1,0:T(8,128)} %copy-done.6, f32[192,128]{1,0:T(8,128)} %copy-done.9, f32[256,128]{1,0:T(8,128)} %constant.86.clone.basis_ref, f32[2,256,256]{2,1,0:T(8,128)} %constant.87.clone.face_ref, f32[128,256]{1,0:T(8,128)} %constant.88.clone.side_ref, ...), custom_call_target="tpu_custom_call" | custom-call | tf_op jit(solution)/shard_map/pallas_call | solution.py:373
  116.0 1.6 convolution_multiply_fusion.3.across_ref
  117.5 1.0 fusion.14
  118.5 1.0 fusion.12
  119.6 0.9 convolution_multiply_fusion.1.far_ref
  120.5 0.9 convolution_multiply_fusion.2.near_ref
  121.3 1.8 %convolution_multiply_fusion.along_ref = f32[64,384]{1,0:T(8,128)} fusion(f32[384,128]{1,0:T(8,128)S(1)} %copy-done.3, f32[2,64,128]{2,1,0:T(8,128)} %get-tuple-element.47.side_ref), kind=kOutput, calls=%fused_computation | convolution fusion | flops 37773312 | bytes 327680 | tf_op jit(solution)/shard_map/dot_general | solution.py:20
  123.1 3.6 %shard_map.163 = f32[16,48,384]{2,1,0:T(8,128)} custom-call(s32[1]{0:T(128)} %bitcast.half_ref, f32[16,48,384]{2,1,0:T(8,128)} %get-tuple-element.48.u_ref, f32[16,48,768]{2,1,0:T(8,128)} %get-tuple-element.32.coef_ref, f32[48,768]{1,0:T(8,128)} %get-tuple-element.34.join_ref, f32[48,1]{1,0:T(8,128)} %copy.17.row_ref, f32[1,768]{1,0:T(1,128)} %constant.102.col_ref, ...), custom_call_target="tpu_custom_call" | custom-call | tf_op jit(solution)/shard_map/pallas_call | solution.py:525
  126.7 0.0 all-to-all-done.1
  126.8 1.0 copy-done.1
  127.8 4.9 %all-to-all-start.2 = ((f32[16,48,384]{2,1,0:T(8,128)}), f32[16,48,384]{2,1,0:T(8,128)S(1)}, u32[]{:S(2)}, u32[]{:S(2)}) async-start(f32[16,48,384]{2,1,0:T(8,128)} %shard_map.163), calls=%async_computation.2 | async-start | bytes 2359296 | tf_op jit(solution)/shard_map/all_to_all | solution.py:866
  132.7 0.0 copy-start.4
  132.7 0.5 fusion.4
  133.2 0.4 copy-done.4
  133.6 1.7 fusion.distant_ref
  135.3 1.6 fusion.2.near_ref
  136.9 20.9 %shard_map.162.refs_1_ = f32[768,384]{1,0:T(8,128)} custom-call(s32[1]{0:T(128)} %bitcast.3.place_ref, f32[768,384]{1,0:T(8,128)} %get-tuple-element.39.low_ref, f32[768,384]{1,0:T(8,128)} %get-tuple-element.40.high_ref, f32[768,1]{1,0:T(8,128)} %constant.99.row_ref.row_eigen_ref, f32[1,768]{1,0:T(1,128)} %constant.103.col_eigen_ref, ...), custom_call_target="tpu_custom_call" | custom-call | flops 188743680 | bytes 7077888 | tf_op jit(solution)/shard_map/pallas_call | solution.py:811
  157.8 0.0 all-to-all-done.2
  157.8 0.0 copy-start.2
  157.8 1.0 copy-done.2
  158.9 10.7 %shard_map.164 = f32[768,768]{1,0:T(8,128)} custom-call(bf16[768,768]{1,0:T(8,128)(2,1)} %constant.83.clone.high_ref, bf16[768,768]{1,0:T(8,128)(2,1)} %constant.84.clone.low_ref, f32[768,384]{1,0:T(8,128)} %bitcast.31, f32[768,384]{1,0:T(8,128)} %shard_map.162.refs_1_, f32[768,384]{1,0:T(8,128)} %bitcast.32), custom_call_target="tpu_custom_call" | custom-call | tf_op jit(solution)/shard_map/pallas_call | solution.py:101
  (15 shorter events, 0.1 us)
Async XLA Ops:
  10.4 6.5 %copy-start.10 = (f32[768]{0:T(1024)S(1)}, f32[768]{0:T(1024)}, u32[]{:S(2)}) copy-start(f32[768]{0:T(1024)} %constant.94.clone) | copy-start | bytes 9220
  10.4 38.8 %all-to-all-start = ((f32[16,48,768]{2,1,0:T(8,128)}), f32[16,48,768]{2,1,0:T(8,128)S(1)}, u32[]{:S(2)}, u32[]{:S(2)}) async-start(f32[16,48,768]{2,1,0:T(8,128)} %bitcast.30), calls=%async_computation | async-start | bytes 4718592 | tf_op jit(solution)/shard_map/all_to_all | solution.py:866
  49.2 1.4 copy-start
  55.2 9.6 %collective-permute-start = (f32[48,768]{1,0:T(8,128)}, f32[48,768]{1,0:T(8,128)S(1)}, u32[]{:S(2)}, u32[]{:S(2)}) collective-permute-start(f32[48,768]{1,0:T(8,128)} %get-tuple-element.35), channel_id=1, source_target_pairs={{0,16},{1,17},{2,18},{3,19},{4,20},{5,21},{6,22},{7,23},{8,24},{9,... | collective-permute-start | bytes 442376 | tf_op jit(solution)/shard_map/ppermute | solution.py:907
  64.8 0.7 copy-start.8
  85.2 5.1 %collective-permute-start.1 = (f32[192,128]{1,0:T(8,128)S(1)}, f32[192,128]{1,0:T(8,128)S(1)}, u32[]{:S(2)}, u32[]{:S(2)}) collective-permute-start(f32[192,128]{1,0:T(8,128)S(1)} %reduce_sum.9), channel_id=1, source_target_pairs={{0,8},{8,0},{16,24},{24,16},{1,9},{9,1},{17,25},{25,17},{2,10},{10... | collective-permute-start | bytes 294920 | tf_op jit(solution)/shard_map/ppermute | solution.py:871
  90.3 7.3 %copy-start.6 = (f32[192,128]{1,0:T(8,128)}, f32[192,128]{1,0:T(8,128)S(1)}, u32[]{:S(2)}) copy-start(f32[192,128]{1,0:T(8,128)S(1)} %add.40.own_ref) | copy-start | bytes 294916
  90.3 7.3 %collective-permute-start.2 = (f32[192,128]{1,0:T(8,128)S(1)}, f32[192,128]{1,0:T(8,128)S(1)}, u32[]{:S(2)}, u32[]{:S(2)}) collective-permute-start(f32[192,128]{1,0:T(8,128)S(1)} %add.40.own_ref), channel_id=1, source_target_pairs={{0,16},{8,24},{16,0},{24,8},{1,17},{9,25},{17,1},{25,9},{2,18},{10... | collective-permute-start | bytes 294920 | tf_op jit(solution)/shard_map/ppermute | solution.py:871
  97.6 0.7 copy-start.9
  98.2 28.5 %all-to-all-start.1 = ((f32[16,48,384]{2,1,0:T(8,128)}), f32[16,48,384]{2,1,0:T(8,128)S(1)}, u32[]{:S(2)}, u32[]{:S(2)}) async-start(f32[16,48,384]{2,1,0:T(8,128)} %get-tuple-element.38), calls=%async_computation.1 | async-start | bytes 2359296 | tf_op jit(solution)/shard_map/all_to_all | solution.py:866
  102.1 17.5 %copy-start.3 = (f32[384,128]{1,0:T(8,128)S(1)}, f32[384,128]{1,0:T(8,128)}, u32[]{:S(2)}) copy-start(f32[384,128]{1,0:T(8,128)} %constant.107) | copy-start | bytes 589828
  126.7 5.9 %copy-start.5 = (f32[2,128,128]{2,1,0:T(8,128)S(1)}, f32[2,128,128]{2,1,0:T(8,128)}, u32[]{:S(2)}) copy-start(f32[2,128,128]{2,1,0:T(8,128)} %get-tuple-element.46) | copy-start | bytes 393220
  126.7 6.0 %copy-start.7 = (f32[768,128]{1,0:T(8,128)S(1)}, f32[768,128]{1,0:T(8,128)}, u32[]{:S(2)}) copy-start(f32[768,128]{1,0:T(8,128)} %constant.105) | copy-start | bytes 1179652
  126.7 1.0 copy-start.1
  127.8 30.1 %all-to-all-start.2 = ((f32[16,48,384]{2,1,0:T(8,128)}), f32[16,48,384]{2,1,0:T(8,128)S(1)}, u32[]{:S(2)}, u32[]{:S(2)}) async-start(f32[16,48,384]{2,1,0:T(8,128)} %shard_map.163), calls=%async_computation.2 | async-start | bytes 2359296 | tf_op jit(solution)/shard_map/all_to_all | solution.py:866
  132.7 0.9 copy-start.4
  157.8 1.0 copy-start.2

commit v3 on v2

--- a/solution.py
+++ b/solution.py
@@ -459,6 +459,31 @@
     )(upper, spectrum, coef)
 
 
+def reach_body(half_ref, f_ref, coef_ref, last_ref):
+    planes = f_ref.shape[0]
+    upper = half_ref[0]
+    value = jnp.zeros_like(last_ref)
+    for j in range(planes):
+        place = jnp.where(upper == 1, planes - 1 - j, j)
+        value = (f_ref[place] + value) * coef_ref[j]
+    last_ref[...] = value
+
+
+def reach(upper, spectrum, coef):
+    planes, rows, cols = spectrum.shape
+    block, flat = block_specs(planes, rows)
+    return pl.pallas_call(
+        reach_body,
+        grid_spec=pltpu.PrefetchScalarGridSpec(
+            num_scalar_prefetch=1,
+            grid=(cols // WIDTH,),
+            in_specs=[block, block],
+            out_specs=flat,
+        ),
+        out_shape=jax.ShapeDtypeStruct((rows, cols), jnp.float32),
+    )(upper, spectrum, coef)
+
+
 def finish_body(half_ref, g_ref, coef_ref, join_ref, far_ref, u_ref, edge_ref):
     planes = g_ref.shape[0]
     upper = half_ref[0]
@@ -518,10 +543,10 @@
         out_ref[place] = u_ref[place] + value
 
 
-def add_ghost(upper, u, coef, join, row_value, col_value, along, across, near, far, width=WIDTH, first=0):
+def add_ghost(upper, u, coef, join, row_value, col_value, along, across, near, far):
     planes, rows, cols = u.shape
-    block, flat = block_specs(planes, rows, width)
-    far_block, far_flat = block_specs(planes, rows, width, first)
+    width = WIDTH
+    block, flat = block_specs(planes, rows)
     return pl.pallas_call(
         ghost_body,
         grid_spec=pltpu.PrefetchScalarGridSpec(
@@ -529,10 +554,10 @@
             grid=(cols // width,),
             in_specs=[
                 block,
-                far_block,
-                far_flat,
+                block,
+                flat,
                 pl.BlockSpec((rows, 1), lambda i, u: (0, 0)),
-                pl.BlockSpec((1, width), lambda i, u: (0, i + first)),
+                pl.BlockSpec((1, width), lambda i, u: (0, i)),
                 pl.BlockSpec((4 * planes, width), lambda i, u: (0, i)),
                 pl.BlockSpec((rows, 4 * planes), lambda i, u: (0, 0)),
                 flat,
@@ -545,12 +570,62 @@
     )(upper, u, coef, join, row_value, col_value, along, across, near, far)
 
 
+def late_body(
+    half_ref, u_ref, coef_ref, join_ref, row_ref, col_ref, face_ref, side_ref, mine_ref, fold_ref,
+    out_ref, g_ref, along_ref, across_ref, near_ref, far_ref,
+):
+    mine, fold = mine_ref[...], fold_ref[...]
+    along_ref[...] = 4.0 * dot(side_ref[0], fold, NT)
+    across_ref[...] = 4.0 * dot(mine, side_ref[1], NT)
+    near_ref[...] = 4.0 * dot(dot(mine, face_ref[0]), fold, NT)
+    far_ref[...] = 4.0 * dot(dot(mine, face_ref[1]), fold, NT)
+    ghost_body(
+        half_ref, u_ref, coef_ref, join_ref, row_ref, col_ref, along_ref, across_ref, near_ref,
+        far_ref, out_ref, g_ref,
+    )
+
+
+def add_late(upper, u, coef, join, row_value, col_value, face_v, side_v, mine, fold, width):
+    planes, rows, cols = u.shape
+    first = (coef.shape[2] - cols) // width
+    block, _ = block_specs(planes, rows, width)
+    coef_block, join_block = block_specs(planes, rows, width, first)
+    f32 = jnp.float32
+    return pl.pallas_call(
+        late_body,
+        grid_spec=pltpu.PrefetchScalarGridSpec(
+            num_scalar_prefetch=1,
+            grid=(cols // width,),
+            in_specs=[
+                block,
+                coef_block,
+                join_block,
+                pl.BlockSpec((rows, 1), lambda i, u: (0, 0)),
+                pl.BlockSpec((1, width), lambda i, u: (0, i + first)),
+                pl.BlockSpec(face_v.shape, lambda i, u: (0, 0, 0)),
+                pl.BlockSpec(side_v.shape, lambda i, u: (0, 0, 0)),
+                pl.BlockSpec(mine.shape, lambda i, u: (0, 0)),
+                pl.BlockSpec((width, PANELS), lambda i, u: (i + first, 0)),
+            ],
+            out_specs=block,
+            scratch_shapes=[
+                pltpu.VMEM((planes, rows, width), f32),
+                pltpu.VMEM((4 * planes, width), f32),
+                pltpu.VMEM((rows, 4 * planes), f32),
+                pltpu.VMEM((rows, width), f32),
+                pltpu.VMEM((rows, width), f32),
+            ],
+        ),
+        out_shape=jax.ShapeDtypeStruct(u.shape, f32),
+    )(upper, u, coef, join, row_value, col_value, face_v, side_v, mine, fold)
+
+
 def boundary_body(
-    half_ref, g_ref, coef_ref, join_ref, far_ref, row_ref, col_ref, fold_ref, mine_ref,
+    half_ref, f_ref, coef_ref, join_ref, far_ref, row_ref, col_ref, fold_ref, mine_ref,
     pick_row_ref, pick_col_ref, front_ref, back_ref, part_ref, face_ref, rows_ref, cols_ref,
-    stage_ref, u_ref,
+    stage_ref, g_ref,
 ):
-    planes, rows, width = g_ref.shape
+    planes, rows, width = f_ref.shape
     upper = half_ref[0]
     step = pl.program_id(0)
 
@@ -561,10 +636,23 @@
         cols_ref[...] = jnp.zeros_like(cols_ref)
 
     row_value, col_value = row_ref[...], col_ref[...]
-    value = (far_ref[...] + coef_ref[planes - 1] * g_ref[planes - 1]) * join_ref[...]
+    value = jnp.zeros_like(far_ref)
+    for j in range(planes):
+        value = (f_ref[jnp.where(upper == 1, planes - 1 - j, j)] + value) * coef_ref[j]
+        g_ref[j] = value
+    value = (far_ref[...] + coef_ref[planes - 1] * value) * join_ref[...]
     for j in range(planes - 1, -1, -1):
         value = g_ref[j] + coef_ref[j] * value
-        u_ref[jnp.where(upper == 1, planes - 1 - j, j)] = value
+        place = jnp.where(upper == 1, planes - 1 - j, j)
+
+        @pl.when(step == 0)
+        def _(place=place, value=value):
+            front_ref[place] = value
+
+        @pl.when(step != 0)
+        def _(place=place, value=value):
+            back_ref[place] = value
+
         by_row = value * row_value
         total = by_row[:8]
         for k in range(8, rows, 8):
@@ -575,12 +663,6 @@
         for k in range(PANELS, width, PANELS):
             total = total + by_col[:, k : k + PANELS]
         cols_ref[:, j * PANELS : (j + 1) * PANELS] += total
-    for target, turn in ((front_ref, 0), (back_ref, 1)):
-
-        @pl.when(step == turn)
-        def _(target=target):
-            target[...] = u_ref[...]
-
     fold = fold_ref[...]
     face_ref[...] += dot(value, fold)
     rows_ref[...] += dot(stage_ref[...], fold)
@@ -595,11 +677,12 @@
         )
 
 
-def finish_boundary(upper, g, coef, join, far, row_value, col_value, fold, mine):
-    planes, rows, cols = g.shape
-    width = cols // 2
+def finish_boundary(upper, f, coef, join, far, row_value, col_value, fold, mine):
+    planes, rows, cols = f.shape
+    width = cols // 3
     block, flat = block_specs(planes, rows, width)
-    still = pl.BlockSpec((planes, rows, width), lambda i, u: (0, 0, 0))
+    front = pl.BlockSpec((planes, rows, width), lambda i, u: (0, 0, 0))
+    back = pl.BlockSpec((planes, rows, width), lambda i, u: (0, 0, jnp.maximum(i - 1, 0)))
     pick_row = np.zeros((2, planes, planes, 8), np.float32)
     pick_col = np.zeros((planes, PANELS, 2, planes), np.float32)
     for j in range(planes):
@@ -612,7 +695,7 @@
         boundary_body,
         grid_spec=pltpu.PrefetchScalarGridSpec(
             num_scalar_prefetch=1,
-            grid=(2,),
+            grid=(3,),
             in_specs=[
                 block,
                 block,
@@ -625,7 +708,7 @@
                 whole((2 * planes, 8 * planes)),
                 whole((planes * PANELS, 2 * planes)),
             ],
-            out_specs=[still, still, whole((PANELS + 4 * planes, PANELS))],
+            out_specs=[front, back, whole((PANELS + 4 * planes, PANELS))],
             scratch_shapes=[
                 pltpu.VMEM((rows, PANELS), f32),
                 pltpu.VMEM((8 * planes, PANELS), f32),
@@ -636,11 +719,11 @@
         ),
         out_shape=[
             jax.ShapeDtypeStruct((planes, rows, width), f32),
-            jax.ShapeDtypeStruct((planes, rows, width), f32),
+            jax.ShapeDtypeStruct((planes, rows, 2 * width), f32),
             jax.ShapeDtypeStruct((PANELS + 4 * planes, PANELS), f32),
         ],
     )(
-        upper, g, coef, join, far, row_value, col_value, fold, mine,
+        upper, f, coef, join, far, row_value, col_value, fold, mine,
         pick_row.reshape(2 * planes, -1), pick_col.reshape(-1, 2 * planes),
     )
 
@@ -648,8 +731,8 @@
 TINY = 2.0**-60
 GROUP = 32
 UNROLL = 4
-TALL = 24
-LANES = 384
+TALL = 32
+LANES = 256
 
 
 def whole_steps(count):
@@ -852,7 +935,7 @@
     groups = [list(range(half)), list(range(half, devices))]
     local = depth <= 32 and rows % 8 == 0
     block = grid // 4
-    split = grid // 2
+    split = grid // 3
     tables = {
         name: value.astype(np.float32) for name, value in small_tables(depth, grid, edge).items()
     }
@@ -903,11 +986,15 @@
             )
         else:
             spectrum, mixed, corner = lax.optimization_barrier((spectrum, mixed, corner))
-        g, last = sweep(upper, spectrum, coef)
+        if local:
+            last = reach(upper, spectrum, coef)
+        else:
+            g, last = sweep(upper, spectrum, coef)
         far = lax.ppermute(last, AXES, [(i, i ^ half) for i in range(devices)])
         if local:
             u, sent, part = finish_boundary(
-                upper, g, coef, join, far, my_edge[:, None], edge_value[None, :], fold, my_fold
+                upper, spectrum, coef, join, far, my_edge[:, None], edge_value[None, :], fold,
+                my_fold,
             )
         else:
             u, outer = finish(upper, g, coef, join, far)
@@ -931,17 +1018,11 @@
             u = exchange(u).reshape(grid, split)
         face_v, side_v = panel_potential(part, other, tb, mixed, corner)
         if local:
-            back = fold[split:]
-            near, distant = (
-                4.0 * dot(dot(my_fold, face_v[i]), back, NT, precision=HIGH) for i in (0, 1)
+            sent = add_late(
+                upper, sent, coef, join, my_edge[:, None], edge_value[None, :], face_v, side_v,
+                my_fold, fold, split,
             )
-            along = 4.0 * dot(side_v[0], back, NT)
-            across = 4.0 * dot(my_fold, side_v[1], NT)
-            sent = add_ghost(
-                upper, sent, coef, join, my_edge[:, None], edge_value[None, :], along, across,
-                near, distant, split, 1,
-            )
-            sent = exchange(sent).reshape(grid, split)
+            sent = exchange(sent).reshape(grid, grid - split)
             front = fold[:split]
             rows_v = dot(fold * 4.0, jnp.concatenate([face_v[0], face_v[1]], 1), precision=HIGH)
             near = dot(rows_v[:, :PANELS], front, NT, precision=HIGH)

time: 171 us -> 161 us (0.942)
  matrix products: 10.9 us -> 3.22 us
  Pallas kernels: 96.8 us -> 90.3 us
  waiting for transfers between devices: 19.6 us -> 25.6 us
  local copies, waits for them, and re-layouts: 8.08 us -> 6.13 us
    dot_general x9 -> x3, matrix products: 10.9 us -> 3.22 us  [dot(): lax.dot_general(a, b, (dims, ((), ())), precision=precision, preferred_el...]
    all_to_all x3, waiting for transfers between devices: 5.32 us -> 11.3 us  [exchange(): lax.all_to_all(x, AXES, split_axis=0, concat_axis=0, tiled=True, axis_ind...]
    pallas_call x1, Pallas kernels: 20.9 us -> 15.8 us  [plane_layers(): pl.pallas_call(functools.partial(plane_body, depth), grid_spec=pltpu.Pref...]
    pallas_call x1, Pallas kernels: 9.7 us -> 7.15 us  [weights(): pl.pallas_call(functools.partial(weight_body, depth), grid_spec=pltpu.Pre...]
    unnamed x22 -> x20, local copies, waits for them, and re-layouts: 5.19 us -> 3.26 us
  transfers between devices with their start and end apart: 6 -> 6, of which waited for: 4 -> 5; matrix products, arithmetic and copies ran while one was open for 9% -> 4% of each run, Pallas kernels for 38% -> 37%
where the time goes in v3:
time: 161 us; the launch traced here: 160 us
  Pallas kernels  90.3 us (56%)
  waiting for transfers between devices  25.6 us (16%)
  starting transfers between devices  20.3 us (13%)
  blocking collectives  13.1 us (8%)
  local copies, waits for them, and re-layouts  6.13 us (4%)
  matrix products  3.22 us (2%)
    pallas_call x2, Pallas kernels, double_product(): pl.pallas_call(functools.partial(product_body, len(values)), out_shape=ja...  21 us
    pallas_call x1, Pallas kernels, plane_layers(): pl.pallas_call(functools.partial(plane_body, depth), grid_spec=pltpu.Pref...  15.8 us
    all_to_all x3, starting transfers between devices, exchange(): lax.all_to_all(x, AXES, split_axis=0, concat_axis=0, tiled=True, axis_ind...  15.4 us
    pallas_call x1, Pallas kernels, panel_potential(): pl.pallas_call(panels_body, out_shape=[jax.ShapeDtypeStruct((2, PANELS, P...  13.8 us
    all_gather x1, blocking collectives, on_device(): part = lax.all_gather(part, 'py', axis=0, tiled=False).sum(0)  13.1 us
    all_to_all x3, waiting for transfers between devices, exchange(): lax.all_to_all(x, AXES, split_axis=0, concat_axis=0, tiled=True, axis_ind...  11.3 us
    ppermute x2, waiting for transfers between devices, hop(): return lax.ppermute(x, 'px', [(i, i ^ bit) for i in range(slow)])  10.1 us
    pallas_call x1, Pallas kernels, corner_table(): pl.pallas_call(functools.partial(corner_body, edge, depth), grid=(hb // S...  7.62 us
  transfers between devices with their start and end apart: 6, of which 5 were waited for; matrix products, arithmetic and copies ran while one was open for 4% of the time, Pallas kernels for 37%

profile of v3, /device:TPU:0, one launch (start us, length us, event | category | flops | bytes accessed | tf_op | source)
XLA Modules:
  0.0 159.7 jit_solution(3913498401683529768)
XLA Ops:
  0.0 10.4 %shard_map.154 = f32[768,768]{1,0:T(8,128)} custom-call(bf16[768,768]{1,0:T(8,128)(2,1)} %constant.80.clone.high_ref, bf16[768,768]{1,0:T(8,128)(2,1)} %constant.81.clone.low_ref, f32[768,768]{1,0:T(8,128)} %bitcast.21), custom_call_target="tpu_custom_call" | custom-call | tf_op jit(solution)/shard_map/pallas_call | solution.py:101
  10.4 0.0 copy-start.9
  10.4 6.4 %all-to-all-start = ((f32[16,48,768]{2,1,0:T(8,128)}), f32[16,48,768]{2,1,0:T(8,128)S(1)}, u32[]{:S(2)}, u32[]{:S(2)}) async-start(f32[16,48,768]{2,1,0:T(8,128)} %bitcast.17), calls=%async_computation | async-start | bytes 4718592 | tf_op jit(solution)/shard_map/all_to_all | solution.py:949
  16.9 0.0 copy-done.9
  16.9 0.1 dynamic_slice.9
  17.0 0.7 broadcast_add_fusion.mu_ref
  17.7 2.9 %shard_map.158 = (f32[16,48,768]{2,1,0:T(8,128)}, f32[48,768]{1,0:T(8,128)}) custom-call(f32[48,768]{1,0:T(8,128)} %broadcast_add_fusion.mu_ref), custom_call_target="tpu_custom_call" | custom-call | flops 11796480 | bytes 2359296 | tf_op jit(solution)/shard_map/pallas_call | solution.py:418
  20.6 7.2 %shard_map.157 = (f32[768,256]{1,0:T(8,128)}, f32[768,256]{1,0:T(8,128)}) custom-call(s32[1]{0:T(128)} %bitcast.3.place_ref, f32[768,1]{1,0:T(8,128)} %constant.96.row_ref.row_eigen_ref, f32[1,256]{1,0:T(1,128)} %constant.98.col_ref), custom_call_target="tpu_custom_call" | custom-call | flops 25165824 | bytes 1572864 | tf_op jit(solution)/shard_map/pallas_call | solution.py:784
  27.8 5.9 %shard_map.155.mixed_ref = f32[2,16,128,256]{3,2,1,0:T(8,128)} custom-call(f32[128,256]{1,0:T(8,128)} %constant.89.clone.wave_ref), custom_call_target="tpu_custom_call" | custom-call | flops 134217728 | bytes 2097152 | tf_op jit(solution)/shard_map/pallas_call | solution.py:152
  33.7 7.6 %shard_map.156 = (f32[64,64,128]{2,1,0:T(8,128)}, f32[64,64,128]{2,1,0:T(8,128)}) custom-call(f32[64,128]{1,0:T(8,128)} %constant.90.clone.wave_ref), custom_call_target="tpu_custom_call" | custom-call | flops 134217728 | bytes 2097152 | tf_op jit(solution)/shard_map/pallas_call | solution.py:202
  41.3 7.9 %all-to-all-done.f_ref = f32[16,48,768]{2,1,0:T(8,128)S(1)} async-done(((f32[16,48,768]{2,1,0:T(8,128)}), f32[16,48,768]{2,1,0:T(8,128)S(1)}, u32[]{:S(2)}, u32[]{:S(2)}) %all-to-all-start) | async-done | bytes 2359328 | tf_op jit(solution)/shard_map/all_to_all | solution.py:949
  49.2 0.0 copy-start
  49.2 1.4 copy-done
  50.6 3.7 %shard_map.159 = f32[48,768]{1,0:T(8,128)} custom-call(s32[1]{0:T(128)} %bitcast.half_ref, f32[16,48,768]{2,1,0:T(8,128)} %copy-done, f32[16,48,768]{2,1,0:T(8,128)} %get-tuple-element.30.coef_ref), custom_call_target="tpu_custom_call" | custom-call | tf_op jit(solution)/shard_map/pallas_call | solution.py:475
  54.3 2.6 %collective-permute-start = (f32[48,768]{1,0:T(8,128)}, f32[48,768]{1,0:T(8,128)S(1)}, u32[]{:S(2)}, u32[]{:S(2)}) collective-permute-start(f32[48,768]{1,0:T(8,128)} %shard_map.159), channel_id=1, source_target_pairs={{0,16},{1,17},{2,18},{3,19},{4,20},{5,21},{6,22},{7,23},{8,24},{9,... | collective-permute-start | bytes 442376 | tf_op jit(solution)/shard_map/ppermute | solution.py:993
  56.9 0.8 dynamic-slice_bitcast_fusion
  57.7 0.7 copy.17.row_ref
  58.4 1.3 constant_dynamic-slice_fusion.mine_ref
  59.7 4.2 %collective-permute-done.far_ref = f32[48,768]{1,0:T(8,128)S(1)} collective-permute-done((f32[48,768]{1,0:T(8,128)}, f32[48,768]{1,0:T(8,128)S(1)}, u32[]{:S(2)}, u32[]{:S(2)}) %collective-permute-start) | collective-permute-done | bytes 147488 | tf_op jit(solution)/shard_map/ppermute | solution.py:993
  63.9 0.0 copy-start.7
  63.9 0.7 copy-done.7
  64.5 7.2 %shard_map.160 = (f32[16,48,256]{2,1,0:T(8,128)}, f32[16,48,512]{2,1,0:T(8,128)}, f32[192,128]{1,0:T(8,128)}) custom-call(s32[1]{0:T(128)} %bitcast.half_ref, f32[16,48,768]{2,1,0:T(8,128)} %copy-done, f32[16,48,768]{2,1,0:T(8,128)} %get-tuple-element.30.coef_ref, f32[48,768]{1,0:T(8,128)} %get-tuple-element.31.join_ref, f32[48,768]{1,0:T(8,128)} %copy-done.7, ...), custom_call_target="tpu_custom_call" | custom-call | tf_op jit(solution)/shard_map/pallas_call | solution.py:694
  71.8 13.1 %all-gather = f32[1536,128]{1,0:T(8,128)S(1)} all-gather(f32[192,128]{1,0:T(8,128)} %get-tuple-element.33), channel_id=2, replica_groups=mesh['px'=4,'py'=8] {'py'}, dimensions={0}, use_global_device_ids=true | all-gather | bytes 884736 | tf_op jit(solution)/shard_map/all_gather | solution.py:1010
  85.0 0.4 collective-permute-start.1
  85.3 4.8 %collective-permute-done.1 = f32[192,128]{1,0:T(8,128)S(1)} collective-permute-done((f32[192,128]{1,0:T(8,128)S(1)}, f32[192,128]{1,0:T(8,128)S(1)}, u32[]{:S(2)}, u32[]{:S(2)}) %collective-permute-start.1) | collective-permute-done | bytes 98336 | tf_op jit(solution)/shard_map/ppermute | solution.py:954
  90.1 0.0 copy-start.5
  90.1 1.9 %collective-permute-start.2 = (f32[192,128]{1,0:T(8,128)S(1)}, f32[192,128]{1,0:T(8,128)S(1)}, u32[]{:S(2)}, u32[]{:S(2)}) collective-permute-start(f32[192,128]{1,0:T(8,128)S(1)} %add.40.own_ref), channel_id=1, source_target_pairs={{0,16},{8,24},{16,0},{24,8},{1,17},{9,25},{17,1},{25,9},{2,18},{10... | collective-permute-start | bytes 294920 | tf_op jit(solution)/shard_map/ppermute | solution.py:954
  92.0 5.4 %collective-permute-done.2.other_ref = f32[192,128]{1,0:T(8,128)S(1)} collective-permute-done((f32[192,128]{1,0:T(8,128)S(1)}, f32[192,128]{1,0:T(8,128)S(1)}, u32[]{:S(2)}, u32[]{:S(2)}) %collective-permute-start.2) | collective-permute-done | bytes 98336 | tf_op jit(solution)/shard_map/ppermute | solution.py:954
  97.4 3.6 %all-to-all-start.1 = ((f32[16,48,256]{2,1,0:T(8,128)}), f32[16,48,256]{2,1,0:T(8,128)S(1)}, u32[]{:S(2)}, u32[]{:S(2)}) async-start(f32[16,48,256]{2,1,0:T(8,128)} %get-tuple-element.34), calls=%async_computation.1 | async-start | bytes 1572864 | tf_op jit(solution)/shard_map/all_to_all | solution.py:949
  101.0 0.0 copy-done.5
  101.0 0.0 copy-done.8
  101.0 13.8 %shard_map.161 = (f32[2,128,128]{2,1,0:T(8,128)}, f32[2,64,128]{2,1,0:T(8,128)}) custom-call(f32[192,128]{1,0:T(8,128)} %copy-done.5, f32[192,128]{1,0:T(8,128)} %copy-done.8, f32[256,128]{1,0:T(8,128)} %constant.83.clone.basis_ref, f32[2,256,256]{2,1,0:T(8,128)} %constant.84.clone.face_ref, f32[128,256]{1,0:T(8,128)} %constant.85.clone.side_ref, ...), custom_call_target="tpu_custom_call" | custom-call | tf_op jit(solution)/shard_map/pallas_call | solution.py:373
  114.8 5.2 %shard_map.163 = f32[16,48,512]{2,1,0:T(8,128)} custom-call(s32[1]{0:T(128)} %bitcast.half_ref, f32[16,48,512]{2,1,0:T(8,128)} %get-tuple-element.44.u_ref, f32[16,48,768]{2,1,0:T(8,128)} %get-tuple-element.30.coef_ref, f32[48,768]{1,0:T(8,128)} %get-tuple-element.31.join_ref, f32[48,1]{1,0:T(8,128)} %copy.17.row_ref, f32[1,768]{1,0:T(1,128)} %constant.99.col_ref, ...), custom_call_target="tpu_custom_call" | custom-call | tf_op jit(solution)/shard_map/pallas_call | solution.py:594
  120.0 0.0 copy-start.3
  120.0 0.0 all-to-all-done.1
  120.0 0.0 copy-start.2
  120.0 5.4 %all-to-all-start.2 = ((f32[16,48,512]{2,1,0:T(8,128)}), f32[16,48,512]{2,1,0:T(8,128)S(1)}, u32[]{:S(2)}, u32[]{:S(2)}) async-start(f32[16,48,512]{2,1,0:T(8,128)} %shard_map.163), calls=%async_computation.2 | async-start | bytes 3145728 | tf_op jit(solution)/shard_map/all_to_all | solution.py:949
  125.4 0.0 copy-done.4
  125.5 0.0 copy-done.6
  125.5 0.5 fusion.4
  125.9 0.0 copy-done.2
  125.9 0.0 copy-done.3
  125.9 1.4 fusion.distant_ref
  127.3 1.4 fusion.2.near_ref
  128.7 15.8 %shard_map.162.refs_1_ = f32[768,256]{1,0:T(8,128)} custom-call(s32[1]{0:T(128)} %bitcast.3.place_ref, f32[768,256]{1,0:T(8,128)} %get-tuple-element.35.low_ref, f32[768,256]{1,0:T(8,128)} %get-tuple-element.36.high_ref, f32[768,1]{1,0:T(8,128)} %constant.96.row_ref.row_eigen_ref, f32[1,768]{1,0:T(1,128)} %constant.100.col_eigen_ref, ...), custom_call_target="tpu_custom_call" | custom-call | flops 125829120 | bytes 4718592 | tf_op jit(solution)/shard_map/pallas_call | solution.py:894
  144.5 3.4 %all-to-all-done.2 = f32[16,48,512]{2,1,0:T(8,128)S(1)} async-done(((f32[16,48,512]{2,1,0:T(8,128)}), f32[16,48,512]{2,1,0:T(8,128)S(1)}, u32[]{:S(2)}, u32[]{:S(2)}) %all-to-all-start.2) | async-done | bytes 1572896 | tf_op jit(solution)/shard_map/all_to_all | solution.py:949
  147.9 1.2 copy-done.1
  149.1 10.6 %shard_map.164 = f32[768,768]{1,0:T(8,128)} custom-call(bf16[768,768]{1,0:T(8,128)(2,1)} %constant.80.clone.high_ref, bf16[768,768]{1,0:T(8,128)(2,1)} %constant.81.clone.low_ref, f32[768,256]{1,0:T(8,128)} %bitcast.20, f32[768,256]{1,0:T(8,128)} %shard_map.162.refs_1_, f32[768,512]{1,0:T(8,128)} %bitcast.18), custom_call_target="tpu_custom_call" | custom-call | tf_op jit(solution)/shard_map/pallas_call | solution.py:101
  (7 shorter events, 0.1 us)
Async XLA Ops:
  10.4 6.5 %copy-start.9 = (f32[768]{0:T(1024)S(1)}, f32[768]{0:T(1024)}, u32[]{:S(2)}) copy-start(f32[768]{0:T(1024)} %constant.91.clone) | copy-start | bytes 9220
  10.4 38.8 %all-to-all-start = ((f32[16,48,768]{2,1,0:T(8,128)}), f32[16,48,768]{2,1,0:T(8,128)S(1)}, u32[]{:S(2)}, u32[]{:S(2)}) async-start(f32[16,48,768]{2,1,0:T(8,128)} %bitcast.17), calls=%async_computation | async-start | bytes 4718592 | tf_op jit(solution)/shard_map/all_to_all | solution.py:949
  49.2 1.4 copy-start
  54.3 9.6 %collective-permute-start = (f32[48,768]{1,0:T(8,128)}, f32[48,768]{1,0:T(8,128)S(1)}, u32[]{:S(2)}, u32[]{:S(2)}) collective-permute-start(f32[48,768]{1,0:T(8,128)} %shard_map.159), channel_id=1, source_target_pairs={{0,16},{1,17},{2,18},{3,19},{4,20},{5,21},{6,22},{7,23},{8,24},{9,... | collective-permute-start | bytes 442376 | tf_op jit(solution)/shard_map/ppermute | solution.py:993
  63.9 0.7 copy-start.7
  85.0 5.1 %collective-permute-start.1 = (f32[192,128]{1,0:T(8,128)S(1)}, f32[192,128]{1,0:T(8,128)S(1)}, u32[]{:S(2)}, u32[]{:S(2)}) collective-permute-start(f32[192,128]{1,0:T(8,128)S(1)} %reduce_sum.9), channel_id=1, source_target_pairs={{0,8},{8,0},{16,24},{24,16},{1,9},{9,1},{17,25},{25,17},{2,10},{10... | collective-permute-start | bytes 294920 | tf_op jit(solution)/shard_map/ppermute | solution.py:954
  90.1 10.9 %copy-start.5 = (f32[192,128]{1,0:T(8,128)}, f32[192,128]{1,0:T(8,128)S(1)}, u32[]{:S(2)}) copy-start(f32[192,128]{1,0:T(8,128)S(1)} %add.40.own_ref) | copy-start | bytes 294916
  90.1 7.3 %collective-permute-start.2 = (f32[192,128]{1,0:T(8,128)S(1)}, f32[192,128]{1,0:T(8,128)S(1)}, u32[]{:S(2)}, u32[]{:S(2)}) collective-permute-start(f32[192,128]{1,0:T(8,128)S(1)} %add.40.own_ref), channel_id=1, source_target_pairs={{0,16},{8,24},{16,0},{24,8},{1,17},{9,25},{17,1},{25,9},{2,18},{10... | collective-permute-start | bytes 294920 | tf_op jit(solution)/shard_map/ppermute | solution.py:954
  97.4 3.6 %copy-start.8 = (f32[192,128]{1,0:T(8,128)}, f32[192,128]{1,0:T(8,128)S(1)}, u32[]{:S(2)}) copy-start(f32[192,128]{1,0:T(8,128)S(1)} %collective-permute-done.2.other_ref) | copy-start | bytes 294916
  97.4 22.6 %all-to-all-start.1 = ((f32[16,48,256]{2,1,0:T(8,128)}), f32[16,48,256]{2,1,0:T(8,128)S(1)}, u32[]{:S(2)}, u32[]{:S(2)}) async-start(f32[16,48,256]{2,1,0:T(8,128)} %get-tuple-element.34), calls=%async_computation.1 | async-start | bytes 1572864 | tf_op jit(solution)/shard_map/all_to_all | solution.py:949
  120.0 5.4 %copy-start.4 = (f32[2,128,128]{2,1,0:T(8,128)S(1)}, f32[2,128,128]{2,1,0:T(8,128)}, u32[]{:S(2)}) copy-start(f32[2,128,128]{2,1,0:T(8,128)} %get-tuple-element.42.face_ref) | copy-start | bytes 393220
  120.0 5.5 %copy-start.6 = (f32[768,128]{1,0:T(8,128)S(1)}, f32[768,128]{1,0:T(8,128)}, u32[]{:S(2)}) copy-start(f32[768,128]{1,0:T(8,128)} %constant.102) | copy-start | bytes 1179652
  120.0 5.9 %copy-start.3 = (f32[256,128]{1,0:T(8,128)S(1)}, f32[256,128]{1,0:T(8,128)}, u32[]{:S(2)}) copy-start(f32[256,128]{1,0:T(8,128)} %constant.103) | copy-start | bytes 393220
  120.0 5.9 %copy-start.2 = (f32[16,48,256]{2,1,0:T(8,128)}, f32[16,48,256]{2,1,0:T(8,128)S(1)}, u32[]{:S(2)}) copy-start(f32[16,48,256]{2,1,0:T(8,128)S(1)} %all-to-all-done.1) | copy-start | bytes 2359300
  120.0 27.9 %all-to-all-start.2 = ((f32[16,48,512]{2,1,0:T(8,128)}), f32[16,48,512]{2,1,0:T(8,128)S(1)}, u32[]{:S(2)}, u32[]{:S(2)}) async-start(f32[16,48,512]{2,1,0:T(8,128)} %shard_map.163), calls=%async_computation.2 | async-start | bytes 3145728 | tf_op jit(solution)/shard_map/all_to_all | solution.py:949
  147.9 1.2 copy-start.1

commit v4 on v3

--- a/solution.py
+++ b/solution.py
@@ -58,8 +58,15 @@
     return high, (value - high.astype(jnp.float32)).astype(jnp.bfloat16)
 
 
-def bf16_dot(a, b):
-    return lax.dot_general(a, b, (((1,), (0,)), ((), ())), preferred_element_type=jnp.float32)
+def bf16_dot(a, b, dims=((1,), (0,))):
+    return lax.dot_general(a, b, (dims, ((), ())), preferred_element_type=jnp.float32)
+
+
+def dot3(a, b, dims=((1,), (0,))):
+    a_high, a_low = halves(a)
+    b_high, b_low = halves(b)
+    value = bf16_dot(a_high, b_high, dims)
+    return value + (bf16_dot(a_high, b_low, dims) + bf16_dot(a_low, b_high, dims))
 
 
 STRIPE = 256
@@ -67,13 +74,15 @@
 
 def product_body(count, high_ref, low_ref, *refs):
     in_refs, out_ref, mid_high_ref, mid_low_ref = refs[:count], *refs[count:]
-    grid = out_ref.shape[0]
-
-    def first(index, _):
-        at = pl.ds(pl.multiple_of(index * STRIPE, STRIPE), STRIPE)
-        value = in_refs[0][at, :]
+    step = pl.program_id(0)
+    stripes = pl.num_programs(0) // 2
+
+    @pl.when(step < stripes)
+    def _():
+        at = pl.ds(pl.multiple_of(step * STRIPE, STRIPE), STRIPE)
+        value = in_refs[0][...]
         if count == 3:
-            value = jnp.concatenate([value + in_refs[1][at, :], in_refs[2][at, :]], 1)
+            value = jnp.concatenate([value + in_refs[1][...].T, in_refs[2][...]], 1)
         high, low = halves(value)
         value = bf16_dot(high, high_ref[...])
         value = value + bf16_dot(high, low_ref[...])
@@ -81,25 +90,31 @@
         high, low = halves(value)
         mid_high_ref[at, :] = high
         mid_low_ref[at, :] = low
-        return 0
-
-    lax.fori_loop(0, grid // STRIPE, first, 0)
-
-    def second(index, _):
-        at = pl.ds(pl.multiple_of(index * STRIPE, STRIPE), STRIPE)
+
+    @pl.when(step >= stripes)
+    def _():
+        at = pl.ds(pl.multiple_of((step - stripes) * STRIPE, STRIPE), STRIPE)
         value = bf16_dot(high_ref[at, :], mid_high_ref[...])
         value = value + bf16_dot(high_ref[at, :], mid_low_ref[...])
         value = value + bf16_dot(low_ref[at, :], mid_high_ref[...])
-        out_ref[at, :] = value
-        return 0
-
-    lax.fori_loop(0, grid // STRIPE, second, 0)
+        out_ref[...] = value
 
 
 def double_product(values, high, low):
     grid = high.shape[0]
+    stripes = grid // STRIPE
+    table = pl.BlockSpec((grid, grid), lambda i: (0, 0), pipeline_mode=pl.Buffered(1))
     return pl.pallas_call(
         functools.partial(product_body, len(values)),
+        grid=(2 * stripes,),
+        in_specs=[table, table]
+        + [
+            pl.BlockSpec((v.shape[0], STRIPE), lambda i: (0, jnp.minimum(i, stripes - 1)))
+            if k == 1
+            else pl.BlockSpec((STRIPE, v.shape[1]), lambda i: (jnp.minimum(i, stripes - 1), 0))
+            for k, v in enumerate(values)
+        ],
+        out_specs=pl.BlockSpec((STRIPE, grid), lambda i: (jnp.maximum(i - stripes, 0), 0)),
         out_shape=jax.ShapeDtypeStruct((grid, grid), jnp.float32),
         scratch_shapes=[
             pltpu.VMEM((grid, grid), jnp.bfloat16),
@@ -283,10 +298,10 @@
     for axis in (0, 1):
         rows = slice(PANELS + axis * 2 * half, PANELS + (axis + 1) * 2 * half)
         sides.append(jnp.concatenate([total[rows], gap[rows]], 0))
-        hat_ref[axis] = dot(sides[axis], basis, NT)
+        hat_ref[axis] = dot3(sides[axis], basis, NT)
     for s in (0, 1):
-        fx_ref[0, s] = dot(faces[s], basis, NT)
-        fx_ref[1, s] = dot(faces[s], basis, ((0,), (1,)))
+        fx_ref[0, s] = dot3(faces[s], basis, NT)
+        fx_ref[1, s] = dot3(faces[s], basis, ((0,), (1,)))
 
     for s in (0, 1):
 
@@ -329,8 +344,8 @@
 
         lax.fori_loop(0, half, side_rows, 0)
 
-    xs_ref[...] = dot(sides[1], cross_ref[...], TN)
-    ys = dot(sides[0][:, :hb], turn_ref[0], TN) + dot(sides[0][:, hb:], turn_ref[1], TN)
+    xs_ref[...] = dot3(sides[1], cross_ref[...], TN)
+    ys = dot3(sides[0][:, :hb], turn_ref[0], TN) + dot3(sides[0][:, hb:], turn_ref[1], TN)
     width = xs_ref.shape[1]
     to_y = []
     for t, table_ref in ((0, front_ref), (1, back_ref)):
@@ -345,13 +360,13 @@
         to_y.append(lax.fori_loop(0, hb, corner_rows, jnp.zeros((hb, width), jnp.float32)))
     to_y = jnp.concatenate(to_y, 1)
     corner = [
-        jnp.concatenate([dot(turn_ref[x], to_y, NT) for x in (0, 1)], 1),
-        dot(cross_ref[...], tox_ref[...], NT),
+        jnp.concatenate([dot3(turn_ref[x], to_y, NT) for x in (0, 1)], 1),
+        dot3(cross_ref[...], tox_ref[...], NT),
     ]
     for axis in (0, 1):
-        waves = dot(level, hat_ref[axis], TN) * side_ref[...]
-        waves = dot(level, waves) + toside_ref[axis]
-        value = dot(waves, basis) + corner[axis]
+        waves = dot3(level, hat_ref[axis], TN) * side_ref[...]
+        waves = dot3(level, waves) + toside_ref[axis]
+        value = dot3(waves, basis) + corner[axis]
         even, odd = value[: 2 * half], value[2 * half :]
         for part, v in ((0, even + odd), (1, even - odd)):
             for t in (0, 1):
@@ -359,9 +374,9 @@
                 side_out_ref[axis, at : at + half, :] = v[t * half : (t + 1) * half]
     value = []
     for s in (0, 1):
-        full = dot(basis, fx_ref[0, s]) * face_ref[s]
-        rows = dot(basis, full, TN) + acc_ref[0, s]
-        value.append(dot(rows, basis) + dot(basis, acc_ref[1, s], ((0,), (1,))))
+        full = dot3(basis, fx_ref[0, s]) * face_ref[s]
+        rows = dot3(basis, full, TN) + acc_ref[0, s]
+        value.append(dot3(rows, basis) + dot3(basis, acc_ref[1, s], ((0,), (1,))))
     face_out_ref[0] = value[0] + value[1]
     face_out_ref[1] = value[0] - value[1]
 
@@ -384,6 +399,10 @@
             pltpu.VMEM((PANELS, width), f32),
             pltpu.VMEM((PANELS, width), f32),
         ],
+        cost_estimate=pl.CostEstimate(
+            flops=5_000_000_000, bytes_accessed=4 * (mixed.size + 2 * corner[0].size),
+            transcendentals=0,
+        ),
     )(
         own, other, tb["basis"], tb["face"], tb["side"], tb["level"], tb["cross"], tb["turn"],
         mixed, *corner,
@@ -575,10 +594,10 @@
     out_ref, g_ref, along_ref, across_ref, near_ref, far_ref,
 ):
     mine, fold = mine_ref[...], fold_ref[...]
-    along_ref[...] = 4.0 * dot(side_ref[0], fold, NT)
-    across_ref[...] = 4.0 * dot(mine, side_ref[1], NT)
-    near_ref[...] = 4.0 * dot(dot(mine, face_ref[0]), fold, NT)
-    far_ref[...] = 4.0 * dot(dot(mine, face_ref[1]), fold, NT)
+    along_ref[...] = 4.0 * dot3(side_ref[0], fold, NT)
+    across_ref[...] = 4.0 * dot3(mine, side_ref[1], NT)
+    near_ref[...] = 4.0 * dot3(dot3(mine, face_ref[0]), fold, NT)
+    far_ref[...] = 4.0 * dot3(dot3(mine, face_ref[1]), fold, NT)
     ghost_body(
         half_ref, u_ref, coef_ref, join_ref, row_ref, col_ref, along_ref, across_ref, near_ref,
         far_ref, out_ref, g_ref,
@@ -617,6 +636,10 @@
             ],
         ),
         out_shape=jax.ShapeDtypeStruct(u.shape, f32),
+        cost_estimate=pl.CostEstimate(
+            flops=40 * planes * rows * cols, bytes_accessed=12 * planes * rows * cols,
+            transcendentals=0,
+        ),
     )(upper, u, coef, join, row_value, col_value, face_v, side_v, mine, fold)
 
 
@@ -664,22 +687,22 @@
             total = total + by_col[:, k : k + PANELS]
         cols_ref[:, j * PANELS : (j + 1) * PANELS] += total
     fold = fold_ref[...]
-    face_ref[...] += dot(value, fold)
-    rows_ref[...] += dot(stage_ref[...], fold)
+    face_ref[...] += dot3(value, fold)
+    rows_ref[...] += dot3(stage_ref[...], fold)
 
     @pl.when(step == pl.num_programs(0) - 1)
     def _():
         mine = mine_ref[...]
-        part_ref[:PANELS, :] = dot(mine, face_ref[...], TN)
-        part_ref[PANELS : PANELS + 2 * planes, :] = dot(pick_row_ref[...], rows_ref[...])
-        part_ref[PANELS + 2 * planes :, :] = dot(
-            dot(cols_ref[...], pick_col_ref[...]), mine, TN
+        part_ref[:PANELS, :] = dot3(mine, face_ref[...], TN)
+        part_ref[PANELS : PANELS + 2 * planes, :] = dot3(pick_row_ref[...], rows_ref[...])
+        part_ref[PANELS + 2 * planes :, :] = dot3(
+            dot3(cols_ref[...], pick_col_ref[...]), mine, TN
         )
 
 
 def finish_boundary(upper, f, coef, join, far, row_value, col_value, fold, mine):
     planes, rows, cols = f.shape
-    width = cols // 3
+    width = cols // 2
     block, flat = block_specs(planes, rows, width)
     front = pl.BlockSpec((planes, rows, width), lambda i, u: (0, 0, 0))
     back = pl.BlockSpec((planes, rows, width), lambda i, u: (0, 0, jnp.maximum(i - 1, 0)))
@@ -695,7 +718,7 @@
         boundary_body,
         grid_spec=pltpu.PrefetchScalarGridSpec(
             num_scalar_prefetch=1,
-            grid=(3,),
+            grid=(2,),
             in_specs=[
                 block,
                 block,
@@ -719,7 +742,7 @@
         ),
         out_shape=[
             jax.ShapeDtypeStruct((planes, rows, width), f32),
-            jax.ShapeDtypeStruct((planes, rows, 2 * width), f32),
+            jax.ShapeDtypeStruct((planes, rows, cols - width), f32),
             jax.ShapeDtypeStruct((PANELS + 4 * planes, PANELS), f32),
         ],
     )(
@@ -729,7 +752,7 @@
 
 
 TINY = 2.0**-60
-GROUP = 32
+GROUP = 16
 UNROLL = 4
 TALL = 32
 LANES = 256
@@ -819,7 +842,7 @@
 
     @pl.when(pl.program_id(0) == 0)
     def _():
-        along = dot(side_ref[0], fold_ref[...], NT) * (4.0 * TINY / col_ref[...])
+        along = dot(side_ref[1], fold_ref[...], NT) * (4.0 * TINY / col_ref[...])
         odd = lax.broadcasted_iota(jnp.int32, (8, grid), 0) % 2 == 1
         for k in range(UNROLL - 1):
             along_ref[k] = jnp.zeros((8, grid), jnp.float32)
@@ -839,7 +862,7 @@
         for k in range(3):
             pick_ref[2 * depth * k : 2 * depth * (k + 1), :] = pick
 
-    across = dot(rows_fold_ref[...], side_ref[1], NT) * (4.0 * TINY / row_ref[...])
+    across = dot(rows_fold_ref[...], side_ref[0], NT) * (4.0 * TINY / row_ref[...])
     high = across.astype(jnp.bfloat16)
     rest = across - high.astype(jnp.float32)
     middle = rest.astype(jnp.bfloat16)
@@ -921,7 +944,7 @@
             flops=20 * depth * grid * cols, bytes_accessed=24 * grid * cols, transcendentals=0
         ),
     )(
-        place, low, high, eigen[:, None], eigen[None, :], edge_value[:, None],
+        place, low, high, eigen[:grid, None], eigen[None, :], edge_value[:grid, None],
         edge_value[None, :], near, distant, side_v, fold, fold,
     )
 
@@ -934,8 +957,8 @@
     edge = grid // PANELS
     groups = [list(range(half)), list(range(half, devices))]
     local = depth <= 32 and rows % 8 == 0
-    block = grid // 4
-    split = grid // 3
+    split = grid // 2
+    block = split // 2
     tables = {
         name: value.astype(np.float32) for name, value in small_tables(depth, grid, edge).items()
     }
@@ -980,7 +1003,7 @@
         if local:
             index = (rank % half).astype(jnp.int32)
             place = jnp.where(is_upper, half - index, index + 1).reshape(1)
-            weight = weights(depth, place, eigen[:, None], eigen[None, :split], block)
+            weight = weights(depth, place, eigen[:split, None], eigen[None, :], block)
             spectrum, mixed, corner, weight = lax.optimization_barrier(
                 (spectrum, mixed, corner, weight)
             )
@@ -1014,21 +1037,22 @@
             bit *= 2
         other = hop(part, bit)
         if local:
-            u, part, other = lax.optimization_barrier((u, part, other))
-            u = exchange(u).reshape(grid, split)
+            early, part, other = lax.optimization_barrier((u, part, other))
+            u = exchange(early).reshape(grid, split)
         face_v, side_v = panel_potential(part, other, tb, mixed, corner)
         if local:
             sent = add_late(
                 upper, sent, coef, join, my_edge[:, None], edge_value[None, :], face_v, side_v,
                 my_fold, fold, split,
             )
+            u, sent = lax.optimization_barrier((u, sent))
             sent = exchange(sent).reshape(grid, grid - split)
-            front = fold[:split]
-            rows_v = dot(fold * 4.0, jnp.concatenate([face_v[0], face_v[1]], 1), precision=HIGH)
-            near = dot(rows_v[:, :PANELS], front, NT, precision=HIGH)
-            distant = dot(rows_v[:, PANELS:], front, NT, precision=HIGH)
+            near, distant = (
+                dot(dot(4.0 * fold[:split], face_v[i], NT, precision=HIGH), fold, NT, precision=HIGH)
+                for i in (0, 1)
+            )
             layers = plane_layers(
-                depth, place, *weight, eigen, edge_value, near, distant, side_v, fold, block
+                depth, place, *weight, eigen, edge_value, near, distant, side_v, fold, block,
             )
             return double_product([u, layers, sent], *sine_pair)[None]
         else:

time: 161 us -> 158 us (0.981)
  waiting for transfers between devices: 25.6 us -> 20.6 us
  Pallas kernels: 90.3 us -> 92 us
    all_to_all x3, waiting for transfers between devices: 11.3 us -> 6.23 us  [exchange(): lax.all_to_all(x, AXES, split_axis=0, concat_axis=0, tiled=True, axis_ind...]
    pallas_call x1, Pallas kernels: 15.8 us -> 19.6 us  [plane_layers(): pl.pallas_call(functools.partial(plane_body, depth), grid_spec=pltpu.Pref...]
    pallas_call x1, Pallas kernels: 7.15 us -> 9.89 us  [weights(): pl.pallas_call(functools.partial(weight_body, depth), grid_spec=pltpu.Pre...]
    dot_general x3 -> x4, matrix products: 3.22 us -> 3.81 us  [dot(): lax.dot_general(a, b, (dims, ((), ())), precision=precision, preferred_el...]
  transfers between devices with their start and end apart: 6 -> 6, of which waited for: 5 -> 5; matrix products, arithmetic and copies ran while one was open for 4% -> 5% of each run, Pallas kernels for 37% -> 40%
where the time goes in v4:
time: 158 us; the launch traced here: 157 us
  Pallas kernels  92 us (58%)
  waiting for transfers between devices  20.6 us (13%)
  starting transfers between devices  18.9 us (12%)
  blocking collectives  13.1 us (8%)
  local copies, waits for them, and re-layouts  7.63 us (5%)
  matrix products  3.81 us (2%)
    pallas_call x1, Pallas kernels, plane_layers(): pl.pallas_call(functools.partial(plane_body, depth), grid_spec=pltpu.Pref...  19.6 us
    pallas_call x2, Pallas kernels, double_product(): pl.pallas_call(functools.partial(product_body, len(values)), grid=(2 * st...  19.5 us
    all_to_all x3, starting transfers between devices, exchange(): lax.all_to_all(x, AXES, split_axis=0, concat_axis=0, tiled=True, axis_ind...  14.1 us
    all_gather x1, blocking collectives, on_device(): part = lax.all_gather(part, 'py', axis=0, tiled=False).sum(0)  13.1 us
    pallas_call x1, Pallas kernels, panel_potential(): pl.pallas_call(panels_body, out_shape=[jax.ShapeDtypeStruct((2, PANELS, P...  12.2 us
    ppermute x2, waiting for transfers between devices, hop(): return lax.ppermute(x, 'px', [(i, i ^ bit) for i in range(slow)])  10.1 us
    pallas_call x1, Pallas kernels, weights(): pl.pallas_call(functools.partial(weight_body, depth), grid_spec=pltpu.Pre...  9.89 us
    pallas_call x1, Pallas kernels, corner_table(): pl.pallas_call(functools.partial(corner_body, edge, depth), grid=(hb // S...  7.59 us
  transfers between devices with their start and end apart: 6, of which 5 were waited for; matrix products, arithmetic and copies ran while one was open for 5% of the time, Pallas kernels for 40%

profile of v4, /device:TPU:0, one launch (start us, length us, event | category | flops | bytes accessed | tf_op | source)
XLA Modules:
  0.0 157.0 jit_solution(3271628770238120014)
XLA Ops:
  0.0 9.5 %shard_map.154 = f32[768,768]{1,0:T(8,128)} custom-call(bf16[768,768]{1,0:T(8,128)(2,1)} %constant.80.clone.high_ref, bf16[768,768]{1,0:T(8,128)(2,1)} %constant.81.clone.low_ref, f32[768,768]{1,0:T(8,128)} %bitcast.26), custom_call_target="tpu_custom_call" | custom-call | tf_op jit(solution)/shard_map/pallas_call | solution.py:107
  9.5 0.0 copy-start.8
  9.5 6.5 %all-to-all-start = ((f32[16,48,768]{2,1,0:T(8,128)}), f32[16,48,768]{2,1,0:T(8,128)S(1)}, u32[]{:S(2)}, u32[]{:S(2)}) async-start(f32[16,48,768]{2,1,0:T(8,128)} %bitcast.22), calls=%async_computation | async-start | bytes 4718592 | tf_op jit(solution)/shard_map/all_to_all | solution.py:972
  16.0 0.0 copy-done.8
  16.0 0.1 dynamic_slice.9
  16.1 0.7 broadcast_add_fusion.mu_ref
  16.9 3.1 %shard_map.158 = (f32[16,48,768]{2,1,0:T(8,128)}, f32[48,768]{1,0:T(8,128)}) custom-call(f32[48,768]{1,0:T(8,128)} %broadcast_add_fusion.mu_ref), custom_call_target="tpu_custom_call" | custom-call | flops 11796480 | bytes 2359296 | tf_op jit(solution)/shard_map/pallas_call | solution.py:437
  19.9 9.9 %shard_map.157 = (f32[384,768]{1,0:T(8,128)}, f32[384,768]{1,0:T(8,128)}) custom-call(s32[1]{0:T(128)} %bitcast.3.place_ref, f32[384,1]{1,0:T(8,128)} %constant.97.row_ref.row_eigen_ref, f32[1,768]{1,0:T(1,128)} %constant.98.col_ref.col_eigen_ref), custom_call_target="tpu_custom_call" | custom-call | flops 37748736 | bytes 2359296 | tf_op jit(solution)/shard_map/pallas_call | solution.py:807
  29.8 5.9 %shard_map.155.mixed_ref = f32[2,16,128,256]{3,2,1,0:T(8,128)} custom-call(f32[128,256]{1,0:T(8,128)} %constant.89.clone.wave_ref), custom_call_target="tpu_custom_call" | custom-call | flops 134217728 | bytes 2097152 | tf_op jit(solution)/shard_map/pallas_call | solution.py:167
  35.7 7.6 %shard_map.156 = (f32[64,64,128]{2,1,0:T(8,128)}, f32[64,64,128]{2,1,0:T(8,128)}) custom-call(f32[64,128]{1,0:T(8,128)} %constant.90.clone.wave_ref), custom_call_target="tpu_custom_call" | custom-call | flops 134217728 | bytes 2097152 | tf_op jit(solution)/shard_map/pallas_call | solution.py:217
  43.3 5.1 %all-to-all-done.f_ref = f32[16,48,768]{2,1,0:T(8,128)S(1)} async-done(((f32[16,48,768]{2,1,0:T(8,128)}), f32[16,48,768]{2,1,0:T(8,128)S(1)}, u32[]{:S(2)}, u32[]{:S(2)}) %all-to-all-start) | async-done | bytes 2359328 | tf_op jit(solution)/shard_map/all_to_all | solution.py:972
  48.4 0.0 copy-start
  48.4 1.4 copy-done
  49.8 3.7 %shard_map.159 = f32[48,768]{1,0:T(8,128)} custom-call(s32[1]{0:T(128)} %bitcast.half_ref, f32[16,48,768]{2,1,0:T(8,128)} %copy-done, f32[16,48,768]{2,1,0:T(8,128)} %get-tuple-element.32.coef_ref), custom_call_target="tpu_custom_call" | custom-call | tf_op jit(solution)/shard_map/pallas_call | solution.py:494
  53.5 2.6 %collective-permute-start = (f32[48,768]{1,0:T(8,128)}, f32[48,768]{1,0:T(8,128)S(1)}, u32[]{:S(2)}, u32[]{:S(2)}) collective-permute-start(f32[48,768]{1,0:T(8,128)} %shard_map.159), channel_id=1, source_target_pairs={{0,16},{1,17},{2,18},{3,19},{4,20},{5,21},{6,22},{7,23},{8,24},{9,... | collective-permute-start | bytes 442376 | tf_op jit(solution)/shard_map/ppermute | solution.py:1016
  56.1 0.8 dynamic-slice_bitcast_fusion
  56.8 0.7 copy.17.row_ref
  57.5 1.3 constant_dynamic-slice_fusion.mine_ref
  58.9 4.2 %collective-permute-done.far_ref = f32[48,768]{1,0:T(8,128)S(1)} collective-permute-done((f32[48,768]{1,0:T(8,128)}, f32[48,768]{1,0:T(8,128)S(1)}, u32[]{:S(2)}, u32[]{:S(2)}) %collective-permute-start) | collective-permute-done | bytes 147488 | tf_op jit(solution)/shard_map/ppermute | solution.py:1016
  63.0 0.0 copy-start.6
  63.0 0.7 copy-done.6
  63.7 6.3 %shard_map.160 = (f32[16,48,384]{2,1,0:T(8,128)}, f32[16,48,384]{2,1,0:T(8,128)}, f32[192,128]{1,0:T(8,128)}) custom-call(s32[1]{0:T(128)} %bitcast.half_ref, f32[16,48,768]{2,1,0:T(8,128)} %copy-done, f32[16,48,768]{2,1,0:T(8,128)} %get-tuple-element.32.coef_ref, f32[48,768]{1,0:T(8,128)} %get-tuple-element.33.join_ref, f32[48,768]{1,0:T(8,128)} %copy-done.6, ...), custom_call_target="tpu_custom_call" | custom-call | tf_op jit(solution)/shard_map/pallas_call | solution.py:717
  70.0 13.1 %all-gather = f32[1536,128]{1,0:T(8,128)S(1)} all-gather(f32[192,128]{1,0:T(8,128)} %get-tuple-element.35), channel_id=2, replica_groups=mesh['px'=4,'py'=8] {'py'}, dimensions={0}, use_global_device_ids=true | all-gather | bytes 884736 | tf_op jit(solution)/shard_map/all_gather | solution.py:1033
  83.1 0.4 collective-permute-start.1
  83.5 4.8 %collective-permute-done.1 = f32[192,128]{1,0:T(8,128)S(1)} collective-permute-done((f32[192,128]{1,0:T(8,128)S(1)}, f32[192,128]{1,0:T(8,128)S(1)}, u32[]{:S(2)}, u32[]{:S(2)}) %collective-permute-start.1) | collective-permute-done | bytes 98336 | tf_op jit(solution)/shard_map/ppermute | solution.py:977
  88.3 0.0 copy-start.7
  88.3 1.9 %collective-permute-start.2 = (f32[192,128]{1,0:T(8,128)S(1)}, f32[192,128]{1,0:T(8,128)S(1)}, u32[]{:S(2)}, u32[]{:S(2)}) collective-permute-start(f32[192,128]{1,0:T(8,128)S(1)} %add.40.own_ref), channel_id=1, source_target_pairs={{0,16},{8,24},{16,0},{24,8},{1,17},{9,25},{17,1},{25,9},{2,18},{10... | collective-permute-start | bytes 294920 | tf_op jit(solution)/shard_map/ppermute | solution.py:977
  90.2 5.4 %collective-permute-done.2.other_ref = f32[192,128]{1,0:T(8,128)S(1)} collective-permute-done((f32[192,128]{1,0:T(8,128)S(1)}, f32[192,128]{1,0:T(8,128)S(1)}, u32[]{:S(2)}, u32[]{:S(2)}) %collective-permute-start.2) | collective-permute-done | bytes 98336 | tf_op jit(solution)/shard_map/ppermute | solution.py:977
  95.6 0.0 copy-done.7
  95.6 0.6 copy-done.9
  96.2 3.7 %all-to-all-start.1 = ((f32[16,48,384]{2,1,0:T(8,128)}), f32[16,48,384]{2,1,0:T(8,128)S(1)}, u32[]{:S(2)}, u32[]{:S(2)}) async-start(f32[16,48,384]{2,1,0:T(8,128)} %get-tuple-element.36), calls=%async_computation.1 | async-start | bytes 2359296 | tf_op jit(solution)/shard_map/all_to_all | solution.py:972
  99.9 12.2 %shard_map.161 = (f32[2,128,128]{2,1,0:T(8,128)}, f32[2,64,128]{2,1,0:T(8,128)}) custom-call(f32[192,128]{1,0:T(8,128)} %copy-done.7, f32[192,128]{1,0:T(8,128)} %copy-done.9, f32[256,128]{1,0:T(8,128)} %constant.83.clone.basis_ref, f32[2,256,256]{2,1,0:T(8,128)} %constant.84.clone.face_ref, f32[128,256]{1,0:T(8,128)} %constant.85.clone.side_ref, ...), custom_call_target="tpu_custom_call" | custom-call | flops 5000000000 | bytes 8388608 | tf_op jit(solution)/shard_map/pallas_call | solution.py:388
  112.1 4.2 %shard_map.162 = f32[16,48,384]{2,1,0:T(8,128)} custom-call(s32[1]{0:T(128)} %bitcast.half_ref, f32[16,48,384]{2,1,0:T(8,128)} %get-tuple-element.37.u_ref, f32[16,48,768]{2,1,0:T(8,128)} %get-tuple-element.32.coef_ref, f32[48,768]{1,0:T(8,128)} %get-tuple-element.33.join_ref, f32[48,1]{1,0:T(8,128)} %copy.17.row_ref, f32[1,768]{1,0:T(1,128)} %constant.99.col_ref, ...), custom_call_target="tpu_custom_call" | custom-call | flops 11796480 | bytes 3538944 | tf_op jit(solution)/shard_map/pallas_call | solution.py:613
  116.3 1.2 all-to-all-done.1
  117.5 1.0 copy-done.2
  118.5 3.9 %all-to-all-start.2 = ((f32[16,48,384]{2,1,0:T(8,128)}), f32[16,48,384]{2,1,0:T(8,128)S(1)}, u32[]{:S(2)}, u32[]{:S(2)}) async-start(f32[16,48,384]{2,1,0:T(8,128)} %shard_map.162), calls=%async_computation.2 | async-start | bytes 2359296 | tf_op jit(solution)/shard_map/all_to_all | solution.py:972
  122.4 0.0 copy-done.4
  122.5 0.0 copy-done.5
  122.5 0.2 fusion
  122.7 0.2 fusion.2
  123.0 0.0 copy-done.1
  123.0 1.7 %fusion.6.near_ref = f32[384,768]{1,0:T(8,128)} fusion(f32[384,128]{1,0:T(8,128)S(1)} %fusion.2, f32[768,128]{1,0:T(8,128)S(1)} %copy-done.1), kind=kOutput, calls=%fused_computation.9 | convolution fusion | flops 226492416 | bytes 1769472 | tf_op jit(solution)/shard_map/dot_general | solution.py:20
  124.6 1.7 %fusion.7.distant_ref = f32[384,768]{1,0:T(8,128)} fusion(f32[384,128]{1,0:T(8,128)S(1)} %fusion, f32[768,128]{1,0:T(8,128)S(1)} %copy-done.1), kind=kOutput, calls=%fused_computation.10 | convolution fusion | flops 226492416 | bytes 1769472 | tf_op jit(solution)/shard_map/dot_general | solution.py:20
  126.3 19.6 %shard_map.163.refs_1_ = f32[384,768]{1,0:T(8,128)} custom-call(s32[1]{0:T(128)} %bitcast.3.place_ref, f32[384,768]{1,0:T(8,128)} %get-tuple-element.46.low_ref, f32[384,768]{1,0:T(8,128)} %get-tuple-element.47.high_ref, f32[384,1]{1,0:T(8,128)} %constant.97.row_ref.row_eigen_ref, f32[1,768]{1,0:T(1,128)} %constant.98.col_ref.col_eigen_ref, ...), custom_call_target="tpu_custom_call" | custom-call | flops 188743680 | bytes 7077888 | tf_op jit(solution)/shard_map/pallas_call | solution.py:917
  145.9 0.0 all-to-all-done.2
  145.9 0.0 copy-start.3
  145.9 1.0 copy-done.3
  147.0 10.0 %shard_map.164 = f32[768,768]{1,0:T(8,128)} custom-call(bf16[768,768]{1,0:T(8,128)(2,1)} %constant.80.clone.high_ref, bf16[768,768]{1,0:T(8,128)(2,1)} %constant.81.clone.low_ref, f32[768,384]{1,0:T(8,128)} %bitcast.23, f32[384,768]{1,0:T(8,128)} %shard_map.163.refs_1_, f32[768,384]{1,0:T(8,128)} %bitcast.24), custom_call_target="tpu_custom_call" | custom-call | tf_op jit(solution)/shard_map/pallas_call | solution.py:107
  (7 shorter events, 0.1 us)
Async XLA Ops:
  9.5 6.5 %copy-start.8 = (f32[768]{0:T(1024)S(1)}, f32[768]{0:T(1024)}, u32[]{:S(2)}) copy-start(f32[768]{0:T(1024)} %constant.91.clone) | copy-start | bytes 9220
  9.5 38.8 %all-to-all-start = ((f32[16,48,768]{2,1,0:T(8,128)}), f32[16,48,768]{2,1,0:T(8,128)S(1)}, u32[]{:S(2)}, u32[]{:S(2)}) async-start(f32[16,48,768]{2,1,0:T(8,128)} %bitcast.22), calls=%async_computation | async-start | bytes 4718592 | tf_op jit(solution)/shard_map/all_to_all | solution.py:972
  48.4 1.4 copy-start
  53.5 9.6 %collective-permute-start = (f32[48,768]{1,0:T(8,128)}, f32[48,768]{1,0:T(8,128)S(1)}, u32[]{:S(2)}, u32[]{:S(2)}) collective-permute-start(f32[48,768]{1,0:T(8,128)} %shard_map.159), channel_id=1, source_target_pairs={{0,16},{1,17},{2,18},{3,19},{4,20},{5,21},{6,22},{7,23},{8,24},{9,... | collective-permute-start | bytes 442376 | tf_op jit(solution)/shard_map/ppermute | solution.py:1016
  63.0 0.7 copy-start.6
  83.1 5.1 %collective-permute-start.1 = (f32[192,128]{1,0:T(8,128)S(1)}, f32[192,128]{1,0:T(8,128)S(1)}, u32[]{:S(2)}, u32[]{:S(2)}) collective-permute-start(f32[192,128]{1,0:T(8,128)S(1)} %reduce_sum.9), channel_id=1, source_target_pairs={{0,8},{8,0},{16,24},{24,16},{1,9},{9,1},{17,25},{25,17},{2,10},{10... | collective-permute-start | bytes 294920 | tf_op jit(solution)/shard_map/ppermute | solution.py:977
  88.3 7.3 %copy-start.7 = (f32[192,128]{1,0:T(8,128)}, f32[192,128]{1,0:T(8,128)S(1)}, u32[]{:S(2)}) copy-start(f32[192,128]{1,0:T(8,128)S(1)} %add.40.own_ref) | copy-start | bytes 294916
  88.3 7.3 %collective-permute-start.2 = (f32[192,128]{1,0:T(8,128)S(1)}, f32[192,128]{1,0:T(8,128)S(1)}, u32[]{:S(2)}, u32[]{:S(2)}) collective-permute-start(f32[192,128]{1,0:T(8,128)S(1)} %add.40.own_ref), channel_id=1, source_target_pairs={{0,16},{8,24},{16,0},{24,8},{1,17},{9,25},{17,1},{25,9},{2,18},{10... | collective-permute-start | bytes 294920 | tf_op jit(solution)/shard_map/ppermute | solution.py:977
  95.6 0.6 copy-start.9
  96.2 21.3 %all-to-all-start.1 = ((f32[16,48,384]{2,1,0:T(8,128)}), f32[16,48,384]{2,1,0:T(8,128)S(1)}, u32[]{:S(2)}, u32[]{:S(2)}) async-start(f32[16,48,384]{2,1,0:T(8,128)} %get-tuple-element.36), calls=%async_computation.1 | async-start | bytes 2359296 | tf_op jit(solution)/shard_map/all_to_all | solution.py:972
  117.5 1.0 copy-start.2
  117.5 4.9 %copy-start.4 = (f32[384,128]{1,0:T(8,128)S(1)}, f32[384,128]{1,0:T(8,128)}, u32[]{:S(2)}) copy-start(f32[384,128]{1,0:T(8,128)} %constant.103) | copy-start | bytes 589828
  117.5 4.9 %copy-start.5 = (f32[2,128,128]{2,1,0:T(8,128)S(1)}, f32[2,128,128]{2,1,0:T(8,128)}, u32[]{:S(2)}) copy-start(f32[2,128,128]{2,1,0:T(8,128)} %get-tuple-element.43.face_ref) | copy-start | bytes 393220
  117.5 5.5 %copy-start.1 = (f32[768,128]{1,0:T(8,128)S(1)}, f32[768,128]{1,0:T(8,128)}, u32[]{:S(2)}) copy-start(f32[768,128]{1,0:T(8,128)} %constant.82.clone.fold_ref.rows_fold_ref) | copy-start | bytes 1179652
  118.5 27.4 %all-to-all-start.2 = ((f32[16,48,384]{2,1,0:T(8,128)}), f32[16,48,384]{2,1,0:T(8,128)S(1)}, u32[]{:S(2)}, u32[]{:S(2)}) async-start(f32[16,48,384]{2,1,0:T(8,128)} %shard_map.162), calls=%async_computation.2 | async-start | bytes 2359296 | tf_op jit(solution)/shard_map/all_to_all | solution.py:972
  145.9 1.0 copy-start.3

commit v5 on v4

--- a/solution.py
+++ b/solution.py
@@ -284,10 +284,18 @@
 
 def panels_body(
     own_ref, other_ref, basis_ref, face_ref, side_ref, level_ref, cross_ref, turn_ref,
-    mixed_ref, front_ref, back_ref, face_out_ref, side_out_ref,
-    fx_ref, hat_ref, acc_ref, toside_ref, xs_ref, tox_ref,
+    mixed_hbm, front_hbm, back_hbm, face_out_ref, side_out_ref,
+    fx_ref, hat_ref, acc_ref, toside_ref, xs_ref, tox_ref, mixed_ref, front_ref, back_ref, sems,
 ):
     half = mixed_ref.shape[1]
+    loads = [
+        pltpu.make_async_copy(source, target, sems.at[k])
+        for k, (source, target) in enumerate(
+            ((mixed_hbm, mixed_ref), (front_hbm, front_ref), (back_hbm, back_ref))
+        )
+    ]
+    for load in loads:
+        load.start()
     hb = PANELS // 2
     total = (own_ref[...] + other_ref[...]) * 0.5
     gap = (own_ref[...] - other_ref[...]) * 0.5
@@ -303,6 +311,7 @@
         fx_ref[0, s] = dot3(faces[s], basis, NT)
         fx_ref[1, s] = dot3(faces[s], basis, ((0,), (1,)))
 
+    loads[0].wait()
     for s in (0, 1):
 
         def face_rows(block, _, s=s):
@@ -348,6 +357,8 @@
     ys = dot3(sides[0][:, :hb], turn_ref[0], TN) + dot3(sides[0][:, hb:], turn_ref[1], TN)
     width = xs_ref.shape[1]
     to_y = []
+    loads[1].wait()
+    loads[2].wait()
     for t, table_ref in ((0, front_ref), (1, back_ref)):
         mine = ys[:, t * width : (t + 1) * width]
 
@@ -385,8 +396,10 @@
     half = mixed.shape[1]
     width = corner[0].shape[2]
     f32 = jnp.float32
+    vmem = pl.BlockSpec(memory_space=pltpu.VMEM)
     return pl.pallas_call(
         panels_body,
+        in_specs=[vmem] * 8 + [pl.BlockSpec(memory_space=pl.ANY)] * 3,
         out_shape=[
             jax.ShapeDtypeStruct((2, PANELS, PANELS), f32),
             jax.ShapeDtypeStruct((2, 4 * half, PANELS), f32),
@@ -398,6 +411,10 @@
             pltpu.VMEM((2, 4 * half, 2 * PANELS), f32),
             pltpu.VMEM((PANELS, width), f32),
             pltpu.VMEM((PANELS, width), f32),
+            pltpu.VMEM(mixed.shape, f32),
+            pltpu.VMEM(corner[0].shape, f32),
+            pltpu.VMEM(corner[1].shape, f32),
+            pltpu.SemaphoreType.DMA((3,)),
         ],
         cost_estimate=pl.CostEstimate(
             flops=5_000_000_000, bytes_accessed=4 * (mixed.size + 2 * corner[0].size),
@@ -824,8 +841,8 @@
 
 def plane_body(
     depth, place_ref, low_ref, high_ref, row_eigen_ref, col_eigen_ref, row_ref, col_ref,
-    near_ref, distant_ref, side_ref, rows_fold_ref, fold_ref, out_ref, along_ref, across_ref,
-    pick_ref,
+    face_ref, side_ref, rows_fold_ref, fold_ref, out_ref, along_ref, across_ref, pick_ref,
+    near_ref, distant_ref,
 ):
     half = depth // 2
     block, grid = out_ref.shape
@@ -873,6 +890,12 @@
         across_ref[slot(k)] = pair[:, :PANELS]
         across_ref[slot(k + 1)] = pair[:, PANELS:]
 
+    for k, target in ((0, near_ref), (1, distant_ref)):
+        face = dot3(4.0 * rows_fold_ref[...], face_ref[k], NT)
+        for at in range(0, grid, LANES):
+            lanes = slice(at, at + LANES)
+            target[:, lanes] = dot3(face, fold_ref[lanes, :], NT)
+
     for part in range(grid // LANES):
         lanes = slice(part * LANES, (part + 1) * LANES)
 
@@ -907,7 +930,7 @@
         lax.fori_loop(0, block // TALL, rows, 0)
 
 
-def plane_layers(depth, place, low, high, eigen, edge_value, near, distant, side_v, fold, block):
+def plane_layers(depth, place, low, high, eigen, edge_value, face_v, side_v, fold, block):
     grid, cols = low.shape
     slots = whole_steps(depth // 2) + whole_steps(depth)
     f32 = jnp.float32
@@ -926,8 +949,7 @@
                 flat,
                 tall,
                 flat,
-                wide,
-                wide,
+                pl.BlockSpec(face_v.shape, lambda i, u: (0, 0, 0)),
                 pl.BlockSpec(side_v.shape, lambda i, u: (0, 0, 0)),
                 pl.BlockSpec((block, PANELS), lambda i, u: (i, 0)),
                 pl.BlockSpec((cols, PANELS), lambda i, u: (0, 0)),
@@ -937,6 +959,8 @@
                 pltpu.VMEM((slots, 8, cols), f32),
                 pltpu.VMEM((slots, block, PANELS), f32),
                 pltpu.VMEM((6 * depth, depth * PANELS), jnp.bfloat16),
+                pltpu.VMEM((block, cols), f32),
+                pltpu.VMEM((block, cols), f32),
             ],
         ),
         out_shape=jax.ShapeDtypeStruct((grid, cols), f32),
@@ -945,7 +969,7 @@
         ),
     )(
         place, low, high, eigen[:grid, None], eigen[None, :], edge_value[:grid, None],
-        edge_value[None, :], near, distant, side_v, fold, fold,
+        edge_value[None, :], face_v, side_v, fold, fold,
     )
 
 
@@ -975,6 +999,11 @@
 
     def hop(x, bit):
         return lax.ppermute(x, "px", [(i, i ^ bit) for i in range(slow)])
+
+    def swap(x):
+        return lax.ppermute(x, "py", [(i, i ^ 1) for i in range(fast)])
+
+    alternate = [list(range(0, fast, 2)), list(range(1, fast, 2))]
 
     def on_device(charge):
         rank = lax.axis_index(AXES)
@@ -1030,12 +1059,20 @@
             lines = jnp.stack([lines_y, lines_x])
             lines = jnp.where(is_upper, lines[:, :, ::-1], lines)
             part = jnp.concatenate([face, lines.reshape(-1, PANELS)])
-        part = lax.all_gather(part, "py", axis=0, tiled=False).sum(0)
+        middle = part.shape[0] // 2
+        first = lax.axis_index("py") % 2 == 0
+        part = part + swap(part)
+        part = jnp.where(first, part[:middle], part[middle:])
+        part = lax.all_gather(part, "py", axis=0, tiled=False, axis_index_groups=alternate).sum(0)
         bit = 1
         while bit < slow // 2:
             part = part + hop(part, bit)
             bit *= 2
-        other = hop(part, bit)
+        both = jnp.concatenate([part, hop(part, bit)])
+        back = swap(both)
+        low, high = jnp.where(first, both, back), jnp.where(first, back, both)
+        part = jnp.concatenate([low[:middle], high[:middle]])
+        other = jnp.concatenate([low[middle:], high[middle:]])
         if local:
             early, part, other = lax.optimization_barrier((u, part, other))
             u = exchange(early).reshape(grid, split)
@@ -1047,12 +1084,8 @@
             )
             u, sent = lax.optimization_barrier((u, sent))
             sent = exchange(sent).reshape(grid, grid - split)
-            near, distant = (
-                dot(dot(4.0 * fold[:split], face_v[i], NT, precision=HIGH), fold, NT, precision=HIGH)
-                for i in (0, 1)
-            )
             layers = plane_layers(
-                depth, place, *weight, eigen, edge_value, near, distant, side_v, fold, block,
+                depth, place, *weight, eigen, edge_value, face_v, side_v, fold, block,
             )
             return double_product([u, layers, sent], *sine_pair)[None]
         else:

time: 158 us -> 154 us (0.975)
  matrix products: 3.81 us -> 0 us
  blocking collectives: 13.1 us -> 10.6 us
  other arithmetic: 0.79 us -> 2.98 us
    dot_general x4 -> x0, matrix products: 3.81 us -> none  [dot(): lax.dot_general(a, b, (dims, ((), ())), precision=precision, preferred_el...]
    ppermute x0 -> x2, waiting for transfers between devices: none -> 2.78 us  [swap(): return lax.ppermute(x, 'py', [(i, i ^ 1) for i in range(fast)])]
    all_gather x1, blocking collectives: 13.1 us -> 10.6 us  [on_device(): lax.all_gather(part, 'py', axis=0, tiled=False, axis_index_groups=alternate)]
    ppermute x2, waiting for transfers between devices: 10.1 us -> 7.78 us  [hop(): return lax.ppermute(x, 'px', [(i, i ^ bit) for i in range(slow)])]
    unnamed x20 -> x10, local copies, waits for them, and re-layouts: 4.76 us -> 4.14 us
  transfers between devices with their start and end apart: 6 -> 8, of which waited for: 5 -> 7; matrix products, arithmetic and copies ran while one was open for 5% -> 2% of each run, Pallas kernels for 40% -> 41%
where the time goes in v5:
time: 154 us; the launch traced here: 153 us
  Pallas kernels  92.3 us (60%)
  waiting for transfers between devices  21.8 us (14%)
  starting transfers between devices  18.6 us (12%)
  blocking collectives  10.6 us (7%)
  local copies, waits for them, and re-layouts  7.02 us (5%)
  other arithmetic  2.98 us (2%)
    pallas_call x1, Pallas kernels, plane_layers(): pl.pallas_call(functools.partial(plane_body, depth), grid_spec=pltpu.Pref...  20.7 us
    pallas_call x2, Pallas kernels, double_product(): pl.pallas_call(functools.partial(product_body, len(values)), grid=(2 * st...  19.5 us
    all_to_all x3, starting transfers between devices, exchange(): lax.all_to_all(x, AXES, split_axis=0, concat_axis=0, tiled=True, axis_ind...  14 us
    pallas_call x1, Pallas kernels, panel_potential(): pl.pallas_call(panels_body, in_specs=[vmem] * 8 + [pl.BlockSpec(memory_sp...  11.3 us
    all_gather x1, blocking collectives, on_device(): lax.all_gather(part, 'py', axis=0, tiled=False, axis_index_groups=alternate)  10.6 us
    pallas_call x1, Pallas kernels, weights(): pl.pallas_call(functools.partial(weight_body, depth), grid_spec=pltpu.Pre...  9.87 us
    ppermute x2, waiting for transfers between devices, hop(): return lax.ppermute(x, 'px', [(i, i ^ bit) for i in range(slow)])  7.78 us
    pallas_call x1, Pallas kernels, corner_table(): pl.pallas_call(functools.partial(corner_body, edge, depth), grid=(hb // S...  7.61 us
  transfers between devices with their start and end apart: 8, of which 7 were waited for; matrix products, arithmetic and copies ran while one was open for 2% of the time, Pallas kernels for 41%

profile of v5, /device:TPU:0, one launch (start us, length us, event | category | flops | bytes accessed | tf_op | source)
XLA Modules:
  0.0 153.5 jit_solution(6263315970807763803)
XLA Ops:
  0.0 9.5 %shard_map.154 = f32[768,768]{1,0:T(8,128)} custom-call(bf16[768,768]{1,0:T(8,128)(2,1)} %constant.87.clone.high_ref, bf16[768,768]{1,0:T(8,128)(2,1)} %constant.88.clone.low_ref, f32[768,768]{1,0:T(8,128)} %bitcast.13), custom_call_target="tpu_custom_call" | custom-call | tf_op jit(solution)/shard_map/pallas_call | solution.py:107
  9.5 0.0 copy-start.4
  9.5 6.5 %all-to-all-start = ((f32[16,48,768]{2,1,0:T(8,128)}), f32[16,48,768]{2,1,0:T(8,128)S(1)}, u32[]{:S(2)}, u32[]{:S(2)}) async-start(f32[16,48,768]{2,1,0:T(8,128)} %bitcast.10), calls=%async_computation | async-start | bytes 4718592 | tf_op jit(solution)/shard_map/all_to_all | solution.py:996
  16.0 0.0 copy-done.4
  16.0 0.1 dynamic_slice.9
  16.1 0.7 broadcast_add_fusion.mu_ref
  16.8 3.1 %shard_map.158 = (f32[16,48,768]{2,1,0:T(8,128)}, f32[48,768]{1,0:T(8,128)}) custom-call(f32[48,768]{1,0:T(8,128)} %broadcast_add_fusion.mu_ref), custom_call_target="tpu_custom_call" | custom-call | flops 11796480 | bytes 2359296 | tf_op jit(solution)/shard_map/pallas_call | solution.py:454
  20.0 9.9 %shard_map.157 = (f32[384,768]{1,0:T(8,128)}, f32[384,768]{1,0:T(8,128)}) custom-call(s32[1]{0:T(128)} %bitcast.3.place_ref, f32[384,1]{1,0:T(8,128)} %constant.104.row_ref.row_eigen_ref, f32[1,768]{1,0:T(1,128)} %constant.105.col_ref.col_eigen_ref), custom_call_target="tpu_custom_call" | custom-call | flops 37748736 | bytes 2359296 | tf_op jit(solution)/shard_map/pallas_call | solution.py:824
  29.8 5.9 %shard_map.155.mixed_hbm = f32[2,16,128,256]{3,2,1,0:T(8,128)} custom-call(f32[128,256]{1,0:T(8,128)} %constant.96.clone.wave_ref), custom_call_target="tpu_custom_call" | custom-call | flops 134217728 | bytes 2097152 | tf_op jit(solution)/shard_map/pallas_call | solution.py:167
  35.7 7.6 %shard_map.156 = (f32[64,64,128]{2,1,0:T(8,128)}, f32[64,64,128]{2,1,0:T(8,128)}) custom-call(f32[64,128]{1,0:T(8,128)} %constant.97.clone.wave_ref), custom_call_target="tpu_custom_call" | custom-call | flops 134217728 | bytes 2097152 | tf_op jit(solution)/shard_map/pallas_call | solution.py:217
  43.4 5.0 %all-to-all-done.f_ref = f32[16,48,768]{2,1,0:T(8,128)S(1)} async-done(((f32[16,48,768]{2,1,0:T(8,128)}), f32[16,48,768]{2,1,0:T(8,128)S(1)}, u32[]{:S(2)}, u32[]{:S(2)}) %all-to-all-start) | async-done | bytes 2359328 | tf_op jit(solution)/shard_map/all_to_all | solution.py:996
  48.4 0.0 copy-start
  48.4 1.4 copy-done
  49.8 3.7 %shard_map.159 = f32[48,768]{1,0:T(8,128)} custom-call(s32[1]{0:T(128)} %bitcast.half_ref, f32[16,48,768]{2,1,0:T(8,128)} %copy-done, f32[16,48,768]{2,1,0:T(8,128)} %get-tuple-element.32.coef_ref), custom_call_target="tpu_custom_call" | custom-call | tf_op jit(solution)/shard_map/pallas_call | solution.py:511
  53.5 2.6 %collective-permute-start = (f32[48,768]{1,0:T(8,128)}, f32[48,768]{1,0:T(8,128)S(1)}, u32[]{:S(2)}, u32[]{:S(2)}) collective-permute-start(f32[48,768]{1,0:T(8,128)} %shard_map.159), channel_id=1, source_target_pairs={{0,16},{1,17},{2,18},{3,19},{4,20},{5,21},{6,22},{7,23},{8,24},{9,... | collective-permute-start | bytes 442376 | tf_op jit(solution)/shard_map/ppermute | solution.py:1045
  56.1 0.8 dynamic-slice_bitcast_fusion
  56.8 0.7 copy.17.row_ref
  57.5 1.3 constant_dynamic-slice_fusion.mine_ref
  58.8 4.2 %collective-permute-done.far_ref = f32[48,768]{1,0:T(8,128)S(1)} collective-permute-done((f32[48,768]{1,0:T(8,128)}, f32[48,768]{1,0:T(8,128)S(1)}, u32[]{:S(2)}, u32[]{:S(2)}) %collective-permute-start) | collective-permute-done | bytes 147488 | tf_op jit(solution)/shard_map/ppermute | solution.py:1045
  63.0 0.0 copy-start.3
  63.0 0.7 copy-done.3
  63.7 6.3 %shard_map.160 = (f32[16,48,384]{2,1,0:T(8,128)}, f32[16,48,384]{2,1,0:T(8,128)}, f32[192,128]{1,0:T(8,128)}) custom-call(s32[1]{0:T(128)} %bitcast.half_ref, f32[16,48,768]{2,1,0:T(8,128)} %copy-done, f32[16,48,768]{2,1,0:T(8,128)} %get-tuple-element.32.coef_ref, f32[48,768]{1,0:T(8,128)} %get-tuple-element.33.join_ref, f32[48,768]{1,0:T(8,128)} %copy-done.3, ...), custom_call_target="tpu_custom_call" | custom-call | tf_op jit(solution)/shard_map/pallas_call | solution.py:734
  70.0 0.0 collective-permute-start.1
  70.0 1.5 collective-permute-done.1
  71.5 0.9 add.47
  72.4 10.6 %all-gather = f32[384,128]{1,0:T(8,128)S(1)} all-gather(f32[96,128]{1,0:T(8,128)S(1)} %slice_select_fusion), channel_id=2, replica_groups={{0,2,4,6},{1,3,5,7},{8,10,12,14},{9,11,13,15},{16,18,20,22},{17,19,21,2..., dimensions={0}, use_global_device_ids=true | all-gather | bytes 245760 | tf_op jit(solution)/shard_map/all_gather | solution.py:1066
  83.0 0.4 collective-permute-start.2
  83.3 3.8 %collective-permute-done.2 = f32[96,128]{1,0:T(8,128)S(1)} collective-permute-done((f32[96,128]{1,0:T(8,128)S(1)}, f32[96,128]{1,0:T(8,128)S(1)}, u32[]{:S(2)}, u32[]{:S(2)}) %collective-permute-start.2) | collective-permute-done | bytes 49184 | tf_op jit(solution)/shard_map/ppermute | solution.py:1001
  87.1 1.6 %collective-permute-start.3 = (f32[96,128]{1,0:T(8,128)S(1)}, f32[96,128]{1,0:T(8,128)S(1)}, u32[]{:S(2)}, u32[]{:S(2)}) collective-permute-start(f32[96,128]{1,0:T(8,128)S(1)} %add.48), channel_id=1, source_target_pairs={{0,16},{8,24},{16,0},{24,8},{1,17},{9,25},{17,1},{25,9},{2,18},{10... | collective-permute-start | bytes 147464 | tf_op jit(solution)/shard_map/ppermute | solution.py:1001
  88.7 4.0 %collective-permute-done.3 = f32[96,128]{1,0:T(8,128)S(1)} collective-permute-done((f32[96,128]{1,0:T(8,128)S(1)}, f32[96,128]{1,0:T(8,128)S(1)}, u32[]{:S(2)}, u32[]{:S(2)}) %collective-permute-start.3) | collective-permute-done | bytes 49184 | tf_op jit(solution)/shard_map/ppermute | solution.py:1001
  92.7 0.1 collective-permute-start.4
  92.8 1.3 collective-permute-done.4
  94.1 0.6 pad_maximum_fusion.2.other_ref
  94.8 0.6 pad_maximum_fusion.1.own_ref
  95.4 3.7 %all-to-all-start.1 = ((f32[16,48,384]{2,1,0:T(8,128)}), f32[16,48,384]{2,1,0:T(8,128)S(1)}, u32[]{:S(2)}, u32[]{:S(2)}) async-start(f32[16,48,384]{2,1,0:T(8,128)} %get-tuple-element.36), calls=%async_computation.1 | async-start | bytes 2359296 | tf_op jit(solution)/shard_map/all_to_all | solution.py:996
  99.1 11.3 %shard_map.161 = (f32[2,128,128]{2,1,0:T(8,128)}, f32[2,64,128]{2,1,0:T(8,128)}) custom-call(f32[192,128]{1,0:T(8,128)} %pad_maximum_fusion.1.own_ref, f32[192,128]{1,0:T(8,128)} %pad_maximum_fusion.2.other_ref, f32[256,128]{1,0:T(8,128)} %constant.90.clone.basis_ref, f32[2,256,256]{2,1,0:T(8,128)} %constant.91.clone.face_ref, ...), custom_call_target="tpu_custom_call" | custom-call | flops 5000000000 | bytes 8388608 | tf_op jit(solution)/shard_map/pallas_call | solution.py:400
  110.5 4.2 %shard_map.162 = f32[16,48,384]{2,1,0:T(8,128)} custom-call(s32[1]{0:T(128)} %bitcast.half_ref, f32[16,48,384]{2,1,0:T(8,128)} %get-tuple-element.37.u_ref, f32[16,48,768]{2,1,0:T(8,128)} %get-tuple-element.32.coef_ref, f32[48,768]{1,0:T(8,128)} %get-tuple-element.33.join_ref, f32[48,1]{1,0:T(8,128)} %copy.17.row_ref, f32[1,768]{1,0:T(1,128)} %constant.106.col_ref, ...), custom_call_target="tpu_custom_call" | custom-call | flops 11796480 | bytes 3538944 | tf_op jit(solution)/shard_map/pallas_call | solution.py:630
  114.7 2.1 %all-to-all-done.1 = f32[16,48,384]{2,1,0:T(8,128)S(1)} async-done(((f32[16,48,384]{2,1,0:T(8,128)}), f32[16,48,384]{2,1,0:T(8,128)S(1)}, u32[]{:S(2)}, u32[]{:S(2)}) %all-to-all-start.1) | async-done | bytes 1179680 | tf_op jit(solution)/shard_map/all_to_all | solution.py:996
  116.7 0.0 copy-start.1
  116.7 1.0 copy-done.1
  117.8 3.9 %all-to-all-start.2 = ((f32[16,48,384]{2,1,0:T(8,128)}), f32[16,48,384]{2,1,0:T(8,128)S(1)}, u32[]{:S(2)}, u32[]{:S(2)}) async-start(f32[16,48,384]{2,1,0:T(8,128)} %shard_map.162), calls=%async_computation.2 | async-start | bytes 2359296 | tf_op jit(solution)/shard_map/all_to_all | solution.py:996
  121.7 20.7 %shard_map.163.refs_1_ = f32[384,768]{1,0:T(8,128)} custom-call(s32[1]{0:T(128)} %bitcast.3.place_ref, f32[384,768]{1,0:T(8,128)} %get-tuple-element.46.low_ref, f32[384,768]{1,0:T(8,128)} %get-tuple-element.47.high_ref, f32[384,1]{1,0:T(8,128)} %constant.104.row_ref.row_eigen_ref, f32[1,768]{1,0:T(1,128)} %constant.105.col_ref.col_eigen_ref, ...), custom_call_target="tpu_custom_call" | custom-call | flops 188743680 | bytes 7077888 | tf_op jit(solution)/shard_map/pallas_call | solution.py:940
  142.4 0.0 all-to-all-done.2
  142.4 0.0 copy-start.2
  142.4 1.0 copy-done.2
  143.5 10.0 %shard_map.164 = f32[768,768]{1,0:T(8,128)} custom-call(bf16[768,768]{1,0:T(8,128)(2,1)} %constant.87.clone.high_ref, bf16[768,768]{1,0:T(8,128)(2,1)} %constant.88.clone.low_ref, f32[768,384]{1,0:T(8,128)} %bitcast.11, f32[384,768]{1,0:T(8,128)} %shard_map.163.refs_1_, f32[768,384]{1,0:T(8,128)} %bitcast.12), custom_call_target="tpu_custom_call" | custom-call | tf_op jit(solution)/shard_map/pallas_call | solution.py:107
  (6 shorter events, 0.1 us)
Async XLA Ops:
  9.5 6.5 %copy-start.4 = (f32[768]{0:T(1024)S(1)}, f32[768]{0:T(1024)}, u32[]{:S(2)}) copy-start(f32[768]{0:T(1024)} %constant.98.clone) | copy-start | bytes 9220
  9.5 38.8 %all-to-all-start = ((f32[16,48,768]{2,1,0:T(8,128)}), f32[16,48,768]{2,1,0:T(8,128)S(1)}, u32[]{:S(2)}, u32[]{:S(2)}) async-start(f32[16,48,768]{2,1,0:T(8,128)} %bitcast.10), calls=%async_computation | async-start | bytes 4718592 | tf_op jit(solution)/shard_map/all_to_all | solution.py:996
  48.4 1.4 copy-start
  53.5 9.6 %collective-permute-start = (f32[48,768]{1,0:T(8,128)}, f32[48,768]{1,0:T(8,128)S(1)}, u32[]{:S(2)}, u32[]{:S(2)}) collective-permute-start(f32[48,768]{1,0:T(8,128)} %shard_map.159), channel_id=1, source_target_pairs={{0,16},{1,17},{2,18},{3,19},{4,20},{5,21},{6,22},{7,23},{8,24},{9,... | collective-permute-start | bytes 442376 | tf_op jit(solution)/shard_map/ppermute | solution.py:1045
  63.0 0.7 copy-start.3
  70.0 1.5 collective-permute-start.1
  83.0 4.2 %collective-permute-start.2 = (f32[96,128]{1,0:T(8,128)S(1)}, f32[96,128]{1,0:T(8,128)S(1)}, u32[]{:S(2)}, u32[]{:S(2)}) collective-permute-start(f32[96,128]{1,0:T(8,128)S(1)} %reduce_sum.9), channel_id=1, source_target_pairs={{0,8},{8,0},{16,24},{24,16},{1,9},{9,1},{17,25},{25,17},{2,10},{10... | collective-permute-start | bytes 147464 | tf_op jit(solution)/shard_map/ppermute | solution.py:1001
  87.1 5.6 %collective-permute-start.3 = (f32[96,128]{1,0:T(8,128)S(1)}, f32[96,128]{1,0:T(8,128)S(1)}, u32[]{:S(2)}, u32[]{:S(2)}) collective-permute-start(f32[96,128]{1,0:T(8,128)S(1)} %add.48), channel_id=1, source_target_pairs={{0,16},{8,24},{16,0},{24,8},{1,17},{9,25},{17,1},{25,9},{2,18},{10... | collective-permute-start | bytes 147464 | tf_op jit(solution)/shard_map/ppermute | solution.py:1001
  92.7 1.4 collective-permute-start.4
  95.4 21.3 %all-to-all-start.1 = ((f32[16,48,384]{2,1,0:T(8,128)}), f32[16,48,384]{2,1,0:T(8,128)S(1)}, u32[]{:S(2)}, u32[]{:S(2)}) async-start(f32[16,48,384]{2,1,0:T(8,128)} %get-tuple-element.36), calls=%async_computation.1 | async-start | bytes 2359296 | tf_op jit(solution)/shard_map/all_to_all | solution.py:996
  116.7 1.0 copy-start.1
  117.8 24.6 %all-to-all-start.2 = ((f32[16,48,384]{2,1,0:T(8,128)}), f32[16,48,384]{2,1,0:T(8,128)S(1)}, u32[]{:S(2)}, u32[]{:S(2)}) async-start(f32[16,48,384]{2,1,0:T(8,128)} %shard_map.162), calls=%async_computation.2 | async-start | bytes 2359296 | tf_op jit(solution)/shard_map/all_to_all | solution.py:996
  142.4 1.0 copy-start.2

commit v6 on v5

--- a/solution.py
+++ b/solution.py
@@ -283,7 +283,7 @@
 
 
 def panels_body(
-    own_ref, other_ref, basis_ref, face_ref, side_ref, level_ref, cross_ref, turn_ref,
+    first_ref, mine_ref, mate_ref, basis_ref, face_ref, side_ref, level_ref, cross_ref, turn_ref,
     mixed_hbm, front_hbm, back_hbm, face_out_ref, side_out_ref,
     fx_ref, hat_ref, acc_ref, toside_ref, xs_ref, tox_ref, mixed_ref, front_ref, back_ref, sems,
 ):
@@ -297,8 +297,14 @@
     for load in loads:
         load.start()
     hb = PANELS // 2
-    total = (own_ref[...] + other_ref[...]) * 0.5
-    gap = (own_ref[...] - other_ref[...]) * 0.5
+    first = first_ref[0] == 1
+    low = jnp.where(first, mine_ref[...], mate_ref[...])
+    high = jnp.where(first, mate_ref[...], mine_ref[...])
+    middle = low.shape[0] // 2
+    own = jnp.concatenate([low[:middle], high[:middle]], 0)
+    other = jnp.concatenate([low[middle:], high[middle:]], 0)
+    total = (own + other) * 0.5
+    gap = (own - other) * 0.5
     basis = basis_ref[...]
     level = level_ref[...]
     faces = [total[:PANELS], gap[:PANELS]]
@@ -392,14 +398,16 @@
     face_out_ref[1] = value[0] - value[1]
 
 
-def panel_potential(own, other, tb, mixed, corner):
+def panel_potential(first, mine, mate, tb, mixed, corner):
     half = mixed.shape[1]
     width = corner[0].shape[2]
     f32 = jnp.float32
     vmem = pl.BlockSpec(memory_space=pltpu.VMEM)
     return pl.pallas_call(
         panels_body,
-        in_specs=[vmem] * 8 + [pl.BlockSpec(memory_space=pl.ANY)] * 3,
+        in_specs=[pl.BlockSpec(memory_space=pltpu.SMEM)]
+        + [vmem] * 8
+        + [pl.BlockSpec(memory_space=pl.ANY)] * 3,
         out_shape=[
             jax.ShapeDtypeStruct((2, PANELS, PANELS), f32),
             jax.ShapeDtypeStruct((2, 4 * half, PANELS), f32),
@@ -421,7 +429,7 @@
             transcendentals=0,
         ),
     )(
-        own, other, tb["basis"], tb["face"], tb["side"], tb["level"], tb["cross"], tb["turn"],
+        first, mine, mate, tb["basis"], tb["face"], tb["side"], tb["level"], tb["cross"], tb["turn"],
         mixed, *corner,
     )
 
@@ -1068,15 +1076,15 @@
         while bit < slow // 2:
             part = part + hop(part, bit)
             bit *= 2
-        both = jnp.concatenate([part, hop(part, bit)])
-        back = swap(both)
-        low, high = jnp.where(first, both, back), jnp.where(first, back, both)
-        part = jnp.concatenate([low[:middle], high[:middle]])
-        other = jnp.concatenate([low[middle:], high[middle:]])
+        mine = jnp.concatenate([part, hop(part, bit)])
         if local:
-            early, part, other = lax.optimization_barrier((u, part, other))
+            early, mine = lax.optimization_barrier((u, mine))
+        mate = swap(mine)
+        if local:
             u = exchange(early).reshape(grid, split)
-        face_v, side_v = panel_potential(part, other, tb, mixed, corner)
+        face_v, side_v = panel_potential(
+            first.astype(jnp.int32).reshape(1), mine, mate, tb, mixed, corner
+        )
         if local:
             sent = add_late(
                 upper, sent, coef, join, my_edge[:, None], edge_value[None, :], face_v, side_v,

time: 154 us -> 153 us (level)
  waiting for transfers between devices: 21.8 us -> 19.6 us
    all_to_all x3, waiting for transfers between devices: 7.1 us -> 5.07 us  [exchange(): lax.all_to_all(x, AXES, split_axis=0, concat_axis=0, tiled=True, axis_ind...]
    unnamed x10 -> x14, local copies, waits for them, and re-layouts: 4.14 us -> 4.78 us
  transfers between devices with their start and end apart: 8 -> 8, of which waited for: 7 -> 6; matrix products, arithmetic and copies ran while one was open for 2% -> 2% of each run, Pallas kernels for 41% -> 41%
where the time goes in v6:
time: 153 us; the launch traced here: 152 us
  Pallas kernels  92.3 us (60%)
  starting transfers between devices  20.1 us (13%)
  waiting for transfers between devices  19.6 us (13%)
  blocking collectives  10.6 us (7%)
  local copies, waits for them, and re-layouts  7.65 us (5%)
  other arithmetic  1.67 us (1%)
    pallas_call x1, Pallas kernels, plane_layers(): pl.pallas_call(functools.partial(plane_body, depth), grid_spec=pltpu.Pref...  20.7 us
    pallas_call x2, Pallas kernels, double_product(): pl.pallas_call(functools.partial(product_body, len(values)), grid=(2 * st...  19.5 us
    all_to_all x3, starting transfers between devices, exchange(): lax.all_to_all(x, AXES, split_axis=0, concat_axis=0, tiled=True, axis_ind...  15.2 us
    pallas_call x1, Pallas kernels, panel_potential(): pl.pallas_call(panels_body, in_specs=[pl.BlockSpec(memory_space=pltpu.SME...  11.3 us
    all_gather x1, blocking collectives, on_device(): lax.all_gather(part, 'py', axis=0, tiled=False, axis_index_groups=alternate)  10.6 us
    pallas_call x1, Pallas kernels, weights(): pl.pallas_call(functools.partial(weight_body, depth), grid_spec=pltpu.Pre...  9.87 us
    ppermute x2, waiting for transfers between devices, hop(): return lax.ppermute(x, 'px', [(i, i ^ bit) for i in range(slow)])  7.78 us
    pallas_call x1, Pallas kernels, corner_table(): pl.pallas_call(functools.partial(corner_body, edge, depth), grid=(hb // S...  7.6 us
  transfers between devices with their start and end apart: 8, of which 6 were waited for; matrix products, arithmetic and copies ran while one was open for 2% of the time, Pallas kernels for 41%

profile of v6, /device:TPU:0, one launch (start us, length us, event | category | flops | bytes accessed | tf_op | source)
XLA Modules:
  0.0 151.9 jit_solution(2111059044619704009)
XLA Ops:
  0.0 9.5 %shard_map.154 = f32[768,768]{1,0:T(8,128)} custom-call(bf16[768,768]{1,0:T(8,128)(2,1)} %constant.87.clone.high_ref, bf16[768,768]{1,0:T(8,128)(2,1)} %constant.88.clone.low_ref, f32[768,768]{1,0:T(8,128)} %bitcast.14), custom_call_target="tpu_custom_call" | custom-call | tf_op jit(solution)/shard_map/pallas_call | solution.py:107
  9.5 0.0 copy-start.5
  9.5 6.5 %all-to-all-start = ((f32[16,48,768]{2,1,0:T(8,128)}), f32[16,48,768]{2,1,0:T(8,128)S(1)}, u32[]{:S(2)}, u32[]{:S(2)}) async-start(f32[16,48,768]{2,1,0:T(8,128)} %bitcast.11), calls=%async_computation | async-start | bytes 4718592 | tf_op jit(solution)/shard_map/all_to_all | solution.py:1004
  16.0 0.0 copy-done.5
  16.0 0.1 dynamic_slice.9
  16.1 0.7 broadcast_add_fusion.mu_ref
  16.8 3.1 %shard_map.158 = (f32[16,48,768]{2,1,0:T(8,128)}, f32[48,768]{1,0:T(8,128)}) custom-call(f32[48,768]{1,0:T(8,128)} %broadcast_add_fusion.mu_ref), custom_call_target="tpu_custom_call" | custom-call | flops 11796480 | bytes 2359296 | tf_op jit(solution)/shard_map/pallas_call | solution.py:462
  20.0 9.9 %shard_map.157 = (f32[384,768]{1,0:T(8,128)}, f32[384,768]{1,0:T(8,128)}) custom-call(s32[1]{0:T(128)} %bitcast.3.place_ref, f32[384,1]{1,0:T(8,128)} %constant.104.row_ref.row_eigen_ref, f32[1,768]{1,0:T(1,128)} %constant.105.col_ref.col_eigen_ref), custom_call_target="tpu_custom_call" | custom-call | flops 37748736 | bytes 2359296 | tf_op jit(solution)/shard_map/pallas_call | solution.py:832
  29.8 7.6 %shard_map.156 = (f32[64,64,128]{2,1,0:T(8,128)}, f32[64,64,128]{2,1,0:T(8,128)}) custom-call(f32[64,128]{1,0:T(8,128)} %constant.97.clone.wave_ref), custom_call_target="tpu_custom_call" | custom-call | flops 134217728 | bytes 2097152 | tf_op jit(solution)/shard_map/pallas_call | solution.py:217
  37.4 5.9 %shard_map.155.mixed_hbm = f32[2,16,128,256]{3,2,1,0:T(8,128)} custom-call(f32[128,256]{1,0:T(8,128)} %constant.96.clone.wave_ref), custom_call_target="tpu_custom_call" | custom-call | flops 134217728 | bytes 2097152 | tf_op jit(solution)/shard_map/pallas_call | solution.py:167
  43.3 5.0 %all-to-all-done.f_ref = f32[16,48,768]{2,1,0:T(8,128)S(1)} async-done(((f32[16,48,768]{2,1,0:T(8,128)}), f32[16,48,768]{2,1,0:T(8,128)S(1)}, u32[]{:S(2)}, u32[]{:S(2)}) %all-to-all-start) | async-done | bytes 2359328 | tf_op jit(solution)/shard_map/all_to_all | solution.py:1004
  48.4 0.0 copy-start
  48.4 1.4 copy-done
  49.8 3.7 %shard_map.159 = f32[48,768]{1,0:T(8,128)} custom-call(s32[1]{0:T(128)} %bitcast.half_ref, f32[16,48,768]{2,1,0:T(8,128)} %copy-done, f32[16,48,768]{2,1,0:T(8,128)} %get-tuple-element.31.coef_ref), custom_call_target="tpu_custom_call" | custom-call | tf_op jit(solution)/shard_map/pallas_call | solution.py:519
  53.5 2.6 %collective-permute-start = (f32[48,768]{1,0:T(8,128)}, f32[48,768]{1,0:T(8,128)S(1)}, u32[]{:S(2)}, u32[]{:S(2)}) collective-permute-start(f32[48,768]{1,0:T(8,128)} %shard_map.159), channel_id=1, source_target_pairs={{0,16},{1,17},{2,18},{3,19},{4,20},{5,21},{6,22},{7,23},{8,24},{9,... | collective-permute-start | bytes 442376 | tf_op jit(solution)/shard_map/ppermute | solution.py:1053
  56.1 0.8 dynamic-slice_bitcast_fusion
  56.8 0.7 copy.17.row_ref
  57.5 1.3 constant_dynamic-slice_fusion.mine_ref
  58.8 4.2 %collective-permute-done.far_ref = f32[48,768]{1,0:T(8,128)S(1)} collective-permute-done((f32[48,768]{1,0:T(8,128)}, f32[48,768]{1,0:T(8,128)S(1)}, u32[]{:S(2)}, u32[]{:S(2)}) %collective-permute-start) | collective-permute-done | bytes 147488 | tf_op jit(solution)/shard_map/ppermute | solution.py:1053
  63.0 0.0 copy-start.3
  63.0 0.7 copy-done.3
  63.7 6.3 %shard_map.160 = (f32[16,48,384]{2,1,0:T(8,128)}, f32[16,48,384]{2,1,0:T(8,128)}, f32[192,128]{1,0:T(8,128)}) custom-call(s32[1]{0:T(128)} %bitcast.half_ref, f32[16,48,768]{2,1,0:T(8,128)} %copy-done, f32[16,48,768]{2,1,0:T(8,128)} %get-tuple-element.31.coef_ref, f32[48,768]{1,0:T(8,128)} %get-tuple-element.32.join_ref, f32[48,768]{1,0:T(8,128)} %copy-done.3, ...), custom_call_target="tpu_custom_call" | custom-call | tf_op jit(solution)/shard_map/pallas_call | solution.py:742
  70.0 0.0 collective-permute-start.1
  70.0 1.5 collective-permute-done.1
  71.5 0.9 add.47
  72.4 10.6 %all-gather = f32[384,128]{1,0:T(8,128)S(1)} all-gather(f32[96,128]{1,0:T(8,128)S(1)} %slice_select_fusion), channel_id=2, replica_groups={{0,2,4,6},{1,3,5,7},{8,10,12,14},{9,11,13,15},{16,18,20,22},{17,19,21,2..., dimensions={0}, use_global_device_ids=true | all-gather | bytes 245760 | tf_op jit(solution)/shard_map/all_gather | solution.py:1074
  83.0 0.4 collective-permute-start.2
  83.3 3.8 %collective-permute-done.2 = f32[96,128]{1,0:T(8,128)S(1)} collective-permute-done((f32[96,128]{1,0:T(8,128)S(1)}, f32[96,128]{1,0:T(8,128)S(1)}, u32[]{:S(2)}, u32[]{:S(2)}) %collective-permute-start.2) | collective-permute-done | bytes 49184 | tf_op jit(solution)/shard_map/ppermute | solution.py:1009
  87.1 1.6 %collective-permute-start.3 = (f32[96,128]{1,0:T(8,128)S(1)}, f32[96,128]{1,0:T(8,128)S(1)}, u32[]{:S(2)}, u32[]{:S(2)}) collective-permute-start(f32[96,128]{1,0:T(8,128)S(1)} %add.48), channel_id=1, source_target_pairs={{0,16},{8,24},{16,0},{24,8},{1,17},{9,25},{17,1},{25,9},{2,18},{10... | collective-permute-start | bytes 147464 | tf_op jit(solution)/shard_map/ppermute | solution.py:1009
  88.7 4.0 %collective-permute-done.3 = f32[96,128]{1,0:T(8,128)S(1)} collective-permute-done((f32[96,128]{1,0:T(8,128)S(1)}, f32[96,128]{1,0:T(8,128)S(1)}, u32[]{:S(2)}, u32[]{:S(2)}) %collective-permute-start.3) | collective-permute-done | bytes 49184 | tf_op jit(solution)/shard_map/ppermute | solution.py:1009
  92.7 0.0 copy-start.4
  92.7 3.7 %all-to-all-start.1 = ((f32[16,48,384]{2,1,0:T(8,128)}), f32[16,48,384]{2,1,0:T(8,128)S(1)}, u32[]{:S(2)}, u32[]{:S(2)}) async-start(f32[16,48,384]{2,1,0:T(8,128)} %get-tuple-element.35), calls=%async_computation.1 | async-start | bytes 2359296 | tf_op jit(solution)/shard_map/all_to_all | solution.py:1004
  96.5 0.0 copy-done.4
  96.5 0.4 collective-permute-start.4
  96.8 1.0 collective-permute-done.4.mate_ref
  97.9 0.0 copy-start.6
  97.9 0.6 copy-done.6
  98.5 11.3 %shard_map.161 = (f32[2,128,128]{2,1,0:T(8,128)}, f32[2,64,128]{2,1,0:T(8,128)}) custom-call(s32[1]{0:T(128)} %bitcast.7.first_ref, f32[192,128]{1,0:T(8,128)} %copy-done.4, f32[192,128]{1,0:T(8,128)} %copy-done.6, f32[256,128]{1,0:T(8,128)} %constant.90.clone.basis_ref, f32[2,256,256]{2,1,0:T(8,128)} %constant.91.clone.face_ref, ...), custom_call_target="tpu_custom_call" | custom-call | flops 5000000000 | bytes 8388608 | tf_op jit(solution)/shard_map/pallas_call | solution.py:406
  109.8 4.2 %shard_map.162 = f32[16,48,384]{2,1,0:T(8,128)} custom-call(s32[1]{0:T(128)} %bitcast.half_ref, f32[16,48,384]{2,1,0:T(8,128)} %get-tuple-element.36.u_ref, f32[16,48,768]{2,1,0:T(8,128)} %get-tuple-element.31.coef_ref, f32[48,768]{1,0:T(8,128)} %get-tuple-element.32.join_ref, f32[48,1]{1,0:T(8,128)} %copy.17.row_ref, f32[1,768]{1,0:T(1,128)} %constant.106.col_ref, ...), custom_call_target="tpu_custom_call" | custom-call | flops 11796480 | bytes 3538944 | tf_op jit(solution)/shard_map/pallas_call | solution.py:638
  114.0 0.0 all-to-all-done.1
  114.0 0.0 copy-start.1
  114.0 1.0 copy-done.1
  115.1 5.0 %all-to-all-start.2 = ((f32[16,48,384]{2,1,0:T(8,128)}), f32[16,48,384]{2,1,0:T(8,128)S(1)}, u32[]{:S(2)}, u32[]{:S(2)}) async-start(f32[16,48,384]{2,1,0:T(8,128)} %shard_map.162), calls=%async_computation.2 | async-start | bytes 2359296 | tf_op jit(solution)/shard_map/all_to_all | solution.py:1004
  120.1 20.7 %shard_map.163.refs_1_ = f32[384,768]{1,0:T(8,128)} custom-call(s32[1]{0:T(128)} %bitcast.3.place_ref, f32[384,768]{1,0:T(8,128)} %get-tuple-element.44.low_ref, f32[384,768]{1,0:T(8,128)} %get-tuple-element.45.high_ref, f32[384,1]{1,0:T(8,128)} %constant.104.row_ref.row_eigen_ref, f32[1,768]{1,0:T(1,128)} %constant.105.col_ref.col_eigen_ref, ...), custom_call_target="tpu_custom_call" | custom-call | flops 188743680 | bytes 7077888 | tf_op jit(solution)/shard_map/pallas_call | solution.py:948
  140.9 0.0 all-to-all-done.2
  140.9 0.0 copy-start.2
  140.9 1.0 copy-done.2
  141.9 10.0 %shard_map.164 = f32[768,768]{1,0:T(8,128)} custom-call(bf16[768,768]{1,0:T(8,128)(2,1)} %constant.87.clone.high_ref, bf16[768,768]{1,0:T(8,128)(2,1)} %constant.88.clone.low_ref, f32[768,384]{1,0:T(8,128)} %bitcast.12, f32[384,768]{1,0:T(8,128)} %shard_map.163.refs_1_, f32[768,384]{1,0:T(8,128)} %bitcast.13), custom_call_target="tpu_custom_call" | custom-call | tf_op jit(solution)/shard_map/pallas_call | solution.py:107
  (4 shorter events, 0.0 us)
Async XLA Ops:
  9.5 6.5 %copy-start.5 = (f32[768]{0:T(1024)S(1)}, f32[768]{0:T(1024)}, u32[]{:S(2)}) copy-start(f32[768]{0:T(1024)} %constant.98.clone) | copy-start | bytes 9220
  9.5 38.8 %all-to-all-start = ((f32[16,48,768]{2,1,0:T(8,128)}), f32[16,48,768]{2,1,0:T(8,128)S(1)}, u32[]{:S(2)}, u32[]{:S(2)}) async-start(f32[16,48,768]{2,1,0:T(8,128)} %bitcast.11), calls=%async_computation | async-start | bytes 4718592 | tf_op jit(solution)/shard_map/all_to_all | solution.py:1004
  48.4 1.4 copy-start
  53.5 9.6 %collective-permute-start = (f32[48,768]{1,0:T(8,128)}, f32[48,768]{1,0:T(8,128)S(1)}, u32[]{:S(2)}, u32[]{:S(2)}) collective-permute-start(f32[48,768]{1,0:T(8,128)} %shard_map.159), channel_id=1, source_target_pairs={{0,16},{1,17},{2,18},{3,19},{4,20},{5,21},{6,22},{7,23},{8,24},{9,... | collective-permute-start | bytes 442376 | tf_op jit(solution)/shard_map/ppermute | solution.py:1053
  63.0 0.7 copy-start.3
  70.0 1.5 collective-permute-start.1
  83.0 4.2 %collective-permute-start.2 = (f32[96,128]{1,0:T(8,128)S(1)}, f32[96,128]{1,0:T(8,128)S(1)}, u32[]{:S(2)}, u32[]{:S(2)}) collective-permute-start(f32[96,128]{1,0:T(8,128)S(1)} %reduce_sum.9), channel_id=1, source_target_pairs={{0,8},{8,0},{16,24},{24,16},{1,9},{9,1},{17,25},{25,17},{2,10},{10... | collective-permute-start | bytes 147464 | tf_op jit(solution)/shard_map/ppermute | solution.py:1009
  87.1 5.6 %collective-permute-start.3 = (f32[96,128]{1,0:T(8,128)S(1)}, f32[96,128]{1,0:T(8,128)S(1)}, u32[]{:S(2)}, u32[]{:S(2)}) collective-permute-start(f32[96,128]{1,0:T(8,128)S(1)} %add.48), channel_id=1, source_target_pairs={{0,16},{8,24},{16,0},{24,8},{1,17},{9,25},{17,1},{25,9},{2,18},{10... | collective-permute-start | bytes 147464 | tf_op jit(solution)/shard_map/ppermute | solution.py:1009
  92.7 3.7 %copy-start.4 = (f32[192,128]{1,0:T(8,128)}, f32[192,128]{1,0:T(8,128)S(1)}, u32[]{:S(2)}) copy-start(f32[192,128]{1,0:T(8,128)S(1)} %pad_maximum_fusion.mine_ref) | copy-start | bytes 294916
  92.7 21.3 %all-to-all-start.1 = ((f32[16,48,384]{2,1,0:T(8,128)}), f32[16,48,384]{2,1,0:T(8,128)S(1)}, u32[]{:S(2)}, u32[]{:S(2)}) async-start(f32[16,48,384]{2,1,0:T(8,128)} %get-tuple-element.35), calls=%async_computation.1 | async-start | bytes 2359296 | tf_op jit(solution)/shard_map/all_to_all | solution.py:1004
  96.5 1.4 collective-permute-start.4
  97.9 0.6 copy-start.6
  114.0 1.0 copy-start.1
  115.1 25.8 %all-to-all-start.2 = ((f32[16,48,384]{2,1,0:T(8,128)}), f32[16,48,384]{2,1,0:T(8,128)S(1)}, u32[]{:S(2)}, u32[]{:S(2)}) async-start(f32[16,48,384]{2,1,0:T(8,128)} %shard_map.162), calls=%async_computation.2 | async-start | bytes 2359296 | tf_op jit(solution)/shard_map/all_to_all | solution.py:1004
  140.9 1.0 copy-start.2

commit v7 on v6

--- a/solution.py
+++ b/solution.py
@@ -503,29 +503,28 @@
     )(upper, spectrum, coef)
 
 
-def reach_body(half_ref, f_ref, coef_ref, last_ref):
-    planes = f_ref.shape[0]
+def reach_body(half_ref, f_ref, mu_ref, last_ref):
+    planes, _, cols = f_ref.shape
     upper = half_ref[0]
-    value = jnp.zeros_like(last_ref)
-    for j in range(planes):
-        place = jnp.where(upper == 1, planes - 1 - j, j)
-        value = (f_ref[place] + value) * coef_ref[j]
-    last_ref[...] = value
-
-
-def reach(upper, spectrum, coef):
-    planes, rows, cols = spectrum.shape
-    block, flat = block_specs(planes, rows)
+    for at in range(0, cols, WIDTH):
+        part = slice(at, at + WIDTH)
+        diag = mu_ref[:, part] + 2.0
+        coef = 1.0 / diag
+        value = f_ref[jnp.where(upper == 1, planes - 1, 0), :, part] * coef
+        for j in range(1, planes):
+            coef = 1.0 / (diag - coef)
+            value = (f_ref[jnp.where(upper == 1, planes - 1 - j, j), :, part] + value) * coef
+        last_ref[:, part] = value
+
+
+def reach(upper, spectrum, mu):
+    vmem = pl.BlockSpec(memory_space=pltpu.VMEM)
     return pl.pallas_call(
         reach_body,
-        grid_spec=pltpu.PrefetchScalarGridSpec(
-            num_scalar_prefetch=1,
-            grid=(cols // WIDTH,),
-            in_specs=[block, block],
-            out_specs=flat,
-        ),
-        out_shape=jax.ShapeDtypeStruct((rows, cols), jnp.float32),
-    )(upper, spectrum, coef)
+        in_specs=[pl.BlockSpec(memory_space=pltpu.SMEM), vmem, vmem],
+        out_specs=vmem,
+        out_shape=jax.ShapeDtypeStruct(mu.shape, jnp.float32),
+    )(upper, spectrum, mu)
 
 
 def finish_body(half_ref, g_ref, coef_ref, join_ref, far_ref, u_ref, edge_ref):
@@ -1047,7 +1046,7 @@
         else:
             spectrum, mixed, corner = lax.optimization_barrier((spectrum, mixed, corner))
         if local:
-            last = reach(upper, spectrum, coef)
+            last = reach(upper, spectrum, mu)
         else:
             g, last = sweep(upper, spectrum, coef)
         far = lax.ppermute(last, AXES, [(i, i ^ half) for i in range(devices)])

time: 153 us -> 152 us (level)
    ppermute x1, waiting for transfers between devices: 4.18 us -> 1.07 us  [on_device(): far = lax.ppermute(last, AXES, [(i, i ^ half) for i in range(devices)])]
    all_to_all x3, waiting for transfers between devices: 5.07 us -> 8.17 us  [exchange(): lax.all_to_all(x, AXES, split_axis=0, concat_axis=0, tiled=True, axis_ind...]
  transfers between devices with their start and end apart: 8 -> 8, of which waited for: 6 -> 6; matrix products, arithmetic and copies ran while one was open for 2% -> 2% of each run, Pallas kernels for 41% -> 42%
where the time goes in v7:
time: 152 us; the launch traced here: 151 us
  Pallas kernels  91.3 us (60%)
  starting transfers between devices  20.1 us (13%)
  waiting for transfers between devices  19.5 us (13%)
  blocking collectives  10.6 us (7%)
  local copies, waits for them, and re-layouts  7.65 us (5%)
  other arithmetic  1.68 us (1%)
    pallas_call x1, Pallas kernels, plane_layers(): pl.pallas_call(functools.partial(plane_body, depth), grid_spec=pltpu.Pref...  20.8 us
    pallas_call x2, Pallas kernels, double_product(): pl.pallas_call(functools.partial(product_body, len(values)), grid=(2 * st...  19.5 us
    all_to_all x3, starting transfers between devices, exchange(): lax.all_to_all(x, AXES, split_axis=0, concat_axis=0, tiled=True, axis_ind...  15.2 us
    pallas_call x1, Pallas kernels, panel_potential(): pl.pallas_call(panels_body, in_specs=[pl.BlockSpec(memory_space=pltpu.SME...  11.3 us
    all_gather x1, blocking collectives, on_device(): lax.all_gather(part, 'py', axis=0, tiled=False, axis_index_groups=alternate)  10.6 us
    pallas_call x1, Pallas kernels, weights(): pl.pallas_call(functools.partial(weight_body, depth), grid_spec=pltpu.Pre...  9.87 us
    all_to_all x3, waiting for transfers between devices, exchange(): lax.all_to_all(x, AXES, split_axis=0, concat_axis=0, tiled=True, axis_ind...  8.17 us
    ppermute x2, waiting for transfers between devices, hop(): return lax.ppermute(x, 'px', [(i, i ^ bit) for i in range(slow)])  7.78 us
  transfers between devices with their start and end apart: 8, of which 6 were waited for; matrix products, arithmetic and copies ran while one was open for 2% of the time, Pallas kernels for 42%

profile of v7, /device:TPU:0, one launch (start us, length us, event | category | flops | bytes accessed | tf_op | source)
XLA Modules:
  0.0 150.9 jit_solution(15414996757239317529)
XLA Ops:
  0.0 9.5 %shard_map.154 = f32[768,768]{1,0:T(8,128)} custom-call(bf16[768,768]{1,0:T(8,128)(2,1)} %constant.87.clone.high_ref, bf16[768,768]{1,0:T(8,128)(2,1)} %constant.88.clone.low_ref, f32[768,768]{1,0:T(8,128)} %bitcast.14), custom_call_target="tpu_custom_call" | custom-call | tf_op jit(solution)/shard_map/pallas_call | solution.py:107
  9.5 0.0 copy-start.5
  9.5 6.5 %all-to-all-start = ((f32[16,48,768]{2,1,0:T(8,128)}), f32[16,48,768]{2,1,0:T(8,128)S(1)}, u32[]{:S(2)}, u32[]{:S(2)}) async-start(f32[16,48,768]{2,1,0:T(8,128)} %bitcast.11), calls=%async_computation | async-start | bytes 4718592 | tf_op jit(solution)/shard_map/all_to_all | solution.py:1003
  16.0 0.0 copy-done.5
  16.0 0.1 dynamic_slice.9
  16.1 9.9 %shard_map.157 = (f32[384,768]{1,0:T(8,128)}, f32[384,768]{1,0:T(8,128)}) custom-call(s32[1]{0:T(128)} %bitcast.3.place_ref, f32[384,1]{1,0:T(8,128)} %constant.104.row_ref.row_eigen_ref, f32[1,768]{1,0:T(1,128)} %constant.105.col_ref.col_eigen_ref), custom_call_target="tpu_custom_call" | custom-call | flops 37748736 | bytes 2359296 | tf_op jit(solution)/shard_map/pallas_call | solution.py:831
  26.0 7.6 %shard_map.156 = (f32[64,64,128]{2,1,0:T(8,128)}, f32[64,64,128]{2,1,0:T(8,128)}) custom-call(f32[64,128]{1,0:T(8,128)} %constant.97.clone.wave_ref), custom_call_target="tpu_custom_call" | custom-call | flops 134217728 | bytes 2097152 | tf_op jit(solution)/shard_map/pallas_call | solution.py:217
  33.6 5.9 %shard_map.155.mixed_hbm = f32[2,16,128,256]{3,2,1,0:T(8,128)} custom-call(f32[128,256]{1,0:T(8,128)} %constant.96.clone.wave_ref), custom_call_target="tpu_custom_call" | custom-call | flops 134217728 | bytes 2097152 | tf_op jit(solution)/shard_map/pallas_call | solution.py:167
  39.5 0.7 broadcast_add_fusion.mu_ref
  40.2 8.1 %all-to-all-done.f_ref = f32[16,48,768]{2,1,0:T(8,128)S(1)} async-done(((f32[16,48,768]{2,1,0:T(8,128)}), f32[16,48,768]{2,1,0:T(8,128)S(1)}, u32[]{:S(2)}, u32[]{:S(2)}) %all-to-all-start) | async-done | bytes 2359328 | tf_op jit(solution)/shard_map/all_to_all | solution.py:1003
  48.4 0.0 copy-start
  48.4 1.4 copy-done
  49.8 2.7 %shard_map.159 = f32[48,768]{1,0:T(8,128)} custom-call(s32[1]{0:T(128)} %bitcast.half_ref, f32[16,48,768]{2,1,0:T(8,128)} %copy-done, f32[48,768]{1,0:T(8,128)} %broadcast_add_fusion.mu_ref), custom_call_target="tpu_custom_call" | custom-call | tf_op jit(solution)/shard_map/pallas_call | solution.py:522
  52.5 2.6 %collective-permute-start = (f32[48,768]{1,0:T(8,128)}, f32[48,768]{1,0:T(8,128)S(1)}, u32[]{:S(2)}, u32[]{:S(2)}) collective-permute-start(f32[48,768]{1,0:T(8,128)} %shard_map.159), channel_id=1, source_target_pairs={{0,16},{1,17},{2,18},{3,19},{4,20},{5,21},{6,22},{7,23},{8,24},{9,... | collective-permute-start | bytes 442376 | tf_op jit(solution)/shard_map/ppermute | solution.py:1052
  55.0 0.8 dynamic-slice_bitcast_fusion
  55.8 0.7 copy.17.row_ref
  56.5 3.1 %shard_map.158 = (f32[16,48,768]{2,1,0:T(8,128)}, f32[48,768]{1,0:T(8,128)}) custom-call(f32[48,768]{1,0:T(8,128)} %broadcast_add_fusion.mu_ref), custom_call_target="tpu_custom_call" | custom-call | flops 11796480 | bytes 2359296 | tf_op jit(solution)/shard_map/pallas_call | solution.py:462
  59.6 1.3 constant_dynamic-slice_fusion.mine_ref
  61.0 1.1 collective-permute-done.far_ref
  62.0 0.0 copy-start.3
  62.0 0.7 copy-done.3
  62.7 6.3 %shard_map.160 = (f32[16,48,384]{2,1,0:T(8,128)}, f32[16,48,384]{2,1,0:T(8,128)}, f32[192,128]{1,0:T(8,128)}) custom-call(s32[1]{0:T(128)} %bitcast.half_ref, f32[16,48,768]{2,1,0:T(8,128)} %copy-done, f32[16,48,768]{2,1,0:T(8,128)} %get-tuple-element.31.coef_ref, f32[48,768]{1,0:T(8,128)} %get-tuple-element.32.join_ref, f32[48,768]{1,0:T(8,128)} %copy-done.3, ...), custom_call_target="tpu_custom_call" | custom-call | tf_op jit(solution)/shard_map/pallas_call | solution.py:741
  68.9 0.0 collective-permute-start.1
  69.0 1.5 collective-permute-done.1
  70.5 0.9 add.47
  71.4 10.6 %all-gather = f32[384,128]{1,0:T(8,128)S(1)} all-gather(f32[96,128]{1,0:T(8,128)S(1)} %slice_select_fusion), channel_id=2, replica_groups={{0,2,4,6},{1,3,5,7},{8,10,12,14},{9,11,13,15},{16,18,20,22},{17,19,21,2..., dimensions={0}, use_global_device_ids=true | all-gather | bytes 245760 | tf_op jit(solution)/shard_map/all_gather | solution.py:1073
  82.0 0.4 collective-permute-start.2
  82.3 3.8 %collective-permute-done.2 = f32[96,128]{1,0:T(8,128)S(1)} collective-permute-done((f32[96,128]{1,0:T(8,128)S(1)}, f32[96,128]{1,0:T(8,128)S(1)}, u32[]{:S(2)}, u32[]{:S(2)}) %collective-permute-start.2) | collective-permute-done | bytes 49184 | tf_op jit(solution)/shard_map/ppermute | solution.py:1008
  86.1 1.6 %collective-permute-start.3 = (f32[96,128]{1,0:T(8,128)S(1)}, f32[96,128]{1,0:T(8,128)S(1)}, u32[]{:S(2)}, u32[]{:S(2)}) collective-permute-start(f32[96,128]{1,0:T(8,128)S(1)} %add.48), channel_id=1, source_target_pairs={{0,16},{8,24},{16,0},{24,8},{1,17},{9,25},{17,1},{25,9},{2,18},{10... | collective-permute-start | bytes 147464 | tf_op jit(solution)/shard_map/ppermute | solution.py:1008
  87.7 4.0 %collective-permute-done.3 = f32[96,128]{1,0:T(8,128)S(1)} collective-permute-done((f32[96,128]{1,0:T(8,128)S(1)}, f32[96,128]{1,0:T(8,128)S(1)}, u32[]{:S(2)}, u32[]{:S(2)}) %collective-permute-start.3) | collective-permute-done | bytes 49184 | tf_op jit(solution)/shard_map/ppermute | solution.py:1008
  91.7 0.0 copy-start.4
  91.7 3.7 %all-to-all-start.1 = ((f32[16,48,384]{2,1,0:T(8,128)}), f32[16,48,384]{2,1,0:T(8,128)S(1)}, u32[]{:S(2)}, u32[]{:S(2)}) async-start(f32[16,48,384]{2,1,0:T(8,128)} %get-tuple-element.35), calls=%async_computation.1 | async-start | bytes 2359296 | tf_op jit(solution)/shard_map/all_to_all | solution.py:1003
  95.4 0.0 copy-done.4
  95.5 0.4 collective-permute-start.4
  95.8 1.0 collective-permute-done.4.mate_ref
  96.8 0.0 copy-start.6
  96.8 0.6 copy-done.6
  97.5 11.3 %shard_map.161 = (f32[2,128,128]{2,1,0:T(8,128)}, f32[2,64,128]{2,1,0:T(8,128)}) custom-call(s32[1]{0:T(128)} %bitcast.7.first_ref, f32[192,128]{1,0:T(8,128)} %copy-done.4, f32[192,128]{1,0:T(8,128)} %copy-done.6, f32[256,128]{1,0:T(8,128)} %constant.90.clone.basis_ref, f32[2,256,256]{2,1,0:T(8,128)} %constant.91.clone.face_ref, ...), custom_call_target="tpu_custom_call" | custom-call | flops 5000000000 | bytes 8388608 | tf_op jit(solution)/shard_map/pallas_call | solution.py:406
  108.8 4.2 %shard_map.162 = f32[16,48,384]{2,1,0:T(8,128)} custom-call(s32[1]{0:T(128)} %bitcast.half_ref, f32[16,48,384]{2,1,0:T(8,128)} %get-tuple-element.36.u_ref, f32[16,48,768]{2,1,0:T(8,128)} %get-tuple-element.31.coef_ref, f32[48,768]{1,0:T(8,128)} %get-tuple-element.32.join_ref, f32[48,1]{1,0:T(8,128)} %copy.17.row_ref, f32[1,768]{1,0:T(1,128)} %constant.106.col_ref, ...), custom_call_target="tpu_custom_call" | custom-call | flops 11796480 | bytes 3538944 | tf_op jit(solution)/shard_map/pallas_call | solution.py:637
  113.0 0.0 all-to-all-done.1
  113.0 0.0 copy-start.1
  113.0 1.0 copy-done.1
  114.1 5.0 %all-to-all-start.2 = ((f32[16,48,384]{2,1,0:T(8,128)}), f32[16,48,384]{2,1,0:T(8,128)S(1)}, u32[]{:S(2)}, u32[]{:S(2)}) async-start(f32[16,48,384]{2,1,0:T(8,128)} %shard_map.162), calls=%async_computation.2 | async-start | bytes 2359296 | tf_op jit(solution)/shard_map/all_to_all | solution.py:1003
  119.1 20.8 %shard_map.163.refs_1_ = f32[384,768]{1,0:T(8,128)} custom-call(s32[1]{0:T(128)} %bitcast.3.place_ref, f32[384,768]{1,0:T(8,128)} %get-tuple-element.44.low_ref, f32[384,768]{1,0:T(8,128)} %get-tuple-element.45.high_ref, f32[384,1]{1,0:T(8,128)} %constant.104.row_ref.row_eigen_ref, f32[1,768]{1,0:T(1,128)} %constant.105.col_ref.col_eigen_ref, ...), custom_call_target="tpu_custom_call" | custom-call | flops 188743680 | bytes 7077888 | tf_op jit(solution)/shard_map/pallas_call | solution.py:947
  139.9 0.0 all-to-all-done.2
  139.9 0.0 copy-start.2
  139.9 1.0 copy-done.2
  140.9 10.0 %shard_map.164 = f32[768,768]{1,0:T(8,128)} custom-call(bf16[768,768]{1,0:T(8,128)(2,1)} %constant.87.clone.high_ref, bf16[768,768]{1,0:T(8,128)(2,1)} %constant.88.clone.low_ref, f32[768,384]{1,0:T(8,128)} %bitcast.12, f32[384,768]{1,0:T(8,128)} %shard_map.163.refs_1_, f32[768,384]{1,0:T(8,128)} %bitcast.13), custom_call_target="tpu_custom_call" | custom-call | tf_op jit(solution)/shard_map/pallas_call | solution.py:107
  (4 shorter events, 0.0 us)
Async XLA Ops:
  9.5 6.5 %copy-start.5 = (f32[768]{0:T(1024)S(1)}, f32[768]{0:T(1024)}, u32[]{:S(2)}) copy-start(f32[768]{0:T(1024)} %constant.98.clone) | copy-start | bytes 9220
  9.5 38.8 %all-to-all-start = ((f32[16,48,768]{2,1,0:T(8,128)}), f32[16,48,768]{2,1,0:T(8,128)S(1)}, u32[]{:S(2)}, u32[]{:S(2)}) async-start(f32[16,48,768]{2,1,0:T(8,128)} %bitcast.11), calls=%async_computation | async-start | bytes 4718592 | tf_op jit(solution)/shard_map/all_to_all | solution.py:1003
  48.4 1.4 copy-start
  52.5 9.6 %collective-permute-start = (f32[48,768]{1,0:T(8,128)}, f32[48,768]{1,0:T(8,128)S(1)}, u32[]{:S(2)}, u32[]{:S(2)}) collective-permute-start(f32[48,768]{1,0:T(8,128)} %shard_map.159), channel_id=1, source_target_pairs={{0,16},{1,17},{2,18},{3,19},{4,20},{5,21},{6,22},{7,23},{8,24},{9,... | collective-permute-start | bytes 442376 | tf_op jit(solution)/shard_map/ppermute | solution.py:1052
  62.0 0.7 copy-start.3
  68.9 1.5 %collective-permute-start.1 = (f32[192,128]{1,0:T(8,128)}, f32[192,128]{1,0:T(8,128)S(1)}, u32[]{:S(2)}, u32[]{:S(2)}) collective-permute-start(f32[192,128]{1,0:T(8,128)} %get-tuple-element.34), channel_id=1, source_target_pairs={{0,1},{1,0},{2,3},{3,2},{4,5},{5,4},{6,7},{7,6},{8,9},{9,8},{10,11... | collective-permute-start | bytes 294920 | tf_op jit(solution)/shard_map/ppermute | solution.py:1011
  82.0 4.2 %collective-permute-start.2 = (f32[96,128]{1,0:T(8,128)S(1)}, f32[96,128]{1,0:T(8,128)S(1)}, u32[]{:S(2)}, u32[]{:S(2)}) collective-permute-start(f32[96,128]{1,0:T(8,128)S(1)} %reduce_sum.9), channel_id=1, source_target_pairs={{0,8},{8,0},{16,24},{24,16},{1,9},{9,1},{17,25},{25,17},{2,10},{10... | collective-permute-start | bytes 147464 | tf_op jit(solution)/shard_map/ppermute | solution.py:1008
  86.1 5.6 %collective-permute-start.3 = (f32[96,128]{1,0:T(8,128)S(1)}, f32[96,128]{1,0:T(8,128)S(1)}, u32[]{:S(2)}, u32[]{:S(2)}) collective-permute-start(f32[96,128]{1,0:T(8,128)S(1)} %add.48), channel_id=1, source_target_pairs={{0,16},{8,24},{16,0},{24,8},{1,17},{9,25},{17,1},{25,9},{2,18},{10... | collective-permute-start | bytes 147464 | tf_op jit(solution)/shard_map/ppermute | solution.py:1008
  91.7 3.7 %copy-start.4 = (f32[192,128]{1,0:T(8,128)}, f32[192,128]{1,0:T(8,128)S(1)}, u32[]{:S(2)}) copy-start(f32[192,128]{1,0:T(8,128)S(1)} %pad_maximum_fusion.mine_ref) | copy-start | bytes 294916
  91.7 21.3 %all-to-all-start.1 = ((f32[16,48,384]{2,1,0:T(8,128)}), f32[16,48,384]{2,1,0:T(8,128)S(1)}, u32[]{:S(2)}, u32[]{:S(2)}) async-start(f32[16,48,384]{2,1,0:T(8,128)} %get-tuple-element.35), calls=%async_computation.1 | async-start | bytes 2359296 | tf_op jit(solution)/shard_map/all_to_all | solution.py:1003
  95.5 1.4 collective-permute-start.4
  96.8 0.6 copy-start.6
  113.0 1.0 copy-start.1
  114.1 25.8 %all-to-all-start.2 = ((f32[16,48,384]{2,1,0:T(8,128)}), f32[16,48,384]{2,1,0:T(8,128)S(1)}, u32[]{:S(2)}, u32[]{:S(2)}) async-start(f32[16,48,384]{2,1,0:T(8,128)} %shard_map.162), calls=%async_computation.2 | async-start | bytes 2359296 | tf_op jit(solution)/shard_map/all_to_all | solution.py:1003
  139.9 1.0 copy-start.2

commit v8 on v7

--- a/solution.py
+++ b/solution.py
@@ -69,7 +69,7 @@
     return value + (bf16_dot(a_high, b_low, dims) + bf16_dot(a_low, b_high, dims))
 
 
-STRIPE = 256
+STRIPE = 384
 
 
 def product_body(count, high_ref, low_ref, *refs):

time: 152 us -> 152 us (level)
  no operation moved by 1% of the time
where the time goes in v8:
time: 152 us; the launch traced here: 151 us
  Pallas kernels  91.1 us (60%)
  starting transfers between devices  20.1 us (13%)
  waiting for transfers between devices  19.6 us (13%)
  blocking collectives  10.6 us (7%)
  local copies, waits for them, and re-layouts  7.65 us (5%)
  other arithmetic  1.68 us (1%)
    pallas_call x1, Pallas kernels, plane_layers(): pl.pallas_call(functools.partial(plane_body, depth), grid_spec=pltpu.Pref...  20.8 us
    pallas_call x2, Pallas kernels, double_product(): pl.pallas_call(functools.partial(product_body, len(values)), grid=(2 * st...  19.4 us
    all_to_all x3, starting transfers between devices, exchange(): lax.all_to_all(x, AXES, split_axis=0, concat_axis=0, tiled=True, axis_ind...  15.2 us
    pallas_call x1, Pallas kernels, panel_potential(): pl.pallas_call(panels_body, in_specs=[pl.BlockSpec(memory_space=pltpu.SME...  11.3 us
    all_gather x1, blocking collectives, on_device(): lax.all_gather(part, 'py', axis=0, tiled=False, axis_index_groups=alternate)  10.6 us
    pallas_call x1, Pallas kernels, weights(): pl.pallas_call(functools.partial(weight_body, depth), grid_spec=pltpu.Pre...  9.87 us
    all_to_all x3, waiting for transfers between devices, exchange(): lax.all_to_all(x, AXES, split_axis=0, concat_axis=0, tiled=True, axis_ind...  8.18 us
    ppermute x2, waiting for transfers between devices, hop(): return lax.ppermute(x, 'px', [(i, i ^ bit) for i in range(slow)])  7.79 us
  transfers between devices with their start and end apart: 8, of which 6 were waited for; matrix products, arithmetic and copies ran while one was open for 2% of the time, Pallas kernels for 42%

profile of v8, /device:TPU:0, one launch (start us, length us, event | category | flops | bytes accessed | tf_op | source)
XLA Modules:
  0.0 150.8 jit_solution(5577389405898307905)
XLA Ops:
  0.0 9.3 %shard_map.154 = f32[768,768]{1,0:T(8,128)} custom-call(bf16[768,768]{1,0:T(8,128)(2,1)} %constant.87.clone.high_ref, bf16[768,768]{1,0:T(8,128)(2,1)} %constant.88.clone.low_ref, f32[768,768]{1,0:T(8,128)} %bitcast.14), custom_call_target="tpu_custom_call" | custom-call | tf_op jit(solution)/shard_map/pallas_call | solution.py:107
  9.3 0.0 copy-start.5
  9.4 6.4 %all-to-all-start = ((f32[16,48,768]{2,1,0:T(8,128)}), f32[16,48,768]{2,1,0:T(8,128)S(1)}, u32[]{:S(2)}, u32[]{:S(2)}) async-start(f32[16,48,768]{2,1,0:T(8,128)} %bitcast.11), calls=%async_computation | async-start | bytes 4718592 | tf_op jit(solution)/shard_map/all_to_all | solution.py:1003
  15.8 0.0 copy-done.5
  15.8 0.1 dynamic_slice.9
  15.9 9.9 %shard_map.157 = (f32[384,768]{1,0:T(8,128)}, f32[384,768]{1,0:T(8,128)}) custom-call(s32[1]{0:T(128)} %bitcast.3.place_ref, f32[384,1]{1,0:T(8,128)} %constant.104.row_ref.row_eigen_ref, f32[1,768]{1,0:T(1,128)} %constant.105.col_ref.col_eigen_ref), custom_call_target="tpu_custom_call" | custom-call | flops 37748736 | bytes 2359296 | tf_op jit(solution)/shard_map/pallas_call | solution.py:831
  25.8 7.6 %shard_map.156 = (f32[64,64,128]{2,1,0:T(8,128)}, f32[64,64,128]{2,1,0:T(8,128)}) custom-call(f32[64,128]{1,0:T(8,128)} %constant.97.clone.wave_ref), custom_call_target="tpu_custom_call" | custom-call | flops 134217728 | bytes 2097152 | tf_op jit(solution)/shard_map/pallas_call | solution.py:217
  33.4 5.9 %shard_map.155.mixed_hbm = f32[2,16,128,256]{3,2,1,0:T(8,128)} custom-call(f32[128,256]{1,0:T(8,128)} %constant.96.clone.wave_ref), custom_call_target="tpu_custom_call" | custom-call | flops 134217728 | bytes 2097152 | tf_op jit(solution)/shard_map/pallas_call | solution.py:167
  39.3 0.7 broadcast_add_fusion.mu_ref
  40.0 8.1 %all-to-all-done.f_ref = f32[16,48,768]{2,1,0:T(8,128)S(1)} async-done(((f32[16,48,768]{2,1,0:T(8,128)}), f32[16,48,768]{2,1,0:T(8,128)S(1)}, u32[]{:S(2)}, u32[]{:S(2)}) %all-to-all-start) | async-done | bytes 2359328 | tf_op jit(solution)/shard_map/all_to_all | solution.py:1003
  48.2 0.0 copy-start
  48.2 1.4 copy-done
  49.6 2.7 %shard_map.159 = f32[48,768]{1,0:T(8,128)} custom-call(s32[1]{0:T(128)} %bitcast.half_ref, f32[16,48,768]{2,1,0:T(8,128)} %copy-done, f32[48,768]{1,0:T(8,128)} %broadcast_add_fusion.mu_ref), custom_call_target="tpu_custom_call" | custom-call | tf_op jit(solution)/shard_map/pallas_call | solution.py:522
  52.3 2.6 %collective-permute-start = (f32[48,768]{1,0:T(8,128)}, f32[48,768]{1,0:T(8,128)S(1)}, u32[]{:S(2)}, u32[]{:S(2)}) collective-permute-start(f32[48,768]{1,0:T(8,128)} %shard_map.159), channel_id=1, source_target_pairs={{0,16},{1,17},{2,18},{3,19},{4,20},{5,21},{6,22},{7,23},{8,24},{9,... | collective-permute-start | bytes 442376 | tf_op jit(solution)/shard_map/ppermute | solution.py:1052
  54.9 0.8 dynamic-slice_bitcast_fusion
  55.6 0.7 copy.17.row_ref
  56.3 3.1 %shard_map.158 = (f32[16,48,768]{2,1,0:T(8,128)}, f32[48,768]{1,0:T(8,128)}) custom-call(f32[48,768]{1,0:T(8,128)} %broadcast_add_fusion.mu_ref), custom_call_target="tpu_custom_call" | custom-call | flops 11796480 | bytes 2359296 | tf_op jit(solution)/shard_map/pallas_call | solution.py:462
  59.4 1.3 constant_dynamic-slice_fusion.mine_ref
  60.8 1.1 collective-permute-done.far_ref
  61.8 0.0 copy-start.3
  61.8 0.7 copy-done.3
  62.5 6.3 %shard_map.160 = (f32[16,48,384]{2,1,0:T(8,128)}, f32[16,48,384]{2,1,0:T(8,128)}, f32[192,128]{1,0:T(8,128)}) custom-call(s32[1]{0:T(128)} %bitcast.half_ref, f32[16,48,768]{2,1,0:T(8,128)} %copy-done, f32[16,48,768]{2,1,0:T(8,128)} %get-tuple-element.31.coef_ref, f32[48,768]{1,0:T(8,128)} %get-tuple-element.32.join_ref, f32[48,768]{1,0:T(8,128)} %copy-done.3, ...), custom_call_target="tpu_custom_call" | custom-call | tf_op jit(solution)/shard_map/pallas_call | solution.py:741
  68.7 0.0 collective-permute-start.1
  68.8 1.5 collective-permute-done.1
  70.3 0.9 add.47
  71.2 10.6 %all-gather = f32[384,128]{1,0:T(8,128)S(1)} all-gather(f32[96,128]{1,0:T(8,128)S(1)} %slice_select_fusion), channel_id=2, replica_groups={{0,2,4,6},{1,3,5,7},{8,10,12,14},{9,11,13,15},{16,18,20,22},{17,19,21,2..., dimensions={0}, use_global_device_ids=true | all-gather | bytes 245760 | tf_op jit(solution)/shard_map/all_gather | solution.py:1073
  81.8 0.3 collective-permute-start.2
  82.1 3.8 %collective-permute-done.2 = f32[96,128]{1,0:T(8,128)S(1)} collective-permute-done((f32[96,128]{1,0:T(8,128)S(1)}, f32[96,128]{1,0:T(8,128)S(1)}, u32[]{:S(2)}, u32[]{:S(2)}) %collective-permute-start.2) | collective-permute-done | bytes 49184 | tf_op jit(solution)/shard_map/ppermute | solution.py:1008
  85.9 1.6 %collective-permute-start.3 = (f32[96,128]{1,0:T(8,128)S(1)}, f32[96,128]{1,0:T(8,128)S(1)}, u32[]{:S(2)}, u32[]{:S(2)}) collective-permute-start(f32[96,128]{1,0:T(8,128)S(1)} %add.48), channel_id=1, source_target_pairs={{0,16},{8,24},{16,0},{24,8},{1,17},{9,25},{17,1},{25,9},{2,18},{10... | collective-permute-start | bytes 147464 | tf_op jit(solution)/shard_map/ppermute | solution.py:1008
  87.5 4.0 %collective-permute-done.3 = f32[96,128]{1,0:T(8,128)S(1)} collective-permute-done((f32[96,128]{1,0:T(8,128)S(1)}, f32[96,128]{1,0:T(8,128)S(1)}, u32[]{:S(2)}, u32[]{:S(2)}) %collective-permute-start.3) | collective-permute-done | bytes 49184 | tf_op jit(solution)/shard_map/ppermute | solution.py:1008
  91.5 0.0 copy-start.4
  91.5 3.7 %all-to-all-start.1 = ((f32[16,48,384]{2,1,0:T(8,128)}), f32[16,48,384]{2,1,0:T(8,128)S(1)}, u32[]{:S(2)}, u32[]{:S(2)}) async-start(f32[16,48,384]{2,1,0:T(8,128)} %get-tuple-element.35), calls=%async_computation.1 | async-start | bytes 2359296 | tf_op jit(solution)/shard_map/all_to_all | solution.py:1003
  95.3 0.0 copy-done.4
  95.3 0.4 collective-permute-start.4
  95.6 1.0 collective-permute-done.4.mate_ref
  96.7 0.0 copy-start.6
  96.7 0.6 copy-done.6
  97.3 11.3 %shard_map.161 = (f32[2,128,128]{2,1,0:T(8,128)}, f32[2,64,128]{2,1,0:T(8,128)}) custom-call(s32[1]{0:T(128)} %bitcast.7.first_ref, f32[192,128]{1,0:T(8,128)} %copy-done.4, f32[192,128]{1,0:T(8,128)} %copy-done.6, f32[256,128]{1,0:T(8,128)} %constant.90.clone.basis_ref, f32[2,256,256]{2,1,0:T(8,128)} %constant.91.clone.face_ref, ...), custom_call_target="tpu_custom_call" | custom-call | flops 5000000000 | bytes 8388608 | tf_op jit(solution)/shard_map/pallas_call | solution.py:406
  108.6 4.2 %shard_map.162 = f32[16,48,384]{2,1,0:T(8,128)} custom-call(s32[1]{0:T(128)} %bitcast.half_ref, f32[16,48,384]{2,1,0:T(8,128)} %get-tuple-element.36.u_ref, f32[16,48,768]{2,1,0:T(8,128)} %get-tuple-element.31.coef_ref, f32[48,768]{1,0:T(8,128)} %get-tuple-element.32.join_ref, f32[48,1]{1,0:T(8,128)} %copy.17.row_ref, f32[1,768]{1,0:T(1,128)} %constant.106.col_ref, ...), custom_call_target="tpu_custom_call" | custom-call | flops 11796480 | bytes 3538944 | tf_op jit(solution)/shard_map/pallas_call | solution.py:637
  112.8 0.0 all-to-all-done.1
  112.9 0.0 copy-start.1
  112.9 1.0 copy-done.1
  113.9 5.0 %all-to-all-start.2 = ((f32[16,48,384]{2,1,0:T(8,128)}), f32[16,48,384]{2,1,0:T(8,128)S(1)}, u32[]{:S(2)}, u32[]{:S(2)}) async-start(f32[16,48,384]{2,1,0:T(8,128)} %shard_map.162), calls=%async_computation.2 | async-start | bytes 2359296 | tf_op jit(solution)/shard_map/all_to_all | solution.py:1003
  118.9 20.8 %shard_map.163.refs_1_ = f32[384,768]{1,0:T(8,128)} custom-call(s32[1]{0:T(128)} %bitcast.3.place_ref, f32[384,768]{1,0:T(8,128)} %get-tuple-element.44.low_ref, f32[384,768]{1,0:T(8,128)} %get-tuple-element.45.high_ref, f32[384,1]{1,0:T(8,128)} %constant.104.row_ref.row_eigen_ref, f32[1,768]{1,0:T(1,128)} %constant.105.col_ref.col_eigen_ref, ...), custom_call_target="tpu_custom_call" | custom-call | flops 188743680 | bytes 7077888 | tf_op jit(solution)/shard_map/pallas_call | solution.py:947
  139.7 0.0 all-to-all-done.2
  139.7 0.0 copy-start.2
  139.7 1.0 copy-done.2
  140.7 10.0 %shard_map.164 = f32[768,768]{1,0:T(8,128)} custom-call(bf16[768,768]{1,0:T(8,128)(2,1)} %constant.87.clone.high_ref, bf16[768,768]{1,0:T(8,128)(2,1)} %constant.88.clone.low_ref, f32[768,384]{1,0:T(8,128)} %bitcast.12, f32[384,768]{1,0:T(8,128)} %shard_map.163.refs_1_, f32[768,384]{1,0:T(8,128)} %bitcast.13), custom_call_target="tpu_custom_call" | custom-call | tf_op jit(solution)/shard_map/pallas_call | solution.py:107
  (4 shorter events, 0.0 us)
Async XLA Ops:
  9.3 6.5 %copy-start.5 = (f32[768]{0:T(1024)S(1)}, f32[768]{0:T(1024)}, u32[]{:S(2)}) copy-start(f32[768]{0:T(1024)} %constant.98.clone) | copy-start | bytes 9220
  9.4 38.8 %all-to-all-start = ((f32[16,48,768]{2,1,0:T(8,128)}), f32[16,48,768]{2,1,0:T(8,128)S(1)}, u32[]{:S(2)}, u32[]{:S(2)}) async-start(f32[16,48,768]{2,1,0:T(8,128)} %bitcast.11), calls=%async_computation | async-start | bytes 4718592 | tf_op jit(solution)/shard_map/all_to_all | solution.py:1003
  48.2 1.4 copy-start
  52.3 9.6 %collective-permute-start = (f32[48,768]{1,0:T(8,128)}, f32[48,768]{1,0:T(8,128)S(1)}, u32[]{:S(2)}, u32[]{:S(2)}) collective-permute-start(f32[48,768]{1,0:T(8,128)} %shard_map.159), channel_id=1, source_target_pairs={{0,16},{1,17},{2,18},{3,19},{4,20},{5,21},{6,22},{7,23},{8,24},{9,... | collective-permute-start | bytes 442376 | tf_op jit(solution)/shard_map/ppermute | solution.py:1052
  61.8 0.7 copy-start.3
  68.7 1.5 %collective-permute-start.1 = (f32[192,128]{1,0:T(8,128)}, f32[192,128]{1,0:T(8,128)S(1)}, u32[]{:S(2)}, u32[]{:S(2)}) collective-permute-start(f32[192,128]{1,0:T(8,128)} %get-tuple-element.34), channel_id=1, source_target_pairs={{0,1},{1,0},{2,3},{3,2},{4,5},{5,4},{6,7},{7,6},{8,9},{9,8},{10,11... | collective-permute-start | bytes 294920 | tf_op jit(solution)/shard_map/ppermute | solution.py:1011
  81.8 4.2 %collective-permute-start.2 = (f32[96,128]{1,0:T(8,128)S(1)}, f32[96,128]{1,0:T(8,128)S(1)}, u32[]{:S(2)}, u32[]{:S(2)}) collective-permute-start(f32[96,128]{1,0:T(8,128)S(1)} %reduce_sum.9), channel_id=1, source_target_pairs={{0,8},{8,0},{16,24},{24,16},{1,9},{9,1},{17,25},{25,17},{2,10},{10... | collective-permute-start | bytes 147464 | tf_op jit(solution)/shard_map/ppermute | solution.py:1008
  85.9 5.6 %collective-permute-start.3 = (f32[96,128]{1,0:T(8,128)S(1)}, f32[96,128]{1,0:T(8,128)S(1)}, u32[]{:S(2)}, u32[]{:S(2)}) collective-permute-start(f32[96,128]{1,0:T(8,128)S(1)} %add.48), channel_id=1, source_target_pairs={{0,16},{8,24},{16,0},{24,8},{1,17},{9,25},{17,1},{25,9},{2,18},{10... | collective-permute-start | bytes 147464 | tf_op jit(solution)/shard_map/ppermute | solution.py:1008
  91.5 3.7 %copy-start.4 = (f32[192,128]{1,0:T(8,128)}, f32[192,128]{1,0:T(8,128)S(1)}, u32[]{:S(2)}) copy-start(f32[192,128]{1,0:T(8,128)S(1)} %pad_maximum_fusion.mine_ref) | copy-start | bytes 294916
  91.5 21.3 %all-to-all-start.1 = ((f32[16,48,384]{2,1,0:T(8,128)}), f32[16,48,384]{2,1,0:T(8,128)S(1)}, u32[]{:S(2)}, u32[]{:S(2)}) async-start(f32[16,48,384]{2,1,0:T(8,128)} %get-tuple-element.35), calls=%async_computation.1 | async-start | bytes 2359296 | tf_op jit(solution)/shard_map/all_to_all | solution.py:1003
  95.3 1.4 collective-permute-start.4
  96.7 0.6 copy-start.6
  112.9 1.0 copy-start.1
  113.9 25.8 %all-to-all-start.2 = ((f32[16,48,384]{2,1,0:T(8,128)}), f32[16,48,384]{2,1,0:T(8,128)S(1)}, u32[]{:S(2)}, u32[]{:S(2)}) async-start(f32[16,48,384]{2,1,0:T(8,128)} %shard_map.162), calls=%async_computation.2 | async-start | bytes 2359296 | tf_op jit(solution)/shard_map/all_to_all | solution.py:1003
  139.7 1.0 copy-start.2
